TPU v7x, 128 devices: a whole 4x4x4 slice. The times are simulated.
128 devices in a mesh: face: 8 (over x, core), sub: 16 (over y, z).
Axes of the slice: x: 4, y: 4, z: 4, core: 2. Of those that a mesh axis runs over, the one named last changes fastest.
Arguments:
- grid_latent: bfloat16 [65536, 512], P(('face', 'sub')), may hold values from -6 to 6
- mesh_latent: bfloat16 [16384, 512], P(('face', 'sub')), may hold values from -6 to 6
- edge_latent: bfloat16 [131072, 512], P(('face', 'sub')), may hold values from -6 to 6
- mesh_cotangent: bfloat16 [16384, 512], P(('face', 'sub')), may hold values from -6 to 6
- edge_cotangent: bfloat16 [131072, 512], P(('face', 'sub')), may hold values from -6 to 6
- grid_send: int32 [128, 4, 256], P(('face', 'sub')), may hold values from 0 to 511
- grid_slot: int32 [131072], P(('face', 'sub')), may hold values from 0 to 1535, as said below
- grid_target: int32 [131072], P(('face', 'sub')), may hold values from 0 to 127
- mesh_halo: int32 [128, 4, 64], P(('face', 'sub')), may hold values from 0 to 127
- mesh_send: int32 [128, 128, 4], P(('face', 'sub')), may hold values from 0 to 127
- mesh_slot: int32 [131072], P(('face', 'sub')), may hold values from 0 to 895, as said below
- mesh_target: int32 [131072], P(('face', 'sub')), may hold values from 0 to 127
- weights: bfloat16 [10, 512, 512], replicated, may hold values from -0.25 to 0.25
Outputs:
- mesh_update: bfloat16 [16384, 512], P(('face', 'sub'))
- grid_grad: bfloat16 [65536, 512], P(('face', 'sub'))
- mesh_grad: bfloat16 [16384, 512], P(('face', 'sub'))
- edge_grad: bfloat16 [131072, 512], P(('face', 'sub'))
- weight_grads: bfloat16 [10, 512, 512], replicated
Inputs may be any that keep to these rules, and one draw needn't show every extreme that they name: grid_slot[e] names the edge device's own 512 grid rows or, above them, the 256 rows listed by each of its four neighbours in direction order. grid_target[e] is local to the edge's device. grid_send[q, k] lists local rows of device q for the device d with nb(d, k) = q; a row may appear in several slots. mesh_slot[e] names the own 128 mesh rows, then the 64 rows listed by each of the four neighbours, then 4 far rows from each device, source major. mesh_target[e] is local to the edge's device. mesh_halo[q, k] lists local rows of device q for its neighbour in direction k. mesh_send[q, d] lists local rows of device q for far edges of device d.
All inputs are finite; a program needn't handle non-finite values.
Results may differ from a plain program's by a relative error of at most 0.016.
Values may be sent and summed in bfloat16 or wider, within the bound.
No kernel may reach another device: no remote copies, remote signals or barrier semaphores. Data moves between devices by JAX's collectives and lax.ppermute only.
A program may use at most 128 MiB of HBM per device.

v0:
```python
import functools

import jax
import jax.numpy as jnp
from jax import lax
from jax.experimental import pallas as pl
from jax.experimental.pallas import tpu as pltpu
from jax.sharding import PartitionSpec as P

norm_eps = 1e-05
f32 = jnp.float32
bf16 = jnp.bfloat16
AXES = ("face", "sub")
CHUNK = 256


def shifted(value, axis, steps):
    count = lax.axis_size(axis)
    pairs = [(source, (source + steps) % count) for source in range(count)]
    return lax.ppermute(value, axis, pairs)


def outgoing_rows(blocks):
    routes = (("sub", 1), ("sub", -1), ("face", 1), ("face", -1))
    return [shifted(block, axis, step) for block, (axis, step) in zip(blocks, routes)]


def returned_rows(blocks):
    routes = (("sub", -1), ("sub", 1), ("face", -1), ("face", 1))
    return [shifted(block, axis, step) for block, (axis, step) in zip(blocks, routes)]


def dot(a, b):
    return jnp.dot(a, b, preferred_element_type=f32)


def dot_nt(a, b):
    return lax.dot_general(a, b, (((1,), (1,)), ((), ())), preferred_element_type=f32)


def dot_tn(a, b):
    return lax.dot_general(a, b, (((0,), (0,)), ((), ())), preferred_element_type=f32)


def halves(values):
    upper = values.astype(bf16)
    return upper, (values - upper.astype(f32)).astype(bf16)


def mean(values):
    return jnp.sum(values, axis=-1, keepdims=True) * (1.0 / values.shape[-1])


def norm_parts(values):
    centre = values - mean(values)
    inverse = lax.rsqrt(mean(centre * centre) + norm_eps)
    return centre * inverse, inverse


def norm_back(normed, inverse, upstream):
    return inverse * (upstream - mean(upstream) - normed * mean(upstream * normed))


def sigmoid(values):
    return 1.0 / (1.0 + jnp.exp(-values))


def silu(values):
    return values * sigmoid(values)


def slope(values):
    s = sigmoid(values)
    return s * (1.0 + values * (1.0 - s))


def pick_rows(row, offset, count):
    column = jnp.transpose(jnp.broadcast_to(row, (128, 128))) - offset
    lane = lax.broadcasted_iota(jnp.int32, (128, 128), 1)
    return jnp.concatenate(
        [jnp.where(column == lane + 128 * b, 1.0, 0.0).astype(bf16) for b in range(count // 128)],
        axis=1,
    )


def pick(ref, first, rows, offset, count):
    return jnp.concatenate(
        [pick_rows(ref[pl.ds(first + r, 1), :], offset, count) for r in range(rows)], axis=0
    )


def put(ref, first, rows, offset, count):
    place = lax.broadcasted_iota(jnp.int32, (count, 128), 0) + offset
    return jnp.concatenate(
        [
            jnp.where(place == jnp.broadcast_to(ref[pl.ds(first + r, 1), :], (count, 128)), 1.0, 0.0).astype(bf16)
            for r in range(rows)
        ],
        axis=1,
    )


def chunks(count, body):
    def step(i, carry):
        body(i, pl.ds(pl.multiple_of(i * CHUNK, CHUNK), CHUNK))
        return carry

    lax.fori_loop(0, count, step, 0)


def call(body, outs, args, weights=None, picks=(), scratch=(), flops=10**9, vmem=40 << 20, name=None):
    whole = pl.BlockSpec(memory_space=pltpu.VMEM)
    in_specs = [whole] * len(args)
    for k in picks:
        in_specs.append(
            pl.BlockSpec((None, weights.shape[1], weights.shape[2]), functools.partial(lambda k, i: (k, 0, 0), k))
        )
    shapes = [jax.ShapeDtypeStruct(s, d) for s, d in outs]
    total = sum(a.size * a.dtype.itemsize for a in args) + sum(s.size * s.dtype.itemsize for s in shapes)
    total += len(picks) * 512 * 1024
    return pl.pallas_call(
        body,
        grid=(1,),
        out_shape=shapes,
        in_specs=in_specs,
        out_specs=[whole] * len(shapes),
        scratch_shapes=list(scratch),
        compiler_params=pltpu.CompilerParams(vmem_limit_bytes=vmem),
        cost_estimate=pl.CostEstimate(flops=flops, bytes_accessed=total, transcendentals=0),
        name=name,
    )(*args, *([weights] * len(picks)))


def project_body(grid, table, w0, project, out0, out1, out2, out3):
    chunks(2, lambda i, s: project.__setitem__((s, slice(None)), dot(grid[s, :], w0[...]).astype(bf16)))
    for k, out in enumerate((out0, out1, out2, out3)):
        out[...] = dot(pick(table, 2 * k, 2, 0, 512), project[...]).astype(bf16)


def encode_own_body(project, slot, target, mesh, edge, w1, w3, own, edge_pre):
    upper, lower = halves(dot(mesh[...], w1[...]))

    def step(i, s):
        receiver = pick(target, 2 * i, 2, 0, 128)
        own[s, :] = (
            dot(pick(slot, 2 * i, 2, 0, 512), project[...]) + dot(receiver, upper) + dot(receiver, lower)
        )
        edge_pre[s, :] = dot(edge[s, :], w3[...])

    chunks(4, step)


def far_slots(slot):
    far = slot - 384
    return jnp.where(slot < 384, slot, 384 + (far & 3) * 128 + (far >> 2))


def encode_body(
    own, in0, in1, in2, in3, slot, target, mesh, halo, far, w2, w4,
    pre_out, linear_out, hidden_out, middle_out, sender_out, h0, h1, h2, h3, far_out,
    total, wide,
):
    total[...] = jnp.zeros_like(total)

    def step(i, s):
        pre = own[s, :]
        for k, block in enumerate((in0, in1, in2, in3)):
            pre = pre + dot(pick(slot, 2 * i, 2, 512 + 256 * k, 256), block[...])
        pre_out[s, :] = pre
        hidden = silu(pre).astype(bf16)
        hidden_out[s, :] = hidden
        linear = dot(hidden, w2[...])
        linear_out[s, :] = linear
        message = norm_parts(linear)[0].astype(bf16)
        total[...] += dot(put(target, 2 * i, 2, 0, 128), message)

    chunks(4, step)
    middle = (mesh[...].astype(f32) + total[...]).astype(bf16)
    middle_out[...] = middle
    sender = dot(middle, w4[...]).astype(bf16)
    sender_out[...] = sender
    rows = dot(pick(halo, 0, 2, 0, 128), sender).astype(bf16)
    for k, out in enumerate((h0, h1, h2, h3)):
        out[...] = rows[64 * k : 64 * k + 64, :]
    for r in range(4):
        picked = dot(pick(far, r, 1, 0, 128), sender)
        for c in range(4):
            wide[pl.ds(4 * c + r, 128, stride=16), :] = picked[:, 128 * c : 128 * c + 128]
    far_out[...] = wide[...].astype(bf16)


def process_own_body(middle, sender, edge_pre, slot, target, w5, w7, own, update_own):
    upper, lower = halves(dot(middle[...], w5[...]))
    update_own[...] = dot(middle[...], w7[...])

    def step(i, s):
        receiver = pick(target, 2 * i, 2, 0, 128)
        own[s, :] = (
            edge_pre[s, :] + dot(pick(slot, 2 * i, 2, 0, 128), sender[...]) + dot(receiver, upper) + dot(receiver, lower)
        )

    chunks(4, step)


def gather_far(wide, source, first):
    for r in range(4):
        for c in range(4):
            source[first + 128 * r : first + 128 * r + 128, 128 * c : 128 * c + 128] = wide[
                pl.ds(4 * c + r, 128, stride=16), :
            ].astype(bf16)


def process_body(
    own, in0, in1, in2, in3, far_in, slot, target, middle, update_own, mesh_cot, edge_cot, w6, w8, w9,
    mesh_update, hidden_out, round_out, uhidden_out, cot_linear_out, cot_update_out, plinear_out, cround_out,
    receive_out, sender_own, h0, h1, h2, h3, far_out,
    source, pre_s, normed_s, inverse_s, lower_s, total, wide, slots,
):
    slots[...] = far_slots(slot[...])
    for k, block in enumerate((in0, in1, in2, in3)):
        source[64 * k : 64 * k + 64, :] = block[...]
    wide[...] = far_in[...].astype(f32)
    gather_far(wide, source, 256)
    total[...] = jnp.zeros_like(total)

    def forward(i, s):
        pre = own[s, :] + dot(pick(slots, 2 * i, 2, 128, 768), source[...])
        pre_s[s, :] = pre
        hidden = silu(pre).astype(bf16)
        hidden_out[s, :] = hidden
        normed, inverse = norm_parts(dot(hidden, w6[...]))
        normed_s[s, :] = normed
        inverse_s[s, :] = jnp.broadcast_to(inverse, (CHUNK, 128))
        total[...] += dot(put(target, 2 * i, 2, 0, 128), normed.astype(bf16))

    chunks(4, forward)
    rounded = total[...].astype(bf16)
    round_out[...] = rounded
    pre = update_own[...] + dot(rounded, w8[...])
    uhidden = silu(pre).astype(bf16)
    uhidden_out[...] = uhidden
    normed, inverse = norm_parts(dot(uhidden, w9[...]))
    mesh_update[...] = (middle[...].astype(f32) + normed).astype(bf16)
    cot_linear = norm_back(normed, inverse, mesh_cot[...].astype(f32)).astype(bf16)
    cot_linear_out[...] = cot_linear
    cot_update = (dot_nt(cot_linear, w9[...]) * slope(pre)).astype(bf16)
    cot_update_out[...] = cot_update
    upper, lower = halves(dot_nt(cot_update, w8[...]))

    def backward(i, s):
        receiver = pick(target, 2 * i, 2, 0, 128)
        upstream = dot(receiver, upper) + dot(receiver, lower) + edge_cot[s, :].astype(f32)
        cot = norm_back(normed_s[s, :], inverse_s[s, 0:1], upstream).astype(bf16)
        plinear_out[s, :] = cot
        high, low = halves(dot_nt(cot, w6[...]) * slope(pre_s[s, :]))
        cround_out[s, :] = high
        lower_s[s, :] = low

    chunks(4, backward)
    kept = jnp.concatenate([put(target, 0, 8, 0, 128), put(slots, 0, 8, 0, 128)], axis=0)
    kept = dot(kept, cround_out[...]) + dot(kept, lower_s[...])
    receive_out[...] = kept[0:128, :].astype(bf16)
    sender_own[...] = kept[128:256, :]
    spread = put(slots, 0, 8, 128, 256)
    spread = (dot(spread, cround_out[...]) + dot(spread, lower_s[...])).astype(bf16)
    for k, out in enumerate((h0, h1, h2, h3)):
        out[...] = spread[64 * k : 64 * k + 64, :]
    for half in range(2):
        spread = put(slots, 0, 8, 384 + 256 * half, 256)
        spread = dot(spread, cround_out[...]) + dot(spread, lower_s[...])
        for q in range(2):
            for c in range(4):
                wide[pl.ds(4 * c + 2 * half + q, 128, stride=16), :] = spread[
                    128 * q : 128 * q + 128, 128 * c : 128 * c + 128
                ]
    far_out[...] = wide[...].astype(bf16)


def process_grads_body(
    scales, edge, cround, hidden, plinear, middle, receive, cot_update, rounded, uhidden, cot_linear, edge_cot, mesh_cot,
    w3, w5, w7, edge_grad, middle_part, grads,
):
    pairs = ((edge, cround), (middle, receive), (hidden, plinear), (middle, cot_update), (rounded, cot_update), (uhidden, cot_linear))
    for k, (x, y) in enumerate(pairs):
        grads[k] = (dot_tn(x[...], y[...]) * scales[k]).astype(bf16)
    middle_part[...] = mesh_cot[...].astype(f32) + dot_nt(cot_update[...], w7[...]) + dot_nt(receive[...], w5[...])

    def step(i, s):
        edge_grad[s, :] = (edge_cot[s, :].astype(f32) + dot_nt(cround[s, :], w3[...])).astype(bf16)

    chunks(4, step)


def encode_back_body(
    in0, in1, in2, in3, far_in, halo, far, sender_own, middle_part, pre, linear, slot, target, w2, w4,
    cot_sender_out, cot_middle_out, elinear_out, upper_out, lower_out, g0, g1, g2, g3,
    source, wide,
):
    for k, block in enumerate((in0, in1, in2, in3)):
        source[64 * k : 64 * k + 64, :] = block[...]
    wide[...] = far_in[...].astype(f32)
    gather_far(wide, source, 256)
    owners = jnp.concatenate([put(halo, 0, 2, 0, 128), put(far, 0, 4, 0, 128)], axis=1)
    cot_sender = (sender_own[...] + dot(owners, source[...])).astype(bf16)
    cot_sender_out[...] = cot_sender
    cot_middle = middle_part[...] + dot_nt(cot_sender, w4[...])
    cot_middle_out[...] = cot_middle
    upper, lower = halves(cot_middle)

    def step(i, s):
        receiver = pick(target, 2 * i, 2, 0, 128)
        normed, inverse = norm_parts(linear[s, :])
        cot = norm_back(normed, inverse, dot(receiver, upper) + dot(receiver, lower)).astype(bf16)
        elinear_out[s, :] = cot
        high, low = halves(dot_nt(cot, w2[...]) * slope(pre[s, :]))
        upper_out[s, :] = high
        lower_out[s, :] = low

    chunks(4, step)
    for k, out in enumerate((g0, g1, g2, g3)):
        spread = put(slot, 0, 8, 512 + 256 * k, 256)
        out[...] = (dot(spread, upper_out[...]) + dot(spread, lower_out[...])).astype(bf16)


def encode_grads_body(
    scales, upper, lower, slot, target, cot_middle, mesh, middle, cot_sender, hidden, elinear, w1,
    grid_own, mesh_grad, grads,
):
    grads[0] = (dot_tn(hidden[...], elinear[...]) * scales[1]).astype(bf16)
    grads[1] = (dot_tn(middle[...], cot_sender[...]) * scales[2]).astype(bf16)
    kept = put(target, 0, 8, 0, 128)
    receive = (dot(kept, upper[...]) + dot(kept, lower[...])).astype(bf16)
    grads[2] = (dot_tn(mesh[...], receive) * scales[0]).astype(bf16)
    mesh_grad[...] = (cot_middle[...] + dot_nt(receive, w1[...])).astype(bf16)
    for k in range(2):
        kept = put(slot, 0, 8, 256 * k, 256)
        grid_own[256 * k : 256 * k + 256, :] = dot(kept, upper[...]) + dot(kept, lower[...])


def grid_back_body(scales, grid_own, in0, in1, in2, in3, table, grid, w0, grid_grad, grads, cot):
    def step(i, s):
        total = grid_own[s, :]
        for k, block in enumerate((in0, in1, in2, in3)):
            total = total + dot(put(table, 2 * k, 2, i * CHUNK, 256), block[...])
        total = total.astype(bf16)
        cot[s, :] = total
        grid_grad[s, :] = dot_nt(total, w0[...]).astype(bf16)

    chunks(2, step)
    grads[...] = (dot_tn(grid[...], cot[...]) * scales[0]).astype(bf16)


def scaled(body, scales):
    return functools.partial(body, scales)


def on_device(
    grid_latent, mesh_latent, edge_latent, mesh_cotangent, edge_cotangent, grid_send, grid_slot, grid_target,
    mesh_halo, mesh_send, mesh_slot, mesh_target, weights,
):
    peers = lax.axis_size("face") * lax.axis_size("sub")
    mesh_rows, latent = mesh_latent.shape
    edges = grid_slot.shape[0]
    grid_scale = 1.0 / (edges * peers) ** 0.5
    edge_scale = 1.0 / (mesh_slot.shape[0] * peers) ** 0.5
    node_scale = 1.0 / (mesh_rows * peers) ** 0.5
    grid_table = grid_send.reshape(8, 128)
    halo_table = mesh_halo.reshape(2, 128)
    far_table = mesh_send[0].T
    gslot, gtarget = grid_slot.reshape(8, 128), grid_target.reshape(8, 128)
    mslot, mtarget = mesh_slot.reshape(8, 128), mesh_target.reshape(8, 128)
    big, small, halo = (edges, latent), (mesh_rows, latent), (64, latent)
    vm = pltpu.VMEM

    project, *outgoing = call(
        project_body, [((512, latent), bf16)] + [((256, latent), bf16)] * 4,
        (grid_latent, grid_table), weights, (0,), name="project",
    )
    arrived = outgoing_rows(outgoing)
    own, edge_pre = call(
        encode_own_body, [(big, f32)] * 2, (project, gslot, gtarget, mesh_latent, edge_latent),
        weights, (1, 3), flops=2 * 10**9, name="encode_own",
    )
    pre, linear, hidden, middle, sender, *halos, far_out = call(
        encode_body,
        [(big, f32), (big, f32), (big, bf16), (small, bf16), (small, bf16)] + [(halo, bf16)] * 4 + [((2048, 128), bf16)],
        (own, *arrived, gslot, gtarget, mesh_latent, halo_table, far_table), weights, (2, 4),
        scratch=(vm(small, f32), vm((2048, 128), f32)), flops=2 * 10**9, name="encode",
    )
    far_in = lax.all_to_all(far_out.reshape(peers, 16, 128), AXES, 0, 0, tiled=True).reshape(2048, 128)
    halo_in = outgoing_rows(halos)
    own, update_own = call(
        process_own_body, [(big, f32), (small, f32)], (middle, sender, edge_pre, mslot, mtarget),
        weights, (5, 7), name="process_own",
    )
    (
        mesh_update, phidden, rounded, uhidden, cot_linear, cot_update, plinear, cround, receive, sender_own,
        *halos, far_out,
    ) = call(
        process_body,
        [(small, bf16), (big, bf16)] + [(small, bf16)] * 4 + [(big, bf16)] * 2
        + [(small, bf16), (small, f32)] + [(halo, bf16)] * 4 + [((2048, 128), bf16)],
        (own, *halo_in, far_in, mslot, mtarget, middle, update_own, mesh_cotangent, edge_cotangent),
        weights, (6, 8, 9),
        scratch=(
            vm((768, latent), bf16), vm(big, f32), vm(big, f32), vm((edges, 128), f32), vm(big, bf16),
            vm(small, f32), vm((2048, 128), f32), vm((8, 128), jnp.int32),
        ),
        flops=8 * 10**9, name="process",
    )
    far_back = lax.all_to_all(far_out.reshape(peers, 16, 128), AXES, 0, 0, tiled=True).reshape(2048, 128)
    halo_back = returned_rows(halos)
    edge_grad, middle_part, process_grads = call(
        scaled(process_grads_body, [edge_scale] * 3 + [node_scale] * 3),
        [(big, bf16), (small, f32), ((6, latent, latent), bf16)],
        (edge_latent, cround, phidden, plinear, middle, receive, cot_update, rounded, uhidden, cot_linear,
         edge_cotangent, mesh_cotangent),
        weights, (3, 5, 7), flops=3 * 10**9, name="process_grads",
    )
    process_grads = lax.psum(process_grads, AXES)
    cot_sender, cot_middle, elinear, upper, lower, *partials = call(
        encode_back_body,
        [(small, bf16), (small, f32), (big, bf16), (big, bf16), (big, bf16)] + [((256, latent), bf16)] * 4,
        (*halo_back, far_back, halo_table, far_table, sender_own, middle_part, pre, linear, gslot, gtarget),
        weights, (2, 4), scratch=(vm((768, latent), bf16), vm((2048, 128), f32)), flops=4 * 10**9, name="encode_back",
    )
    partials = returned_rows(partials)
    grid_own, mesh_grad, encode_grads = call(
        scaled(encode_grads_body, [grid_scale, grid_scale, edge_scale]),
        [((512, latent), f32), (small, bf16), ((3, latent, latent), bf16)],
        (upper, lower, gslot, gtarget, cot_middle, mesh_latent, middle, cot_sender, hidden, elinear),
        weights, (1,), flops=2 * 10**9, name="encode_grads",
    )
    grid_grad, grid_wgrad = call(
        scaled(grid_back_body, [grid_scale]), [((512, latent), bf16), ((latent, latent), bf16)],
        (grid_own, *partials, grid_table, grid_latent), weights, (0,),
        scratch=(vm((512, latent), bf16),), name="grid_back",
    )
    late, process_grads = lax.optimization_barrier(
        (jnp.concatenate([grid_wgrad[None], encode_grads], axis=0), process_grads)
    )
    late = lax.psum(late, AXES)
    weight_grads = jnp.stack(
        [late[0], late[3], late[1], process_grads[0], late[2], process_grads[1], process_grads[2],
         process_grads[3], process_grads[4], process_grads[5]]
    )
    return (mesh_update, grid_grad, mesh_grad, edge_grad, weight_grads)


def solution(mesh):
    row = P(AXES, None)
    return jax.shard_map(
        on_device,
        mesh=mesh,
        in_specs=(row, row, row, row, row, P(AXES, None, None), P(AXES), P(AXES), P(AXES, None, None),
                  P(AXES, None, None), P(AXES), P(AXES), P()),
        out_specs=(row, row, row, row, P()),
        check_vma=False,
    )
```

profile of v0, /device:TPU:1, one launch (start us, length us, event | category | flops | bytes accessed | tf_op | source)
XLA Modules:
  0.0 427.5 jit_solution(15068623087624820498)
XLA Ops:
  7.9 2.5 copy-done
  11.4 2.1 project.1
  14.3 2.5 collective-permute-start
  16.7 4.6 %collective-permute-start.1 = (bf16[256,512]{1,0:T(8,128)(2,1)}, bf16[256,512]{1,0:T(8,128)(2,1)}, u32[]{:S(2)}, u32[]{:S(2)}) collective-permute-start(bf16[256,512]{1,0:T(8,128)(2,1)} %get-tuple-element.61), channel_id=1, source_target_pairs={{0,15},{1,0},{2,1},{3,2},{4,3},{5,4},{6,5},{7,6},{8,7},{9,8},{10,9... | collective-permute-start | bytes 786440 | tf_op jit(solution)/shard_map/ppermute | solution.py:20
  21.3 2.1 collective-permute-start.2
  23.5 2.5 copy-done.1
  27.0 2.7 encode_own.1
  31.1 7.2 %encode.1 = (f32[1024,512]{1,0:T(8,128)S(1)}, f32[1024,512]{1,0:T(8,128)S(1)}, bf16[1024,512]{1,0:T(8,128)(2,1)S(1)}, bf16[128,512]{1,0:T(8,128)(2,1)S(1)}, bf16...) custom-call(f32[1024,512]{1,0:T(8,128)S(1)} %get-tuple-element.59.ow, ...), custom_call_target="tpu_custom_call" | custom-call | flops 2000000000 | bytes 10628096 | tf_op jit(solution)/shard_map/encode/pallas_call | solution.py:121
  42.0 6.7 %all-to-all-start = ((bf16[128,16,128]{2,1,0:T(8,128)(2,1)}), bf16[128,16,128]{2,1,0:T(8,128)(2,1)}, u32[]{:S(2)}, u32[]{:S(2)}) async-start(bf16[128,16,128]{2,1,0:T(8,128)(2,1)} %bitcast.15), calls=%async_computation | async-start | bytes 1048576 | tf_op jit(solution)/shard_map/all_to_all | solution.py:390
  50.3 4.3 %collective-permute-start.5 = (bf16[64,512]{1,0:T(8,128)(2,1)}, bf16[64,512]{1,0:T(8,128)(2,1)S(1)}, u32[]{:S(2)}, u32[]{:S(2)}) collective-permute-start(bf16[64,512]{1,0:T(8,128)(2,1)} %get-tuple-element.69), channel_id=1, source_target_pairs={{0,15},{1,0},{2,1},{3,2},{4,3},{5,4},{6,5},{7,6},{8,7},{9,8},{10,9... | collective-permute-start | bytes 196616 | tf_op jit(solution)/shard_map/ppermute | solution.py:20
  56.4 2.5 copy-done.2
  62.7 1.9 process_own.1
  69.2 2.5 copy-done.3
  80.2 13.0 %process.1 = (bf16[128,512]{1,0:T(8,128)(2,1)}, bf16[1024,512]{1,0:T(8,128)(2,1)S(1)}, bf16[128,512]{1,0:T(8,128)(2,1)S(1)}, bf16[128,512]{1,0:T(8,128)(2,1)S(1)...) custom-call(f32[1024,512]{1,0:T(8,128)S(1)} %copy-done.41, ...), custom_call_target="tpu_custom_call" | custom-call | flops 8000000000 | bytes 11018240 | tf_op jit(solution)/shard_map/process/pallas_call | solution.py:121
  93.3 6.1 %process_grads.1 = (bf16[1024,512]{1,0:T(8,128)(2,1)}, f32[128,512]{1,0:T(8,128)S(1)}, bf16[6,512,512]{2,1,0:T(8,128)(2,1)S(1)}) custom-call(bf16[1024,512]{1,0:T(8,128)(2,1)S(1)} %copy-done.4, bf16[1024,512]{1,0:T(8,128)(2,1)S(1)} %get-tuple-element.81.cround, bf16[1024,512]{1,0:T(8,128)(2,1)S(1)} %get-tuple-element.82.hidden, ...), custom_call_target="tpu_custom_call" | custom-call | flops 3000000000 | bytes 12189696 | tf_op jit(solution)/shard_map/process_grads/pallas_call | solution.py:121
  101.8 6.5 %all-to-all-start.1 = ((bf16[128,16,128]{2,1,0:T(8,128)(2,1)}), bf16[128,16,128]{2,1,0:T(8,128)(2,1)}, u32[]{:S(2)}, u32[]{:S(2)}) async-start(bf16[128,16,128]{2,1,0:T(8,128)(2,1)} %bitcast.14), calls=%async_computation.1 | async-start | bytes 1048576 | tf_op jit(solution)/shard_map/all_to_all | solution.py:411
  108.4 5.8 %collective-permute-start.8 = (bf16[64,512]{1,0:T(8,128)(2,1)}, bf16[64,512]{1,0:T(8,128)(2,1)S(1)}, u32[]{:S(2)}, u32[]{:S(2)}) collective-permute-start(bf16[64,512]{1,0:T(8,128)(2,1)} %get-tuple-element.75), channel_id=1, source_target_pairs={{0,15},{1,0},{2,1},{3,2},{4,3},{5,4},{6,5},{7,6},{8,7},{9,8},{10,9... | collective-permute-start | bytes 196616 | tf_op jit(solution)/shard_map/ppermute | solution.py:20
  117.4 6.0 %collective-permute-done.9.in1 = bf16[64,512]{1,0:T(8,128)(2,1)S(1)} collective-permute-done((bf16[64,512]{1,0:T(8,128)(2,1)}, bf16[64,512]{1,0:T(8,128)(2,1)S(1)}, u32[]{:S(2)}, u32[]{:S(2)}) %collective-permute-start.9) | collective-permute-done | bytes 65568 | tf_op jit(solution)/shard_map/ppermute | solution.py:20
  130.6 7.9 %encode_back.1 = (bf16[128,512]{1,0:T(8,128)(2,1)S(1)}, f32[128,512]{1,0:T(8,128)S(1)}, bf16[1024,512]{1,0:T(8,128)(2,1)S(1)}, bf16[1024,512]{1,0:T(8,128)(2,1)S...) custom-call(bf16[64,512]{1,0:T(8,128)(2,1)S(1)} %collective-permute-, ...), custom_call_target="tpu_custom_call" | custom-call | flops 4000000000 | bytes 11152384 | tf_op jit(solution)/shard_map/encode_back/pallas_call | solution.py:121
  141.9 3.1 encode_grads.1
  147.5 2.1 grid_back.1
  151.1 107.0 %all-reduce.3.cloned.1.call-done = bf16[6,512,512]{2,1,0:T(8,128)(2,1)} async-done(((bf16[6,512,512]{2,1,0:T(8,128)(2,1)}), bf16[6,512,512]{2,1,0:T(8,128)(2,1)}) %all-reduce.3.cloned.1.call-update) | async-done | bytes 3145744 | tf_op jit(solution)/shard_map/psum | solution.py:420
  258.2 154.3 %all-reduce.5.cloned.1.call-done = bf16[4,512,512]{2,1,0:T(8,128)(2,1)} async-done(((bf16[4,512,512]{2,1,0:T(8,128)(2,1)}), bf16[4,512,512]{2,1,0:T(8,128)(2,1)}) %all-reduce.5.cloned.1.call-update) | async-done | bytes 2097168 | tf_op jit(solution)/shard_map/psum | solution.py:442
  418.3 2.3 copy-done.56
  (157 shorter events, 55.2 us)
Async XLA Ops:
  7.2 16.3 %copy-start.33 = (s32[1024]{0:T(1024)S(1)}, s32[1024]{0:T(1024)}, u32[]{:S(2)}) copy-start(s32[1024]{0:T(1024)} %param.20) | copy-start | bytes 12292
  7.2 16.3 %copy-start.32 = (s32[1024]{0:T(1024)S(1)}, s32[1024]{0:T(1024)}, u32[]{:S(2)}) copy-start(s32[1024]{0:T(1024)} %param.19) | copy-start | bytes 12292
  14.3 16.8 %collective-permute-start = (bf16[256,512]{1,0:T(8,128)(2,1)}, bf16[256,512]{1,0:T(8,128)(2,1)}, u32[]{:S(2)}, u32[]{:S(2)}) collective-permute-start(bf16[256,512]{1,0:T(8,128)(2,1)} %get-tuple-element.60), channel_id=1, source_target_pairs={{0,1},{1,2},{2,3},{3,4},{4,5},{5,6},{6,7},{7,8},{8,9},{9,10},{10,1... | collective-permute-start | bytes 786440 | tf_op jit(solution)/shard_map/ppermute | solution.py:20
  16.7 14.3 %collective-permute-start.1 = (bf16[256,512]{1,0:T(8,128)(2,1)}, bf16[256,512]{1,0:T(8,128)(2,1)}, u32[]{:S(2)}, u32[]{:S(2)}) collective-permute-start(bf16[256,512]{1,0:T(8,128)(2,1)} %get-tuple-element.61), channel_id=1, source_target_pairs={{0,15},{1,0},{2,1},{3,2},{4,3},{5,4},{6,5},{7,6},{8,7},{9,8},{10,9... | collective-permute-start | bytes 786440 | tf_op jit(solution)/shard_map/ppermute | solution.py:20
  21.3 9.8 %collective-permute-start.2 = (bf16[256,512]{1,0:T(8,128)(2,1)}, bf16[256,512]{1,0:T(8,128)(2,1)}, u32[]{:S(2)}, u32[]{:S(2)}) collective-permute-start(bf16[256,512]{1,0:T(8,128)(2,1)} %get-tuple-element.62), channel_id=1, source_target_pairs={{0,16},{16,32},{32,48},{48,64},{64,80},{80,96},{96,112},{112,0},{1... | collective-permute-start | bytes 786440 | tf_op jit(solution)/shard_map/ppermute | solution.py:20
  23.4 7.7 %collective-permute-start.3 = (bf16[256,512]{1,0:T(8,128)(2,1)}, bf16[256,512]{1,0:T(8,128)(2,1)}, u32[]{:S(2)}, u32[]{:S(2)}) collective-permute-start(bf16[256,512]{1,0:T(8,128)(2,1)} %get-tuple-element.63), channel_id=1, source_target_pairs={{0,112},{16,0},{32,16},{48,32},{64,48},{80,64},{96,80},{112,96},{1... | collective-permute-start | bytes 786440 | tf_op jit(solution)/shard_map/ppermute | solution.py:20
  42.0 27.2 %all-to-all-start = ((bf16[128,16,128]{2,1,0:T(8,128)(2,1)}), bf16[128,16,128]{2,1,0:T(8,128)(2,1)}, u32[]{:S(2)}, u32[]{:S(2)}) async-start(bf16[128,16,128]{2,1,0:T(8,128)(2,1)} %bitcast.15), calls=%async_computation | async-start | bytes 1048576 | tf_op jit(solution)/shard_map/all_to_all | solution.py:390
  48.7 209.4 %all-reduce.3.cloned.1.call-start = ((), (), s32[]{:S(2)}) async-start(), calls=%async_computation.2 | async-start | bytes 6291456 | tf_op jit(solution)/shard_map/psum | solution.py:420
  48.8 18.0 %collective-permute-start.4 = (bf16[64,512]{1,0:T(8,128)(2,1)}, bf16[64,512]{1,0:T(8,128)(2,1)S(1)}, u32[]{:S(2)}, u32[]{:S(2)}) collective-permute-start(bf16[64,512]{1,0:T(8,128)(2,1)} %get-tuple-element.68), channel_id=1, source_target_pairs={{0,1},{1,2},{2,3},{3,4},{4,5},{5,6},{6,7},{7,8},{8,9},{9,10},{10,1... | collective-permute-start | bytes 196616 | tf_op jit(solution)/shard_map/ppermute | solution.py:20
  50.3 17.1 %collective-permute-start.5 = (bf16[64,512]{1,0:T(8,128)(2,1)}, bf16[64,512]{1,0:T(8,128)(2,1)S(1)}, u32[]{:S(2)}, u32[]{:S(2)}) collective-permute-start(bf16[64,512]{1,0:T(8,128)(2,1)} %get-tuple-element.69), channel_id=1, source_target_pairs={{0,15},{1,0},{2,1},{3,2},{4,3},{5,4},{6,5},{7,6},{8,7},{9,8},{10,9... | collective-permute-start | bytes 196616 | tf_op jit(solution)/shard_map/ppermute | solution.py:20
  54.6 13.4 %collective-permute-start.6 = (bf16[64,512]{1,0:T(8,128)(2,1)}, bf16[64,512]{1,0:T(8,128)(2,1)S(1)}, u32[]{:S(2)}, u32[]{:S(2)}) collective-permute-start(bf16[64,512]{1,0:T(8,128)(2,1)} %get-tuple-element.70), channel_id=1, source_target_pairs={{0,16},{16,32},{32,48},{48,64},{64,80},{80,96},{96,112},{112,0},{1... | collective-permute-start | bytes 196616 | tf_op jit(solution)/shard_map/ppermute | solution.py:20
  56.4 12.2 %collective-permute-start.7 = (bf16[64,512]{1,0:T(8,128)(2,1)}, bf16[64,512]{1,0:T(8,128)(2,1)S(1)}, u32[]{:S(2)}, u32[]{:S(2)}) collective-permute-start(bf16[64,512]{1,0:T(8,128)(2,1)} %get-tuple-element.71), channel_id=1, source_target_pairs={{0,112},{16,0},{32,16},{48,32},{64,48},{80,64},{96,80},{112,96},{1... | collective-permute-start | bytes 196616 | tf_op jit(solution)/shard_map/ppermute | solution.py:20
  80.2 13.0 %copy-start.16 = (bf16[1024,512]{1,0:T(8,128)(2,1)S(1)}, bf16[1024,512]{1,0:T(8,128)(2,1)}, u32[]{:S(2)}) copy-start(bf16[1024,512]{1,0:T(8,128)(2,1)} %edge_cot.3) | copy-start | bytes 3145732
  101.8 40.1 %slice-start = ((s8[5242880]{0:T(1024)(128)(4,1)}), s8[1048576]{0:T(1024)(128)(4,1)S(1)}, s32[]{:S(2)}) async-start(s8[5242880]{0:T(1024)(128)(4,1)} %bitcast.12), calls=%async_computation.4 | async-start | bytes 2097152
  101.8 22.9 %all-to-all-start.1 = ((bf16[128,16,128]{2,1,0:T(8,128)(2,1)}), bf16[128,16,128]{2,1,0:T(8,128)(2,1)}, u32[]{:S(2)}, u32[]{:S(2)}) async-start(bf16[128,16,128]{2,1,0:T(8,128)(2,1)} %bitcast.14), calls=%async_computation.1 | async-start | bytes 1048576 | tf_op jit(solution)/shard_map/all_to_all | solution.py:411
  108.3 304.1 %all-reduce.5.cloned.1.call-start = ((), (), s32[]{:S(2)}) async-start(), calls=%async_computation.3 | async-start | bytes 4194304 | tf_op jit(solution)/shard_map/psum | solution.py:442
  108.4 9.1 %collective-permute-start.8 = (bf16[64,512]{1,0:T(8,128)(2,1)}, bf16[64,512]{1,0:T(8,128)(2,1)S(1)}, u32[]{:S(2)}, u32[]{:S(2)}) collective-permute-start(bf16[64,512]{1,0:T(8,128)(2,1)} %get-tuple-element.75), channel_id=1, source_target_pairs={{0,15},{1,0},{2,1},{3,2},{4,3},{5,4},{6,5},{7,6},{8,7},{9,8},{10,9... | collective-permute-start | bytes 196616 | tf_op jit(solution)/shard_map/ppermute | solution.py:20
  114.1 9.3 %collective-permute-start.9 = (bf16[64,512]{1,0:T(8,128)(2,1)}, bf16[64,512]{1,0:T(8,128)(2,1)S(1)}, u32[]{:S(2)}, u32[]{:S(2)}) collective-permute-start(bf16[64,512]{1,0:T(8,128)(2,1)} %copy-done.46), channel_id=1, source_target_pairs={{0,1},{1,2},{2,3},{3,4},{4,5},{5,6},{6,7},{7,8},{8,9},{9,10},{10,1... | collective-permute-start | bytes 196616 | tf_op jit(solution)/shard_map/ppermute | solution.py:20
  114.1 9.3 %collective-permute-start.10 = (bf16[64,512]{1,0:T(8,128)(2,1)}, bf16[64,512]{1,0:T(8,128)(2,1)S(1)}, u32[]{:S(2)}, u32[]{:S(2)}) collective-permute-start(bf16[64,512]{1,0:T(8,128)(2,1)} %copy-done.45), channel_id=1, source_target_pairs={{0,112},{16,0},{32,16},{48,32},{64,48},{80,64},{96,80},{112,96},{1... | collective-permute-start | bytes 196616 | tf_op jit(solution)/shard_map/ppermute | solution.py:20
  114.8 9.3 %collective-permute-start.11 = (bf16[64,512]{1,0:T(8,128)(2,1)}, bf16[64,512]{1,0:T(8,128)(2,1)S(1)}, u32[]{:S(2)}, u32[]{:S(2)}) collective-permute-start(bf16[64,512]{1,0:T(8,128)(2,1)} %copy-done.44), channel_id=1, source_target_pairs={{0,16},{16,32},{32,48},{48,64},{64,80},{80,96},{96,112},{112,0},{1... | collective-permute-start | bytes 196616 | tf_op jit(solution)/shard_map/ppermute | solution.py:20
  138.5 7.4 %collective-permute-start.12 = (bf16[256,512]{1,0:T(8,128)(2,1)S(1)}, bf16[256,512]{1,0:T(8,128)(2,1)S(1)}, u32[]{:S(2)}, u32[]{:S(2)}) collective-permute-start(bf16[256,512]{1,0:T(8,128)(2,1)S(1)} %get-tuple-element.99), channel_id=1, source_target_pairs={{0,15},{1,0},{2,1},{3,2},{4,3},{5,4},{6,5},{7,6},{8,7},{9,8},{10,9... | collective-permute-start | bytes 786440 | tf_op jit(solution)/shard_map/ppermute | solution.py:20
  138.6 8.8 %collective-permute-start.13 = (bf16[256,512]{1,0:T(8,128)(2,1)S(1)}, bf16[256,512]{1,0:T(8,128)(2,1)S(1)}, u32[]{:S(2)}, u32[]{:S(2)}) collective-permute-start(bf16[256,512]{1,0:T(8,128)(2,1)S(1)} %get-tuple-element.100), channel_id=1, source_target_pairs={{0,1},{1,2},{2,3},{3,4},{4,5},{5,6},{6,7},{7,8},{8,9},{9,10},{10,1... | collective-permute-start | bytes 786440 | tf_op jit(solution)/shard_map/ppermute | solution.py:20
  140.1 7.4 %collective-permute-start.14 = (bf16[256,512]{1,0:T(8,128)(2,1)S(1)}, bf16[256,512]{1,0:T(8,128)(2,1)S(1)}, u32[]{:S(2)}, u32[]{:S(2)}) collective-permute-start(bf16[256,512]{1,0:T(8,128)(2,1)S(1)} %get-tuple-element.101), channel_id=1, source_target_pairs={{0,112},{16,0},{32,16},{48,32},{64,48},{80,64},{96,80},{112,96},{1... | collective-permute-start | bytes 786440 | tf_op jit(solution)/shard_map/ppermute | solution.py:20
  141.6 5.8 %collective-permute-start.15 = (bf16[256,512]{1,0:T(8,128)(2,1)S(1)}, bf16[256,512]{1,0:T(8,128)(2,1)S(1)}, u32[]{:S(2)}, u32[]{:S(2)}) collective-permute-start(bf16[256,512]{1,0:T(8,128)(2,1)S(1)} %get-tuple-element.102), channel_id=1, source_target_pairs={{0,16},{16,32},{32,48},{48,64},{64,80},{80,96},{96,112},{112,0},{1... | collective-permute-start | bytes 786440 | tf_op jit(solution)/shard_map/ppermute | solution.py:20
  (56 other events, 157.7 us)
Sparse Core Ops, SparseCore 0:
  101.9 156.1 all-reduce.2
  263.0 149.4 all-reduce.4
where the time goes:
time: 429 us; the launch traced here: 427 us
  waiting for transfers between devices  271 us (63%)
  local copies, waits for them, and re-layouts  53.3 us (12%)
  Pallas kernels  46.1 us (11%)
  starting transfers between devices  40.8 us (10%)
  between operations  14.4 us (3%)
    psum x1, waiting for transfers between devices, on_device(): late = lax.psum(late, AXES)  154 us
    psum x1, waiting for transfers between devices, on_device(): process_grads = lax.psum(process_grads, AXES)  107 us
    unnamed x125, local copies, waits for them, and re-layouts  52.3 us
    pallas_call x9, Pallas kernels, call(): pl.pallas_call(body, grid=(1,), out_shape=shapes, in_specs=in_specs, out_...  46.1 us
    ppermute x16, starting transfers between devices, shifted(): return lax.ppermute(value, axis, pairs)  27.6 us
    all_to_all x2, starting transfers between devices, on_device(): lax.all_to_all(far_out.reshape(peers, 16, 128), AXES, 0, 0, tiled=True)  13.1 us
    ppermute x16, waiting for transfers between devices, shifted(): return lax.ppermute(value, axis, pairs)  10.1 us
  transfers between devices with their start and end apart: 20, of which 6 were waited for; matrix products, arithmetic and copies ran while one was open for 0% of the time, Pallas kernels for 4%

commit v1 on v0

--- a/solution.py
+++ b/solution.py
@@ -10,7 +10,10 @@
 norm_eps = 1e-05
 f32 = jnp.float32
 bf16 = jnp.bfloat16
-AXES = ("face", "sub")
+AXES = ("x", "core", "y", "z")
+CHIPS = ("x", "y", "z")
+FACE = ("x", "core")
+SUB = ("y", "z")
 CHUNK = 256
 
 
@@ -21,12 +24,12 @@
 
 
 def outgoing_rows(blocks):
-    routes = (("sub", 1), ("sub", -1), ("face", 1), ("face", -1))
+    routes = ((SUB, 1), (SUB, -1), (FACE, 1), (FACE, -1))
     return [shifted(block, axis, step) for block, (axis, step) in zip(blocks, routes)]
 
 
 def returned_rows(blocks):
-    routes = (("sub", -1), ("sub", 1), ("face", -1), ("face", 1))
+    routes = ((SUB, -1), (SUB, 1), (FACE, -1), (FACE, 1))
     return [shifted(block, axis, step) for block, (axis, step) in zip(blocks, routes)]
 
 
@@ -108,9 +111,11 @@
     lax.fori_loop(0, count, step, 0)
 
 
-def call(body, outs, args, weights=None, picks=(), scratch=(), flops=10**9, vmem=40 << 20, name=None):
-    whole = pl.BlockSpec(memory_space=pltpu.VMEM)
-    in_specs = [whole] * len(args)
+def call(body, outs, args, weights=None, picks=(), scratch=(), flops=10**9, vmem=67000000, name=None):
+    def whole(shape):
+        return pl.BlockSpec(shape, lambda i: (0,) * len(shape))
+
+    in_specs = [whole(a.shape) for a in args]
     for k in picks:
         in_specs.append(
             pl.BlockSpec((None, weights.shape[1], weights.shape[2]), functools.partial(lambda k, i: (k, 0, 0), k))
@@ -123,7 +128,7 @@
         grid=(1,),
         out_shape=shapes,
         in_specs=in_specs,
-        out_specs=[whole] * len(shapes),
+        out_specs=[whole(s.shape) for s in shapes],
         scratch_shapes=list(scratch),
         compiler_params=pltpu.CompilerParams(vmem_limit_bytes=vmem),
         cost_estimate=pl.CostEstimate(flops=flops, bytes_accessed=total, transcendentals=0),
@@ -137,7 +142,7 @@
         out[...] = dot(pick(table, 2 * k, 2, 0, 512), project[...]).astype(bf16)
 
 
-def encode_own_body(project, slot, target, mesh, edge, w1, w3, own, edge_pre):
+def encode_own_body(project, slot, target, mesh, w1, own):
     upper, lower = halves(dot(mesh[...], w1[...]))
 
     def step(i, s):
@@ -145,7 +150,6 @@
         own[s, :] = (
             dot(pick(slot, 2 * i, 2, 0, 512), project[...]) + dot(receiver, upper) + dot(receiver, lower)
         )
-        edge_pre[s, :] = dot(edge[s, :], w3[...])
 
     chunks(4, step)
 
@@ -189,14 +193,14 @@
     far_out[...] = wide[...].astype(bf16)
 
 
-def process_own_body(middle, sender, edge_pre, slot, target, w5, w7, own, update_own):
+def process_own_body(middle, sender, edge, slot, target, w3, w5, w7, own, update_own):
     upper, lower = halves(dot(middle[...], w5[...]))
     update_own[...] = dot(middle[...], w7[...])
 
     def step(i, s):
         receiver = pick(target, 2 * i, 2, 0, 128)
         own[s, :] = (
-            edge_pre[s, :] + dot(pick(slot, 2 * i, 2, 0, 128), sender[...]) + dot(receiver, upper) + dot(receiver, lower)
+            dot(edge[s, :], w3[...]) + dot(pick(slot, 2 * i, 2, 0, 128), sender[...]) + dot(receiver, upper) + dot(receiver, lower)
         )
 
     chunks(4, step)
@@ -276,13 +280,21 @@
     far_out[...] = wide[...].astype(bf16)
 
 
+def store_blocks(out, k, term):
+    rows = term.astype(bf16).reshape(4, 8, 16, 512)
+    for c in range(2):
+        for q in range(2):
+            first = 128 * (2 * c + q)
+            out[:, c, :, q, k, :, :] = rows[:, :, :, first : first + 128]
+
+
 def process_grads_body(
     scales, edge, cround, hidden, plinear, middle, receive, cot_update, rounded, uhidden, cot_linear, edge_cot, mesh_cot,
     w3, w5, w7, edge_grad, middle_part, grads,
 ):
     pairs = ((edge, cround), (middle, receive), (hidden, plinear), (middle, cot_update), (rounded, cot_update), (uhidden, cot_linear))
     for k, (x, y) in enumerate(pairs):
-        grads[k] = (dot_tn(x[...], y[...]) * scales[k]).astype(bf16)
+        store_blocks(grads, k, dot_tn(x[...], y[...]) * scales[k])
     middle_part[...] = mesh_cot[...].astype(f32) + dot_nt(cot_update[...], w7[...]) + dot_nt(receive[...], w5[...])
 
     def step(i, s):
@@ -326,18 +338,18 @@
     scales, upper, lower, slot, target, cot_middle, mesh, middle, cot_sender, hidden, elinear, w1,
     grid_own, mesh_grad, grads,
 ):
-    grads[0] = (dot_tn(hidden[...], elinear[...]) * scales[1]).astype(bf16)
-    grads[1] = (dot_tn(middle[...], cot_sender[...]) * scales[2]).astype(bf16)
+    grads[1] = (dot_tn(hidden[...], elinear[...]) * scales[1]).astype(bf16)
+    grads[2] = (dot_tn(middle[...], cot_sender[...]) * scales[2]).astype(bf16)
     kept = put(target, 0, 8, 0, 128)
     receive = (dot(kept, upper[...]) + dot(kept, lower[...])).astype(bf16)
-    grads[2] = (dot_tn(mesh[...], receive) * scales[0]).astype(bf16)
+    grads[0] = (dot_tn(mesh[...], receive) * scales[0]).astype(bf16)
     mesh_grad[...] = (cot_middle[...] + dot_nt(receive, w1[...])).astype(bf16)
     for k in range(2):
         kept = put(slot, 0, 8, 256 * k, 256)
         grid_own[256 * k : 256 * k + 256, :] = dot(kept, upper[...]) + dot(kept, lower[...])
 
 
-def grid_back_body(scales, grid_own, in0, in1, in2, in3, table, grid, w0, grid_grad, grads, cot):
+def grid_back_body(scales, grid_own, in0, in1, in2, in3, table, grid, others, w0, grid_grad, grads, cot):
     def step(i, s):
         total = grid_own[s, :]
         for k, block in enumerate((in0, in1, in2, in3)):
@@ -347,7 +359,46 @@
         grid_grad[s, :] = dot_nt(total, w0[...]).astype(bf16)
 
     chunks(2, step)
-    grads[...] = (dot_tn(grid[...], cot[...]) * scales[0]).astype(bf16)
+    store_blocks(grads, 0, dot_tn(grid[...], cot[...]) * scales[0])
+    for k in range(3):
+        store_blocks(grads, k + 1, others[k])
+
+
+def sum_body(terms, shard):
+    total = terms[0].astype(f32)
+    for d in range(1, terms.shape[0]):
+        total = total + terms[d].astype(f32)
+    total = total.astype(bf16)
+    for p in range(shard.shape[0]):
+        shard[p] = total
+
+
+def assemble_body(order, core, *refs):
+    out = refs[-1]
+    first = core[0] == 0
+    place = 0
+    for own, other in (refs[0:2], refs[2:4]):
+        for k in range(own.shape[2]):
+            for q in range(2):
+                a, b = own[:, q, k].reshape(512, 128), other[:, q, k].reshape(512, 128)
+                out[order[place], :, 128 * q : 128 * q + 128] = jnp.where(first, a, b)
+                out[order[place], :, 256 + 128 * q : 384 + 128 * q] = jnp.where(first, b, a)
+            place += 1
+
+
+def summed_blocks(terms, name):
+    count = terms.shape[4]
+    with jax.named_scope(name):
+        terms = lax.all_to_all(terms.reshape(128, count * 16, 128), AXES, 0, 0, tiled=True)
+    (shard,) = call(
+        sum_body, [((64, count * 16, 128), bf16)], (terms,), flops=10**7, name=name + "_sum",
+    )
+    with jax.named_scope(name + "_spread"):
+        own = lax.all_to_all(shard, CHIPS, 0, 0, tiled=True)
+    with jax.named_scope(name + "_pair"):
+        other = lax.ppermute(own, "core", [(0, 1), (1, 0)])
+    shape = (32, 2, count, 16, 128)
+    return own.reshape(shape), other.reshape(shape)
 
 
 def scaled(body, scales):
@@ -358,7 +409,7 @@
     grid_latent, mesh_latent, edge_latent, mesh_cotangent, edge_cotangent, grid_send, grid_slot, grid_target,
     mesh_halo, mesh_send, mesh_slot, mesh_target, weights,
 ):
-    peers = lax.axis_size("face") * lax.axis_size("sub")
+    peers = lax.axis_size(AXES)
     mesh_rows, latent = mesh_latent.shape
     edges = grid_slot.shape[0]
     grid_scale = 1.0 / (edges * peers) ** 0.5
@@ -370,6 +421,7 @@
     gslot, gtarget = grid_slot.reshape(8, 128), grid_target.reshape(8, 128)
     mslot, mtarget = mesh_slot.reshape(8, 128), mesh_target.reshape(8, 128)
     big, small, halo = (edges, latent), (mesh_rows, latent), (64, latent)
+    block = (4, 2, 8, 2)
     vm = pltpu.VMEM
 
     project, *outgoing = call(
@@ -377,9 +429,9 @@
         (grid_latent, grid_table), weights, (0,), name="project",
     )
     arrived = outgoing_rows(outgoing)
-    own, edge_pre = call(
-        encode_own_body, [(big, f32)] * 2, (project, gslot, gtarget, mesh_latent, edge_latent),
-        weights, (1, 3), flops=2 * 10**9, name="encode_own",
+    (own,) = call(
+        encode_own_body, [(big, f32)], (project, gslot, gtarget, mesh_latent),
+        weights, (1,), flops=10**9, name="encode_own",
     )
     pre, linear, hidden, middle, sender, *halos, far_out = call(
         encode_body,
@@ -390,8 +442,8 @@
     far_in = lax.all_to_all(far_out.reshape(peers, 16, 128), AXES, 0, 0, tiled=True).reshape(2048, 128)
     halo_in = outgoing_rows(halos)
     own, update_own = call(
-        process_own_body, [(big, f32), (small, f32)], (middle, sender, edge_pre, mslot, mtarget),
-        weights, (5, 7), name="process_own",
+        process_own_body, [(big, f32), (small, f32)], (middle, sender, edge_latent, mslot, mtarget),
+        weights, (3, 5, 7), name="process_own",
     )
     (
         mesh_update, phidden, rounded, uhidden, cot_linear, cot_update, plinear, cround, receive, sender_own,
@@ -412,12 +464,12 @@
     halo_back = returned_rows(halos)
     edge_grad, middle_part, process_grads = call(
         scaled(process_grads_body, [edge_scale] * 3 + [node_scale] * 3),
-        [(big, bf16), (small, f32), ((6, latent, latent), bf16)],
+        [(big, bf16), (small, f32), (block + (6, 16, 128), bf16)],
         (edge_latent, cround, phidden, plinear, middle, receive, cot_update, rounded, uhidden, cot_linear,
          edge_cotangent, mesh_cotangent),
         weights, (3, 5, 7), flops=3 * 10**9, name="process_grads",
     )
-    process_grads = lax.psum(process_grads, AXES)
+    early = summed_blocks(process_grads, "early")
     cot_sender, cot_middle, elinear, upper, lower, *partials = call(
         encode_back_body,
         [(small, bf16), (small, f32), (big, bf16), (big, bf16), (big, bf16)] + [((256, latent), bf16)] * 4,
@@ -432,26 +484,34 @@
         weights, (1,), flops=2 * 10**9, name="encode_grads",
     )
     grid_grad, grid_wgrad = call(
-        scaled(grid_back_body, [grid_scale]), [((512, latent), bf16), ((latent, latent), bf16)],
-        (grid_own, *partials, grid_table, grid_latent), weights, (0,),
+        scaled(grid_back_body, [grid_scale]), [((512, latent), bf16), (block + (4, 16, 128), bf16)],
+        (grid_own, *partials, grid_table, grid_latent, encode_grads), weights, (0,),
         scratch=(vm((512, latent), bf16),), name="grid_back",
     )
-    late, process_grads = lax.optimization_barrier(
-        (jnp.concatenate([grid_wgrad[None], encode_grads], axis=0), process_grads)
-    )
-    late = lax.psum(late, AXES)
-    weight_grads = jnp.stack(
-        [late[0], late[3], late[1], process_grads[0], late[2], process_grads[1], process_grads[2],
-         process_grads[3], process_grads[4], process_grads[5]]
-    )
+    late = summed_blocks(grid_wgrad, "late")
+    core = lax.axis_index("core").reshape(1)
+    order = (3, 5, 6, 7, 8, 9, 0, 1, 2, 4)
+    weight_grads = pl.pallas_call(
+        functools.partial(assemble_body, order),
+        grid_spec=pltpu.PrefetchScalarGridSpec(
+            num_scalar_prefetch=1,
+            grid=(1,),
+            in_specs=[pl.BlockSpec(a.shape, lambda i, c: (0,) * 5) for a in (*early, *late)],
+            out_specs=pl.BlockSpec(weights.shape, lambda i, c: (0, 0, 0)),
+        ),
+        out_shape=jax.ShapeDtypeStruct(weights.shape, bf16),
+        compiler_params=pltpu.CompilerParams(vmem_limit_bytes=67000000),
+        name="assemble",
+    )(core, *early, *late)
     return (mesh_update, grid_grad, mesh_grad, edge_grad, weight_grads)
 
 
 def solution(mesh):
     row = P(AXES, None)
+    wide = jax.sharding.Mesh(mesh.devices.reshape(4, 2, 4, 4), AXES)
     return jax.shard_map(
         on_device,
-        mesh=mesh,
+        mesh=wide,
         in_specs=(row, row, row, row, row, P(AXES, None, None), P(AXES), P(AXES), P(AXES, None, None),
                   P(AXES, None, None), P(AXES), P(AXES), P()),
         out_specs=(row, row, row, row, P()),

time: 429 us -> 261 us (0.61)
  waiting for transfers between devices: 271 us -> 99.2 us
  local copies, waits for them, and re-layouts: 53.3 us -> 3.94 us
  starting transfers between devices: 40.8 us -> 75.6 us
  Pallas kernels: 46.1 us -> 80.7 us
  between operations: 14.4 us -> 0.77 us
    psum x2 -> x0, waiting for transfers between devices: 261 us -> none  [the longest x1 154 us: on_device(): late = lax.psum(late, AXES)]
    all_to_all x0 -> x4, waiting for transfers between devices: none -> 58.2 us  [the longest x2 32.8 us: summed_blocks(): own = lax.all_to_all(shard, CHIPS, 0, 0, tiled=True)]
    unnamed x125 -> x14, local copies, waits for them, and re-layouts: 52.3 us -> 2 us
    pallas_call x9 -> x11, Pallas kernels: 46.1 us -> 75 us  [call(): pl.pallas_call(body, grid=(1,), out_shape=shapes, in_specs=in_specs, out_...]
    all_to_all x0 -> x4, starting transfers between devices: none -> 27 us  [the longest x2 14.3 us: summed_blocks(): lax.all_to_all(terms.reshape(128, count * 16, 128), AXES, 0, 0, tiled=True)]
    ppermute x16, waiting for transfers between devices: 10.1 us -> 33.3 us  [shifted(): return lax.ppermute(value, axis, pairs)]
    pallas_call x0 -> x1, Pallas kernels: none -> 5.74 us  [on_device(): pl.pallas_call(functools.partial(assemble_body, order), grid_spec=pltpu.P...]
    all_to_all x2, waiting for transfers between devices: 0.01 us -> 5.48 us  [on_device(): lax.all_to_all(far_out.reshape(peers, 16, 128), AXES, 0, 0, tiled=True)]
  transfers between devices with their start and end apart: 20 -> 24, of which waited for: 6 -> 9; matrix products, arithmetic and copies ran while one was open for 0% -> 0% of each run, Pallas kernels for 4% -> 18%
where the time goes in v1:
time: 261 us; the launch traced here: 260 us
  waiting for transfers between devices  99.2 us (38%)
  Pallas kernels  80.7 us (31%)
  starting transfers between devices  75.6 us (29%)
  local copies, waits for them, and re-layouts  3.94 us (2%)
    pallas_call x11, Pallas kernels, call(): pl.pallas_call(body, grid=(1,), out_shape=shapes, in_specs=in_specs, out_...  75 us
    ppermute x16, waiting for transfers between devices, shifted(): return lax.ppermute(value, axis, pairs)  33.3 us
    all_to_all x2, waiting for transfers between devices, summed_blocks(): own = lax.all_to_all(shard, CHIPS, 0, 0, tiled=True)  32.8 us
    ppermute x16, starting transfers between devices, shifted(): return lax.ppermute(value, axis, pairs)  29 us
    all_to_all x2, waiting for transfers between devices, summed_blocks(): lax.all_to_all(terms.reshape(128, count * 16, 128), AXES, 0, 0, tiled=True)  25.5 us
    all_to_all x2, starting transfers between devices, on_device(): lax.all_to_all(far_out.reshape(peers, 16, 128), AXES, 0, 0, tiled=True)  14.6 us
    all_to_all x2, starting transfers between devices, summed_blocks(): lax.all_to_all(terms.reshape(128, count * 16, 128), AXES, 0, 0, tiled=True)  14.3 us
    all_to_all x2, starting transfers between devices, summed_blocks(): own = lax.all_to_all(shard, CHIPS, 0, 0, tiled=True)  12.7 us
  transfers between devices with their start and end apart: 24, of which 9 were waited for; matrix products, arithmetic and copies ran while one was open for 0% of the time, Pallas kernels for 18%

profile of v1, /device:TPU:1, one launch (start us, length us, event | category | flops | bytes accessed | tf_op | source)
XLA Modules:
  0.0 260.3 jit_solution(15257264524133159826)
XLA Ops:
  7.6 4.6 %collective-permute-start.1 = (bf16[256,512]{1,0:T(8,128)(2,1)}, bf16[256,512]{1,0:T(8,128)(2,1)}, u32[]{:S(2)}, u32[]{:S(2)}) collective-permute-start(bf16[256,512]{1,0:T(8,128)(2,1)} %get-tuple-element.56), channel_id=1, source_target_pairs={{0,15},{1,0},{2,1},{3,2},{4,3},{5,4},{6,5},{7,6},{8,7},{9,8},{10,9... | collective-permute-start | bytes 786440 | tf_op jit(solution)/shard_map/ppermute | solution.py:23
  14.9 4.8 %encode_own.1.own = f32[1024,512]{1,0:T(8,128)} custom-call(bf16[512,512]{1,0:T(8,128)(2,1)} %get-tuple-element.54.project, s32[8,128]{1,0:T(8,128)} %bitcast.24, s32[8,128]{1,0:T(8,128)} %bitcast.28, bf16[128,512]{1,0:T(8,128)(2,1)} %mesh.5, bf16[10,512,512]{2,1,0:T(8,128)(2,1)} %w0.3), custom_call_target="tpu_custom_call" | custom-call | flops 1000000000 | bytes 3284992 | tf_op jit(solution)/shard_map/encode_own/pallas_call | solution.py:126
  20.4 9.2 %encode.1 = (f32[1024,512]{1,0:T(8,128)}, f32[1024,512]{1,0:T(8,128)}, bf16[1024,512]{1,0:T(8,128)(2,1)}, bf16[128,512]{1,0:T(8,128)(2,1)}, bf16[128,512]{1,0:T(...) custom-call(f32[1024,512]{1,0:T(8,128)} %encode_own.1.own, ...), custom_call_target="tpu_custom_call" | custom-call | flops 2000000000 | bytes 10628096 | tf_op jit(solution)/shard_map/encode/pallas_call | solution.py:126
  29.6 8.3 %all-to-all-start = ((bf16[128,16,128]{2,1,0:T(8,128)(2,1)}), bf16[128,16,128]{2,1,0:T(8,128)(2,1)}, u32[]{:S(2)}, u32[]{:S(2)}) async-start(bf16[128,16,128]{2,1,0:T(8,128)(2,1)} %bitcast.22), calls=%async_computation | async-start | bytes 1048576 | tf_op jit(solution)/shard_map/all_to_all | solution.py:442
  39.4 4.1 %collective-permute-start.5 = (bf16[64,512]{1,0:T(8,128)(2,1)}, bf16[64,512]{1,0:T(8,128)(2,1)}, u32[]{:S(2)}, u32[]{:S(2)}) collective-permute-start(bf16[64,512]{1,0:T(8,128)(2,1)} %get-tuple-element.63), channel_id=1, source_target_pairs={{0,15},{1,0},{2,1},{3,2},{4,3},{5,4},{6,5},{7,6},{8,7},{9,8},{10,9... | collective-permute-start | bytes 196616 | tf_op jit(solution)/shard_map/ppermute | solution.py:23
  45.3 5.6 %process_own.1 = (f32[1024,512]{1,0:T(8,128)}, f32[128,512]{1,0:T(8,128)}) custom-call(bf16[128,512]{1,0:T(8,128)(2,1)} %get-tuple-element.59.middle, bf16[128,512]{1,0:T(8,128)(2,1)} %get-tuple-element.60.sender, bf16[1024,512]{1,0:T(8,128)(2,1)} %edge.3, s32[8,128]{1,0:T(8,128)} %bitcast.34, s32[8,128]{1,0:T(8,128)} %bitcast.36, bf16[10,512,512]{2,1,0:T(8,128)(2,1)} %w0.3, ...), custom_call_target="tpu_custom_call" | custom-call | flops 1000000000 | bytes 5251072 | tf_op jit(solution)/shard_map/process_own/pallas_call | solution.py:126
  51.3 15.5 %process.1 = (bf16[128,512]{1,0:T(8,128)(2,1)}, bf16[1024,512]{1,0:T(8,128)(2,1)}, bf16[128,512]{1,0:T(8,128)(2,1)}, bf16[128,512]{1,0:T(8,128)(2,1)}, bf16[128,...) custom-call(f32[1024,512]{1,0:T(8,128)} %get-tuple-element.61.own, ...), custom_call_target="tpu_custom_call" | custom-call | flops 8000000000 | bytes 11018240 | tf_op jit(solution)/shard_map/process/pallas_call | solution.py:126
  66.7 6.4 %all-to-all-start.1 = ((bf16[128,16,128]{2,1,0:T(8,128)(2,1)}), bf16[128,16,128]{2,1,0:T(8,128)(2,1)}, u32[]{:S(2)}, u32[]{:S(2)}) async-start(bf16[128,16,128]{2,1,0:T(8,128)(2,1)} %bitcast.23), calls=%async_computation.1 | async-start | bytes 1048576 | tf_op jit(solution)/shard_map/all_to_all | solution.py:463
  73.1 8.4 %process_grads.1 = (bf16[1024,512]{1,0:T(8,128)(2,1)}, f32[128,512]{1,0:T(8,128)}, bf16[4,2,8,2,6,16,128]{6,5,4,3,2,1,0:T(8,128)(2,1)}) custom-call(bf16[1024,512]{1,0:T(8,128)(2,1)} %edge.3, bf16[1024,512]{1,0:T(8,128)(2,1)} %get-tuple-element.75.cround, bf16[1024,512]{1,0:T(8,128)(2,1)} %get-tuple-element.76.hidden, ...), custom_call_target="tpu_custom_call" | custom-call | flops 3000000000 | bytes 12189696 | tf_op jit(solution)/shard_map/process_grads/pallas_call | solution.py:126
  81.5 5.2 %all-to-all-done.1 = bf16[128,16,128]{2,1,0:T(8,128)(2,1)} async-done(((bf16[128,16,128]{2,1,0:T(8,128)(2,1)}), bf16[128,16,128]{2,1,0:T(8,128)(2,1)}, u32[]{:S(2)}, u32[]{:S(2)}) %all-to-all-start.1) | async-done | bytes 524320 | tf_op jit(solution)/shard_map/all_to_all | solution.py:463
  86.7 5.4 %all-to-all-start.2 = ((bf16[128,96,128]{2,1,0:T(8,128)(2,1)}), bf16[128,96,128]{2,1,0:T(8,128)(2,1)}, u32[]{:S(2)}, u32[]{:S(2)}) async-start(bf16[128,96,128]{2,1,0:T(8,128)(2,1)} %bitcast.19), calls=%async_computation.2 | async-start | bytes 6291456 | tf_op jit(solution)/shard_map/early/all_to_all | solution.py:392
  92.1 5.8 %collective-permute-start.8 = (bf16[64,512]{1,0:T(8,128)(2,1)S(1)}, bf16[64,512]{1,0:T(8,128)(2,1)}, u32[]{:S(2)}, u32[]{:S(2)}) collective-permute-start(bf16[64,512]{1,0:T(8,128)(2,1)S(1)} %copy-done.6), channel_id=1, source_target_pairs={{0,15},{1,0},{2,1},{3,2},{4,3},{5,4},{6,5},{7,6},{8,7},{9,8},{10,9... | collective-permute-start | bytes 196616 | tf_op jit(solution)/shard_map/ppermute | solution.py:23
  99.7 20.8 %collective-permute-done.8.in0 = bf16[64,512]{1,0:T(8,128)(2,1)} collective-permute-done((bf16[64,512]{1,0:T(8,128)(2,1)S(1)}, bf16[64,512]{1,0:T(8,128)(2,1)}, u32[]{:S(2)}, u32[]{:S(2)}) %collective-permute-start.8) | collective-permute-done | bytes 65568 | tf_op jit(solution)/shard_map/ppermute | solution.py:23
  120.5 11.8 %collective-permute-done.9.in1 = bf16[64,512]{1,0:T(8,128)(2,1)} collective-permute-done((bf16[64,512]{1,0:T(8,128)(2,1)S(1)}, bf16[64,512]{1,0:T(8,128)(2,1)}, u32[]{:S(2)}, u32[]{:S(2)}) %collective-permute-start.9) | collective-permute-done | bytes 65568 | tf_op jit(solution)/shard_map/ppermute | solution.py:23
  132.3 10.0 %encode_back.1 = (bf16[128,512]{1,0:T(8,128)(2,1)}, f32[128,512]{1,0:T(8,128)}, bf16[1024,512]{1,0:T(8,128)(2,1)}, bf16[1024,512]{1,0:T(8,128)(2,1)}, bf16[1024,...) custom-call(bf16[64,512]{1,0:T(8,128)(2,1)} %collective-permute-done, ...), custom_call_target="tpu_custom_call" | custom-call | flops 4000000000 | bytes 11152384 | tf_op jit(solution)/shard_map/encode_back/pallas_call | solution.py:126
  147.2 6.2 %encode_grads.1 = (f32[512,512]{1,0:T(8,128)}, bf16[128,512]{1,0:T(8,128)(2,1)}, bf16[3,512,512]{2,1,0:T(8,128)(2,1)}) custom-call(bf16[1024,512]{1,0:T(8,128)(2,1)} %get-tuple-element.86.upper, bf16[1024,512]{1,0:T(8,128)(2,1)} %get-tuple-element.87.lower, s32[8,128]{1,0:T(8,128)} %bitcast.27, s32[8,128]{1,0:T(8,128)} %bitcast.31, ...), custom_call_target="tpu_custom_call" | custom-call | flops 2000000000 | bytes 8134656 | tf_op jit(solution)/shard_map/encode_grads/pallas_call | solution.py:126
  153.4 5.5 %grid_back.1 = (bf16[512,512]{1,0:T(8,128)(2,1)}, bf16[4,2,8,2,4,16,128]{6,5,4,3,2,1,0:T(8,128)(2,1)}) custom-call(f32[512,512]{1,0:T(8,128)} %get-tuple-element.92.grid_own, bf16[256,512]{1,0:T(8,128)(2,1)} %collective-permute-done.12.in0, bf16[256,512]{1,0:T(8,128)(2,1)} %collective-permute-done.13.in1, bf16[256,512]{1,0:T(8,128)(2,1)} %collective-permute-done.14.in2, ...), custom_call_target="tpu_custom_call" | custom-call | flops 1000000000 | bytes 7344128 | tf_op jit(solution)/shard_map/grid_back/pallas_call | solution.py:126
  159.0 8.9 %all-to-all-start.4 = ((bf16[128,64,128]{2,1,0:T(8,128)(2,1)}), bf16[128,64,128]{2,1,0:T(8,128)(2,1)}, u32[]{:S(2)}, u32[]{:S(2)}) async-start(bf16[128,64,128]{2,1,0:T(8,128)(2,1)} %bitcast.20), calls=%async_computation.4 | async-start | bytes 4194304 | tf_op jit(solution)/shard_map/late/all_to_all | solution.py:392
  171.4 25.5 %all-to-all-done.4.terms = bf16[128,64,128]{2,1,0:T(8,128)(2,1)} async-done(((bf16[128,64,128]{2,1,0:T(8,128)(2,1)}), bf16[128,64,128]{2,1,0:T(8,128)(2,1)}, u32[]{:S(2)}, u32[]{:S(2)}) %all-to-all-start.4) | async-done | bytes 2097184 | tf_op jit(solution)/shard_map/late/all_to_all | solution.py:392
  196.9 5.9 %all-to-all-start.3 = ((bf16[64,96,128]{2,1,0:T(8,128)(2,1)}), bf16[64,96,128]{2,1,0:T(8,128)(2,1)}, u32[]{:S(2)}, u32[]{:S(2)}) async-start(bf16[64,96,128]{2,1,0:T(8,128)(2,1)} %early_sum.1), calls=%async_computation.3 | async-start | bytes 3145728 | tf_op jit(solution)/shard_map/early_spread/all_to_all | solution.py:397
  205.8 18.2 %all-to-all-done.3 = bf16[64,96,128]{2,1,0:T(8,128)(2,1)} async-done(((bf16[64,96,128]{2,1,0:T(8,128)(2,1)}), bf16[64,96,128]{2,1,0:T(8,128)(2,1)}, u32[]{:S(2)}, u32[]{:S(2)}) %all-to-all-start.3) | async-done | bytes 1572896 | tf_op jit(solution)/shard_map/early_spread/all_to_all | solution.py:397
  224.0 6.7 %all-to-all-start.5 = ((bf16[64,64,128]{2,1,0:T(8,128)(2,1)}), bf16[64,64,128]{2,1,0:T(8,128)(2,1)S(1)}, u32[]{:S(2)}, u32[]{:S(2)}) async-start(bf16[64,64,128]{2,1,0:T(8,128)(2,1)} %late_sum.1), calls=%async_computation.5 | async-start | bytes 2097152 | tf_op jit(solution)/shard_map/late_spread/all_to_all | solution.py:397
  232.5 14.5 %all-to-all-done.5 = bf16[64,64,128]{2,1,0:T(8,128)(2,1)S(1)} async-done(((bf16[64,64,128]{2,1,0:T(8,128)(2,1)}), bf16[64,64,128]{2,1,0:T(8,128)(2,1)S(1)}, u32[]{:S(2)}, u32[]{:S(2)}) %all-to-all-start.5) | async-done | bytes 1048608 | tf_op jit(solution)/shard_map/late_spread/all_to_all | solution.py:397
  254.5 5.7 %assemble.1 = bf16[10,512,512]{2,1,0:T(8,128)(2,1)} custom-call(s32[1]{0:T(128)} %bitcast.11.core, bf16[32,2,6,16,128]{4,3,2,1,0:T(8,128)(2,1)} %bitcast.13.refs_0_, bf16[32,2,6,16,128]{4,3,2,1,0:T(8,128)(2,1)} %bitcast.14.refs_1_, bf16[32,2,4,16,128]{4,3,2,1,0:T(8,128)(2,1)} %bitcast.18, bf16[32,2,4,16,128]{4,3,2,1,0:T(8,128)(2,1)} %bitcast.21), custom_call_target="tpu_custom_call" | custom-call | tf_op jit(solution)/shard_map/assemble/pallas_call | solution.py:494
  (52 shorter events, 36.5 us)
Async XLA Ops:
  5.2 14.6 %collective-permute-start = (bf16[256,512]{1,0:T(8,128)(2,1)}, bf16[256,512]{1,0:T(8,128)(2,1)}, u32[]{:S(2)}, u32[]{:S(2)}) collective-permute-start(bf16[256,512]{1,0:T(8,128)(2,1)} %get-tuple-element.55), channel_id=1, source_target_pairs={{0,1},{1,2},{2,3},{3,4},{4,5},{5,6},{6,7},{7,8},{8,9},{9,10},{10,1... | collective-permute-start | bytes 786440 | tf_op jit(solution)/shard_map/ppermute | solution.py:23
  7.6 12.1 %collective-permute-start.1 = (bf16[256,512]{1,0:T(8,128)(2,1)}, bf16[256,512]{1,0:T(8,128)(2,1)}, u32[]{:S(2)}, u32[]{:S(2)}) collective-permute-start(bf16[256,512]{1,0:T(8,128)(2,1)} %get-tuple-element.56), channel_id=1, source_target_pairs={{0,15},{1,0},{2,1},{3,2},{4,3},{5,4},{6,5},{7,6},{8,7},{9,8},{10,9... | collective-permute-start | bytes 786440 | tf_op jit(solution)/shard_map/ppermute | solution.py:23
  12.2 7.5 %collective-permute-start.2 = (bf16[256,512]{1,0:T(8,128)(2,1)}, bf16[256,512]{1,0:T(8,128)(2,1)}, u32[]{:S(2)}, u32[]{:S(2)}) collective-permute-start(bf16[256,512]{1,0:T(8,128)(2,1)} %get-tuple-element.57), channel_id=1, source_target_pairs={{0,16},{16,32},{32,48},{48,64},{64,80},{80,96},{96,112},{112,0},{1... | collective-permute-start | bytes 786440 | tf_op jit(solution)/shard_map/ppermute | solution.py:23
  14.3 6.1 %collective-permute-start.3 = (bf16[256,512]{1,0:T(8,128)(2,1)}, bf16[256,512]{1,0:T(8,128)(2,1)}, u32[]{:S(2)}, u32[]{:S(2)}) collective-permute-start(bf16[256,512]{1,0:T(8,128)(2,1)} %get-tuple-element.58), channel_id=1, source_target_pairs={{0,112},{16,0},{32,16},{48,32},{64,48},{80,64},{96,80},{112,96},{1... | collective-permute-start | bytes 786440 | tf_op jit(solution)/shard_map/ppermute | solution.py:23
  29.6 21.7 %all-to-all-start = ((bf16[128,16,128]{2,1,0:T(8,128)(2,1)}), bf16[128,16,128]{2,1,0:T(8,128)(2,1)}, u32[]{:S(2)}, u32[]{:S(2)}) async-start(bf16[128,16,128]{2,1,0:T(8,128)(2,1)} %bitcast.22), calls=%async_computation | async-start | bytes 1048576 | tf_op jit(solution)/shard_map/all_to_all | solution.py:442
  37.9 13.1 %collective-permute-start.4 = (bf16[64,512]{1,0:T(8,128)(2,1)}, bf16[64,512]{1,0:T(8,128)(2,1)}, u32[]{:S(2)}, u32[]{:S(2)}) collective-permute-start(bf16[64,512]{1,0:T(8,128)(2,1)} %get-tuple-element.62), channel_id=1, source_target_pairs={{0,1},{1,2},{2,3},{3,4},{4,5},{5,6},{6,7},{7,8},{8,9},{9,10},{10,1... | collective-permute-start | bytes 196616 | tf_op jit(solution)/shard_map/ppermute | solution.py:23
  39.4 11.5 %collective-permute-start.5 = (bf16[64,512]{1,0:T(8,128)(2,1)}, bf16[64,512]{1,0:T(8,128)(2,1)}, u32[]{:S(2)}, u32[]{:S(2)}) collective-permute-start(bf16[64,512]{1,0:T(8,128)(2,1)} %get-tuple-element.63), channel_id=1, source_target_pairs={{0,15},{1,0},{2,1},{3,2},{4,3},{5,4},{6,5},{7,6},{8,7},{9,8},{10,9... | collective-permute-start | bytes 196616 | tf_op jit(solution)/shard_map/ppermute | solution.py:23
  43.6 7.4 %collective-permute-start.6 = (bf16[64,512]{1,0:T(8,128)(2,1)}, bf16[64,512]{1,0:T(8,128)(2,1)}, u32[]{:S(2)}, u32[]{:S(2)}) collective-permute-start(bf16[64,512]{1,0:T(8,128)(2,1)} %get-tuple-element.64), channel_id=1, source_target_pairs={{0,16},{16,32},{32,48},{48,64},{64,80},{80,96},{96,112},{112,0},{1... | collective-permute-start | bytes 196616 | tf_op jit(solution)/shard_map/ppermute | solution.py:23
  45.3 5.7 %collective-permute-start.7 = (bf16[64,512]{1,0:T(8,128)(2,1)}, bf16[64,512]{1,0:T(8,128)(2,1)}, u32[]{:S(2)}, u32[]{:S(2)}) collective-permute-start(bf16[64,512]{1,0:T(8,128)(2,1)} %get-tuple-element.65), channel_id=1, source_target_pairs={{0,112},{16,0},{32,16},{48,32},{64,48},{80,64},{96,80},{112,96},{1... | collective-permute-start | bytes 196616 | tf_op jit(solution)/shard_map/ppermute | solution.py:23
  66.7 19.9 %all-to-all-start.1 = ((bf16[128,16,128]{2,1,0:T(8,128)(2,1)}), bf16[128,16,128]{2,1,0:T(8,128)(2,1)}, u32[]{:S(2)}, u32[]{:S(2)}) async-start(bf16[128,16,128]{2,1,0:T(8,128)(2,1)} %bitcast.23), calls=%async_computation.1 | async-start | bytes 1048576 | tf_op jit(solution)/shard_map/all_to_all | solution.py:463
  86.7 72.3 %all-to-all-start.2 = ((bf16[128,96,128]{2,1,0:T(8,128)(2,1)}), bf16[128,96,128]{2,1,0:T(8,128)(2,1)}, u32[]{:S(2)}, u32[]{:S(2)}) async-start(bf16[128,96,128]{2,1,0:T(8,128)(2,1)} %bitcast.19), calls=%async_computation.2 | async-start | bytes 6291456 | tf_op jit(solution)/shard_map/early/all_to_all | solution.py:392
  92.1 28.4 %collective-permute-start.8 = (bf16[64,512]{1,0:T(8,128)(2,1)S(1)}, bf16[64,512]{1,0:T(8,128)(2,1)}, u32[]{:S(2)}, u32[]{:S(2)}) collective-permute-start(bf16[64,512]{1,0:T(8,128)(2,1)S(1)} %copy-done.6), channel_id=1, source_target_pairs={{0,15},{1,0},{2,1},{3,2},{4,3},{5,4},{6,5},{7,6},{8,7},{9,8},{10,9... | collective-permute-start | bytes 196616 | tf_op jit(solution)/shard_map/ppermute | solution.py:23
  97.9 34.4 %collective-permute-start.9 = (bf16[64,512]{1,0:T(8,128)(2,1)S(1)}, bf16[64,512]{1,0:T(8,128)(2,1)}, u32[]{:S(2)}, u32[]{:S(2)}) collective-permute-start(bf16[64,512]{1,0:T(8,128)(2,1)S(1)} %copy-done.5), channel_id=1, source_target_pairs={{0,1},{1,2},{2,3},{3,4},{4,5},{5,6},{6,7},{7,8},{8,9},{9,10},{10,1... | collective-permute-start | bytes 196616 | tf_op jit(solution)/shard_map/ppermute | solution.py:23
  97.9 34.4 %collective-permute-start.10 = (bf16[64,512]{1,0:T(8,128)(2,1)S(1)}, bf16[64,512]{1,0:T(8,128)(2,1)}, u32[]{:S(2)}, u32[]{:S(2)}) collective-permute-start(bf16[64,512]{1,0:T(8,128)(2,1)S(1)} %copy-done.4), channel_id=1, source_target_pairs={{0,112},{16,0},{32,16},{48,32},{64,48},{80,64},{96,80},{112,96},{1... | collective-permute-start | bytes 196616 | tf_op jit(solution)/shard_map/ppermute | solution.py:23
  98.6 33.7 %collective-permute-start.11 = (bf16[64,512]{1,0:T(8,128)(2,1)S(1)}, bf16[64,512]{1,0:T(8,128)(2,1)}, u32[]{:S(2)}, u32[]{:S(2)}) collective-permute-start(bf16[64,512]{1,0:T(8,128)(2,1)S(1)} %copy-done.3), channel_id=1, source_target_pairs={{0,16},{16,32},{32,48},{48,64},{64,80},{80,96},{96,112},{112,0},{1... | collective-permute-start | bytes 196616 | tf_op jit(solution)/shard_map/ppermute | solution.py:23
  142.3 11.1 %collective-permute-start.12 = (bf16[256,512]{1,0:T(8,128)(2,1)}, bf16[256,512]{1,0:T(8,128)(2,1)}, u32[]{:S(2)}, u32[]{:S(2)}) collective-permute-start(bf16[256,512]{1,0:T(8,128)(2,1)} %get-tuple-element.93), channel_id=1, source_target_pairs={{0,15},{1,0},{2,1},{3,2},{4,3},{5,4},{6,5},{7,6},{8,7},{9,8},{10,9... | collective-permute-start | bytes 786440 | tf_op jit(solution)/shard_map/ppermute | solution.py:23
  143.7 9.7 %collective-permute-start.13 = (bf16[256,512]{1,0:T(8,128)(2,1)}, bf16[256,512]{1,0:T(8,128)(2,1)}, u32[]{:S(2)}, u32[]{:S(2)}) collective-permute-start(bf16[256,512]{1,0:T(8,128)(2,1)} %get-tuple-element.94), channel_id=1, source_target_pairs={{0,1},{1,2},{2,3},{3,4},{4,5},{5,6},{6,7},{7,8},{8,9},{9,10},{10,1... | collective-permute-start | bytes 786440 | tf_op jit(solution)/shard_map/ppermute | solution.py:23
  143.8 9.7 %collective-permute-start.14 = (bf16[256,512]{1,0:T(8,128)(2,1)}, bf16[256,512]{1,0:T(8,128)(2,1)}, u32[]{:S(2)}, u32[]{:S(2)}) collective-permute-start(bf16[256,512]{1,0:T(8,128)(2,1)} %get-tuple-element.95), channel_id=1, source_target_pairs={{0,112},{16,0},{32,16},{48,32},{64,48},{80,64},{96,80},{112,96},{1... | collective-permute-start | bytes 786440 | tf_op jit(solution)/shard_map/ppermute | solution.py:23
  146.1 7.4 %collective-permute-start.15 = (bf16[256,512]{1,0:T(8,128)(2,1)}, bf16[256,512]{1,0:T(8,128)(2,1)}, u32[]{:S(2)}, u32[]{:S(2)}) collective-permute-start(bf16[256,512]{1,0:T(8,128)(2,1)} %get-tuple-element.96), channel_id=1, source_target_pairs={{0,16},{16,32},{32,48},{48,64},{64,80},{80,96},{96,112},{112,0},{1... | collective-permute-start | bytes 786440 | tf_op jit(solution)/shard_map/ppermute | solution.py:23
  159.0 37.9 %all-to-all-start.4 = ((bf16[128,64,128]{2,1,0:T(8,128)(2,1)}), bf16[128,64,128]{2,1,0:T(8,128)(2,1)}, u32[]{:S(2)}, u32[]{:S(2)}) async-start(bf16[128,64,128]{2,1,0:T(8,128)(2,1)} %bitcast.20), calls=%async_computation.4 | async-start | bytes 4194304 | tf_op jit(solution)/shard_map/late/all_to_all | solution.py:392
  196.9 27.1 %all-to-all-start.3 = ((bf16[64,96,128]{2,1,0:T(8,128)(2,1)}), bf16[64,96,128]{2,1,0:T(8,128)(2,1)}, u32[]{:S(2)}, u32[]{:S(2)}) async-start(bf16[64,96,128]{2,1,0:T(8,128)(2,1)} %early_sum.1), calls=%async_computation.3 | async-start | bytes 3145728 | tf_op jit(solution)/shard_map/early_spread/all_to_all | solution.py:397
  224.0 23.0 %all-to-all-start.5 = ((bf16[64,64,128]{2,1,0:T(8,128)(2,1)}), bf16[64,64,128]{2,1,0:T(8,128)(2,1)S(1)}, u32[]{:S(2)}, u32[]{:S(2)}) async-start(bf16[64,64,128]{2,1,0:T(8,128)(2,1)} %late_sum.1), calls=%async_computation.5 | async-start | bytes 2097152 | tf_op jit(solution)/shard_map/late_spread/all_to_all | solution.py:397
  230.8 23.8 %collective-permute-start.16 = (bf16[64,96,128]{2,1,0:T(8,128)(2,1)}, bf16[64,96,128]{2,1,0:T(8,128)(2,1)}, u32[]{:S(2)}, u32[]{:S(2)}) collective-permute-start(bf16[64,96,128]{2,1,0:T(8,128)(2,1)} %all-to-all-done.3), channel_id=1, source_target_pairs={{0,16},{16,0},{1,17},{17,1},{2,18},{18,2},{3,19},{19,3},{4,20},{20... | collective-permute-start | bytes 4718600 | tf_op jit(solution)/shard_map/early_pair/ppermute | solution.py:399
  248.0 5.5 %collective-permute-start.17 = (bf16[64,64,128]{2,1,0:T(8,128)(2,1)S(1)}, bf16[64,64,128]{2,1,0:T(8,128)(2,1)S(1)}, u32[]{:S(2)}, u32[]{:S(2)}) collective-permute-start(bf16[64,64,128]{2,1,0:T(8,128)(2,1)S(1)} %all-to-all-done.5), channel_id=1, source_target_pairs={{0,16},{16,0},{1,17},{17,1},{2,18},{18,2},{3,19},{19,3},{4,20},{20... | collective-permute-start | bytes 3145736 | tf_op jit(solution)/shard_map/late_pair/ppermute | solution.py:399
  (7 other events, 54.1 us)

commit v2 on v0

v2 whole, which is shorter than its diff:
```python
import functools

import jax
import jax.numpy as jnp
from jax import lax
from jax.experimental import pallas as pl
from jax.experimental.pallas import tpu as pltpu
from jax.sharding import PartitionSpec as P


norm_eps = 1e-05
f32 = jnp.float32
bf16 = jnp.bfloat16
AXES = ("x", "core", "y", "z")
CHIPS = ("x", "y", "z")
FACE = ("x", "core")
SUB = ("y", "z")
CHUNK = 256


def shifted(value, axis, steps):
    count = lax.axis_size(axis)
    pairs = [(source, (source + steps) % count) for source in range(count)]
    return lax.ppermute(value, axis, pairs)


def outgoing_rows(blocks):
    routes = ((SUB, 1), (SUB, -1), (FACE, 1), (FACE, -1))
    return [shifted(block, axis, step) for block, (axis, step) in zip(blocks, routes)]


def returned_rows(blocks):
    routes = ((SUB, -1), (SUB, 1), (FACE, -1), (FACE, 1))
    return [shifted(block, axis, step) for block, (axis, step) in zip(blocks, routes)]


def dot(a, b):
    return jnp.dot(a, b, preferred_element_type=f32)


def dot_nt(a, b):
    return lax.dot_general(a, b, (((1,), (1,)), ((), ())), preferred_element_type=f32)


def dot_tn(a, b):
    return lax.dot_general(a, b, (((0,), (0,)), ((), ())), preferred_element_type=f32)


def halves(values):
    upper = values.astype(bf16)
    return upper, (values - upper.astype(f32)).astype(bf16)


def mean(values):
    return jnp.sum(values, axis=-1, keepdims=True) * (1.0 / values.shape[-1])


def norm_parts(values):
    centre = values - mean(values)
    inverse = lax.rsqrt(mean(centre * centre) + norm_eps)
    return centre * inverse, inverse


def norm_back(normed, inverse, upstream):
    return inverse * (upstream - mean(upstream) - normed * mean(upstream * normed))


def sigmoid(values):
    return 1.0 / (1.0 + jnp.exp(-values))


def silu(values):
    return values * sigmoid(values)


def slope(values):
    s = sigmoid(values)
    return s * (1.0 + values * (1.0 - s))


def pick_rows(row, offset, count):
    column = jnp.transpose(jnp.broadcast_to(row, (128, 128))) - offset
    lane = lax.broadcasted_iota(jnp.int32, (128, 128), 1)
    return jnp.concatenate(
        [jnp.where(column == lane + 128 * b, 1.0, 0.0).astype(bf16) for b in range(count // 128)],
        axis=1,
    )


def pick(ref, first, rows, offset, count):
    return jnp.concatenate(
        [pick_rows(ref[pl.ds(first + r, 1), :], offset, count) for r in range(rows)], axis=0
    )


def put(ref, first, rows, offset, count):
    return put_rows([ref[pl.ds(first + r, 1), :] for r in range(rows)], offset, count)


def table_rows(table, k):
    return [table[0, k : k + 1, 128 * h : 128 * h + 128] for h in range(2)]


def put_rows(rows, offset, count):
    place = lax.broadcasted_iota(jnp.int32, (count, 128), 0) + offset
    return jnp.concatenate(
        [jnp.where(place == jnp.broadcast_to(row, (count, 128)), 1.0, 0.0).astype(bf16) for row in rows], axis=1
    )


def stack_halves(values):
    return jnp.concatenate(halves(values), axis=0)


def twice(values):
    return jnp.concatenate([values, values], axis=1)


def chunks(count, body):
    def step(i, carry):
        body(i, pl.ds(pl.multiple_of(i * CHUNK, CHUNK), CHUNK))
        return carry

    lax.fori_loop(0, count, step, 0)


def call(body, outs, args, weights=None, picks=(), scratch=(), flops=10**9, vmem=67000000):
    def whole(shape):
        return pl.BlockSpec(shape, lambda i: (0,) * len(shape))

    in_specs = [pl.BlockSpec(memory_space=pltpu.SMEM) if a.shape == (1,) else whole(a.shape) for a in args]
    for k in picks:
        in_specs.append(
            pl.BlockSpec((None, weights.shape[1], weights.shape[2]), functools.partial(lambda k, i: (k, 0, 0), k))
        )
    shapes = [jax.ShapeDtypeStruct(s, d) for s, d in outs]
    total = sum(a.size * a.dtype.itemsize for a in args) + sum(s.size * s.dtype.itemsize for s in shapes)
    total += len(picks) * 512 * 1024
    return pl.pallas_call(
        body,
        grid=(1,),
        out_shape=shapes,
        in_specs=in_specs,
        out_specs=[whole(s.shape) for s in shapes],
        scratch_shapes=list(scratch),
        compiler_params=pltpu.CompilerParams(vmem_limit_bytes=vmem),
        cost_estimate=pl.CostEstimate(flops=flops, bytes_accessed=total, transcendentals=0),
    )(*args, *([weights] * len(picks)))


def project_body(grid, table, w0, project, out0, out1, out2, out3):
    chunks(2, lambda i, s: project.__setitem__((s, slice(None)), dot(grid[s, :], w0[...]).astype(bf16)))
    for k, out in enumerate((out0, out1, out2, out3)):
        picked = jnp.concatenate([pick_rows(row, 0, 512) for row in table_rows(table, k)], axis=0)
        out[...] = dot(picked, project[...]).astype(bf16)


def encode_own_body(project, slot, target, mesh, w1, own, source):
    source[0:512, :] = project[...]
    source[512:768, :] = stack_halves(dot(mesh[...], w1[...]))

    def step(i, s):
        receiver = pick(target, 2 * i, 2, 0, 128)
        own[s, :] = dot(jnp.concatenate([pick(slot, 2 * i, 2, 0, 512), twice(receiver)], axis=1), source[...])

    chunks(4, step)


def far_slots(slot):
    far = slot - 384
    return jnp.where(slot < 384, slot, 384 + (far & 3) * 128 + (far >> 2))


def encode_body(
    own, in0, in1, in2, in3, slot, target, mesh, halo, far, w2, w4,
    pre_out, linear_out, hidden_out, middle_out, sender_out, h0, h1, h2, h3, far_out,
    total, wide,
):
    total[...] = jnp.zeros_like(total)

    def step(i, s):
        pre = own[s, :]
        for k, block in enumerate((in0, in1, in2, in3)):
            pre = pre + dot(pick(slot, 2 * i, 2, 512 + 256 * k, 256), block[...])
        pre_out[s, :] = pre
        hidden = silu(pre).astype(bf16)
        hidden_out[s, :] = hidden
        linear = dot(hidden, w2[...])
        linear_out[s, :] = linear
        message = norm_parts(linear)[0].astype(bf16)
        total[...] += dot(put(target, 2 * i, 2, 0, 128), message)

    chunks(4, step)
    middle = (mesh[...].astype(f32) + total[...]).astype(bf16)
    middle_out[...] = middle
    sender = dot(middle, w4[...]).astype(bf16)
    sender_out[...] = sender
    rows = dot(pick(halo, 0, 2, 0, 128), sender).astype(bf16)
    for k, out in enumerate((h0, h1, h2, h3)):
        out[...] = rows[64 * k : 64 * k + 64, :]
    for r in range(4):
        picked = dot(pick(far, r, 1, 0, 128), sender)
        for c in range(4):
            wide[pl.ds(4 * c + r, 128, stride=16), :] = picked[:, 128 * c : 128 * c + 128]
    far_out[...] = wide[...].astype(bf16)


def process_own_body(middle, sender, edge, slot, target, w3, w5, w7, own, update_own, source):
    source[0:128, :] = sender[...]
    source[128:384, :] = stack_halves(dot(middle[...], w5[...]))
    update_own[...] = dot(middle[...], w7[...])

    def step(i, s):
        receiver = pick(target, 2 * i, 2, 0, 128)
        picked = jnp.concatenate([pick(slot, 2 * i, 2, 0, 128), twice(receiver)], axis=1)
        own[s, :] = dot(edge[s, :], w3[...]) + dot(picked, source[...])

    chunks(4, step)


def gather_far(wide, source, first):
    for r in range(4):
        for c in range(4):
            source[first + 128 * r : first + 128 * r + 128, 128 * c : 128 * c + 128] = wide[
                pl.ds(4 * c + r, 128, stride=16), :
            ].astype(bf16)


def process_body(
    own, in0, in1, in2, in3, far_in, slot, target, middle, update_own, mesh_cot, edge_cot, w6, w8, w9,
    mesh_update, hidden_out, round_out, uhidden_out, cot_linear_out, cot_update_out, plinear_out, cround_out,
    receive_out, sender_own, h0, h1, h2, h3, far_out,
    source, pre_s, normed_s, inverse_s, total, wide, slots,
):
    slots[...] = far_slots(slot[...])
    for k, block in enumerate((in0, in1, in2, in3)):
        source[64 * k : 64 * k + 64, :] = block[...]
    wide[...] = far_in[...].astype(f32)
    gather_far(wide, source, 256)
    total[...] = jnp.zeros_like(total)

    def forward(i, s):
        pre = own[s, :] + dot(pick(slots, 2 * i, 2, 128, 768), source[...])
        pre_s[s, :] = pre
        hidden = silu(pre).astype(bf16)
        hidden_out[s, :] = hidden
        normed, inverse = norm_parts(dot(hidden, w6[...]))
        normed_s[s, :] = normed
        inverse_s[s, :] = jnp.broadcast_to(inverse, (CHUNK, 128))
        total[...] += dot(put(target, 2 * i, 2, 0, 128), normed.astype(bf16))

    chunks(4, forward)
    rounded = total[...].astype(bf16)
    round_out[...] = rounded
    pre = update_own[...] + dot(rounded, w8[...])
    uhidden = silu(pre).astype(bf16)
    uhidden_out[...] = uhidden
    normed, inverse = norm_parts(dot(uhidden, w9[...]))
    mesh_update[...] = (middle[...].astype(f32) + normed).astype(bf16)
    cot_linear = norm_back(normed, inverse, mesh_cot[...].astype(f32)).astype(bf16)
    cot_linear_out[...] = cot_linear
    cot_update = (dot_nt(cot_linear, w9[...]) * slope(pre)).astype(bf16)
    cot_update_out[...] = cot_update
    cot_total = stack_halves(dot_nt(cot_update, w8[...]))

    def backward(i, s):
        receiver = pick(target, 2 * i, 2, 0, 128)
        upstream = dot(twice(receiver), cot_total) + edge_cot[s, :].astype(f32)
        cot = norm_back(normed_s[s, :], inverse_s[s, 0:1], upstream).astype(bf16)
        plinear_out[s, :] = cot
        cround_out[s, :] = (dot_nt(cot, w6[...]) * slope(pre_s[s, :])).astype(bf16)

    chunks(4, backward)
    kept = jnp.concatenate([put(target, 0, 8, 0, 128), put(slots, 0, 8, 0, 128)], axis=0)
    kept = dot(kept, cround_out[...])
    receive_out[...] = kept[0:128, :].astype(bf16)
    sender_own[...] = kept[128:256, :]
    spread = put(slots, 0, 8, 128, 256)
    spread = dot(spread, cround_out[...]).astype(bf16)
    for k, out in enumerate((h0, h1, h2, h3)):
        out[...] = spread[64 * k : 64 * k + 64, :]
    for half in range(2):
        spread = put(slots, 0, 8, 384 + 256 * half, 256)
        spread = dot(spread, cround_out[...])
        for q in range(2):
            for c in range(4):
                wide[pl.ds(4 * c + 2 * half + q, 128, stride=16), :] = spread[
                    128 * q : 128 * q + 128, 128 * c : 128 * c + 128
                ]
    far_out[...] = wide[...].astype(bf16)


def store_blocks(own, other, k, term, held, core):
    held[...] = term.astype(bf16)
    for q in range(2):
        for out, c in ((own, core[0]), (other, 1 - core[0])):
            columns = pl.ds(pl.multiple_of(256 * c + 128 * q, 128), 128)
            out[:, q, k, :, :] = held[:, columns].reshape(32, 16, 128)


def process_grads_body(
    scales, core, edge, cround, hidden, plinear, middle, receive, cot_update, rounded, uhidden, cot_linear, edge_cot, mesh_cot,
    w3, w5, w7, edge_grad, middle_part, grads_own, grads_other, held,
):
    pairs = ((edge, cround), (middle, receive), (hidden, plinear), (middle, cot_update), (rounded, cot_update), (uhidden, cot_linear))
    for k, (x, y) in enumerate(pairs):
        store_blocks(grads_own, grads_other, k, dot_tn(x[...], y[...]) * scales[k], held, core)
    middle_part[...] = mesh_cot[...].astype(f32) + dot_nt(cot_update[...], w7[...]) + dot_nt(receive[...], w5[...])

    def step(i, s):
        edge_grad[s, :] = (edge_cot[s, :].astype(f32) + dot_nt(cround[s, :], w3[...])).astype(bf16)

    chunks(4, step)


def encode_back_body(
    in0, in1, in2, in3, far_in, halo, far, sender_own, middle_part, pre, linear, slot, target, w2, w4,
    cot_sender_out, cot_middle_out, elinear_out, upper_out, g0, g1, g2, g3,
    source, wide,
):
    for k, block in enumerate((in0, in1, in2, in3)):
        source[64 * k : 64 * k + 64, :] = block[...]
    wide[...] = far_in[...].astype(f32)
    gather_far(wide, source, 256)
    owners = jnp.concatenate([put(halo, 0, 2, 0, 128), put(far, 0, 4, 0, 128)], axis=1)
    cot_sender = (sender_own[...] + dot(owners, source[...])).astype(bf16)
    cot_sender_out[...] = cot_sender
    cot_middle = middle_part[...] + dot_nt(cot_sender, w4[...])
    cot_middle_out[...] = cot_middle
    cot_middle = stack_halves(cot_middle)

    def step(i, s):
        receiver = pick(target, 2 * i, 2, 0, 128)
        normed, inverse = norm_parts(linear[s, :])
        cot = norm_back(normed, inverse, dot(twice(receiver), cot_middle)).astype(bf16)
        elinear_out[s, :] = cot
        upper_out[s, :] = (dot_nt(cot, w2[...]) * slope(pre[s, :])).astype(bf16)

    chunks(4, step)
    for k, out in enumerate((g0, g1, g2, g3)):
        spread = put(slot, 0, 8, 512 + 256 * k, 256)
        out[...] = dot(spread, upper_out[...]).astype(bf16)


def encode_grads_body(
    scales, core, upper, slot, target, cot_middle, mesh, middle, cot_sender, hidden, elinear, w1,
    grid_own, mesh_grad, grads_own, grads_other, held,
):
    def store(k, x, y, scale):
        store_blocks(grads_own, grads_other, k, dot_tn(x, y) * scale, held, core)

    store(1, hidden[...], elinear[...], scales[1])
    store(2, middle[...], cot_sender[...], scales[2])
    receive = dot(put(target, 0, 8, 0, 128), upper[...]).astype(bf16)
    store(0, mesh[...], receive, scales[0])
    mesh_grad[...] = (cot_middle[...] + dot_nt(receive, w1[...])).astype(bf16)
    for k in range(2):
        grid_own[256 * k : 256 * k + 256, :] = dot(put(slot, 0, 8, 256 * k, 256), upper[...])


def grid_back_body(scales, core, grid_own, in0, in1, in2, in3, table, grid, w0, grid_grad, grads_own, grads_other, cot, held):
    for i in range(2):
        s = slice(CHUNK * i, CHUNK * i + CHUNK)
        total = grid_own[s, :]
        for k, block in enumerate((in0, in1, in2, in3)):
            total = total + dot(put_rows(table_rows(table, k), i * CHUNK, CHUNK), block[...])
        total = total.astype(bf16)
        cot[s, :] = total
        grid_grad[s, :] = dot_nt(total, w0[...]).astype(bf16)
    store_blocks(grads_own, grads_other, 0, dot_tn(grid[...], cot[...]) * scales[0], held, core)


def pair_body(*refs):
    out = refs[-1]
    place = 0
    for own, got in zip(refs[0:-1:2], refs[1:-1:2]):
        for k in range(own.shape[2]):
            out[:, :, place] = (own[:, :, k].astype(f32) + got[:, :, k].astype(f32)).astype(bf16)
            place += 1


def sum_body(terms, *shard):
    total = terms[0].astype(f32)
    for d in range(1, terms.shape[0]):
        total = total + terms[d].astype(f32)
    total = total.astype(bf16)
    if len(shard[0].shape) == 2:
        shard[0][...] = total
    else:
        for p in range(shard[0].shape[0]):
            shard[0][p] = total


def place_early_body(order, blocks, out):
    for place, k in enumerate(order):
        for c in range(2):
            for q in range(2):
                first = 256 * c + 128 * q
                out[k, :, first : first + 128] = blocks[:, c, :, q, place].reshape(512, 128)


def place_late_body(core, own, other, kept, out):
    del kept
    first = core[0] == 0
    for q in range(2):
        a, b = own[:, q].reshape(512, 128), other[:, q].reshape(512, 128)
        out[:, 128 * q : 128 * q + 128] = jnp.where(first, a, b)
        out[:, 256 + 128 * q : 384 + 128 * q] = jnp.where(first, b, a)


def swapped(value):
    return lax.ppermute(value, "core", [(0, 1), (1, 0)])


def scaled(body, scales):
    return functools.partial(body, scales)


def on_device(
    grid_latent, mesh_latent, edge_latent, mesh_cotangent, edge_cotangent, grid_send, grid_slot, grid_target,
    mesh_halo, mesh_send, mesh_slot, mesh_target, weights,
):
    peers = lax.axis_size(AXES)
    mesh_rows, latent = mesh_latent.shape
    edges = grid_slot.shape[0]
    grid_scale = 1.0 / (edges * peers) ** 0.5
    edge_scale = 1.0 / (mesh_slot.shape[0] * peers) ** 0.5
    node_scale = 1.0 / (mesh_rows * peers) ** 0.5
    grid_table = grid_send
    core = lax.axis_index("core").reshape(1)
    halo_table = mesh_halo.reshape(2, 128)
    far_table = mesh_send[0].T
    gslot, gtarget = grid_slot.reshape(8, 128), grid_target.reshape(8, 128)
    mslot, mtarget = mesh_slot.reshape(8, 128), mesh_target.reshape(8, 128)
    big, small, halo = (edges, latent), (mesh_rows, latent), (64, latent)
    vm = pltpu.VMEM

    project, *outgoing = call(
        project_body, [((512, latent), bf16)] + [((256, latent), bf16)] * 4,
        (grid_latent, grid_table), weights, (0,),
    )
    arrived = outgoing_rows(outgoing)
    (own,) = call(
        encode_own_body, [(big, f32)], (project, gslot, gtarget, mesh_latent),
        weights, (1,), scratch=(vm((768, latent), bf16),), flops=10**9,
    )
    pre, linear, hidden, middle, sender, *halos, far_out = call(
        encode_body,
        [(big, f32), (big, f32), (big, bf16), (small, bf16), (small, bf16)] + [(halo, bf16)] * 4 + [((2048, 128), bf16)],
        (own, *arrived, gslot, gtarget, mesh_latent, halo_table, far_table), weights, (2, 4),
        scratch=(vm(small, f32), vm((2048, 128), f32)), flops=2 * 10**9,
    )
    far_in = lax.all_to_all(far_out.reshape(peers, 16, 128), AXES, 0, 0, tiled=True).reshape(2048, 128)
    halo_in = outgoing_rows(halos)
    own, update_own = call(
        process_own_body, [(big, f32), (small, f32)], (middle, sender, edge_latent, mslot, mtarget),
        weights, (3, 5, 7), scratch=(vm((384, latent), bf16),), flops=2 * 10**9,
    )
    (
        mesh_update, phidden, rounded, uhidden, cot_linear, cot_update, plinear, cround, receive, sender_own,
        *halos, far_out,
    ) = call(
        process_body,
        [(small, bf16), (big, bf16)] + [(small, bf16)] * 4 + [(big, bf16)] * 2
        + [(small, bf16), (small, f32)] + [(halo, bf16)] * 4 + [((2048, 128), bf16)],
        (own, *halo_in, far_in, mslot, mtarget, middle, update_own, mesh_cotangent, edge_cotangent),
        weights, (6, 8, 9),
        scratch=(
            vm((768, latent), bf16), vm(big, f32), vm(big, f32), vm((edges, 128), f32),
            vm(small, f32), vm((2048, 128), f32), vm((8, 128), jnp.int32),
        ),
        flops=8 * 10**9,
    )
    far_back = lax.all_to_all(far_out.reshape(peers, 16, 128), AXES, 0, 0, tiled=True).reshape(2048, 128)
    halo_back = returned_rows(halos)

    def blocks(count):
        return ((32, 2, count, 16, 128), bf16)

    held = vm((latent, latent), bf16)
    edge_grad, middle_part, early_own, early_other = call(
        scaled(process_grads_body, [edge_scale] * 3 + [node_scale] * 3),
        [(big, bf16), (small, f32), blocks(6), blocks(6)],
        (core, edge_latent, cround, phidden, plinear, middle, receive, cot_update, rounded, uhidden, cot_linear,
         edge_cotangent, mesh_cotangent),
        weights, (3, 5, 7), scratch=(held,), flops=3 * 10**9,
    )
    (early,) = call(pair_body, [blocks(6)], (early_own, swapped(early_other)), flops=10**6)
    early, _ = lax.optimization_barrier((early, (halo_back, far_back)))
    early = lax.all_to_all(early.reshape(64, 96, 128), CHIPS, 0, 0, tiled=True)
    (early,) = call(sum_body, [((96, 128), bf16)], (early,), flops=10**7)
    early = lax.all_gather(early, AXES, axis=0, tiled=True).reshape(4, 2, 8, 2, 6, 16, 128)
    (placed,) = call(
        functools.partial(place_early_body, (3, 5, 6, 7, 8, 9)), [(weights.shape, bf16)], (early,),
        flops=10**6,
    )
    cot_sender, cot_middle, elinear, upper, *partials = call(
        encode_back_body,
        [(small, bf16), (small, f32), (big, bf16), (big, bf16)] + [((256, latent), bf16)] * 4,
        (*halo_back, far_back, halo_table, far_table, sender_own, middle_part, pre, linear, gslot, gtarget),
        weights, (2, 4), scratch=(vm((768, latent), bf16), vm((2048, 128), f32)), flops=4 * 10**9,
    )
    partials = returned_rows(partials)
    grid_own, mesh_grad, late_own, late_other = call(
        scaled(encode_grads_body, [grid_scale, grid_scale, edge_scale]),
        [((512, latent), f32), (small, bf16), blocks(3), blocks(3)],
        (core, upper, gslot, gtarget, cot_middle, mesh_latent, middle, cot_sender, hidden, elinear),
        weights, (1,), scratch=(held,), flops=2 * 10**9,
    )
    grid_grad, last_own, last_other = call(
        scaled(grid_back_body, [grid_scale]), [((512, latent), bf16), blocks(1), blocks(1)],
        (core, grid_own, *partials, grid_table, grid_latent), weights, (0,),
        scratch=(vm((512, latent), bf16), held),
    )
    (late,) = call(
        pair_body, [blocks(4)], (last_own, swapped(last_other), late_own, swapped(late_other)),
        flops=10**6,
    )
    late = lax.all_to_all(late.reshape(64, 64, 128), CHIPS, 0, 0, tiled=True)
    (late,) = call(sum_body, [((64, 64, 128), bf16)], (late,), flops=10**7)
    late = lax.all_to_all(late, CHIPS, 0, 0, tiled=True)
    other = swapped(late).reshape(blocks(4)[0])
    late = late.reshape(blocks(4)[0])
    weight_grads = pl.pallas_call(
        place_late_body,
        grid_spec=pltpu.PrefetchScalarGridSpec(
            num_scalar_prefetch=1,
            grid=(4,),
            in_specs=[pl.BlockSpec((32, 2, None, 16, 128), lambda i, c: (0, 0, i, 0, 0))] * 2
            + [pl.BlockSpec(memory_space=pl.ANY)],
            out_specs=pl.BlockSpec((None, latent, latent), lambda i, c: (i + i // 3, 0, 0)),
        ),
        out_shape=jax.ShapeDtypeStruct(weights.shape, bf16),
        input_output_aliases={3: 0},
        compiler_params=pltpu.CompilerParams(vmem_limit_bytes=67000000),
        name="place_late",
    )(core, late, other, placed)
    return (mesh_update, grid_grad, mesh_grad, edge_grad, weight_grads)


def solution(mesh):
    row = P(AXES, None)
    wide = jax.sharding.Mesh(mesh.devices.reshape(4, 2, 4, 4), AXES)

    return jax.shard_map(
        on_device,
        mesh=wide,
        in_specs=(row, row, row, row, row, P(AXES, None, None), P(AXES), P(AXES), P(AXES, None, None),
                  P(AXES, None, None), P(AXES), P(AXES), P()),
        out_specs=(row, row, row, row, P()),
        check_vma=False,
    )
```

time: 429 us -> 239 us (0.56)
  waiting for transfers between devices: 271 us -> 15.2 us
  blocking collectives: 0 us -> 78.2 us
  local copies, waits for them, and re-layouts: 53.3 us -> 0.62 us
  Pallas kernels: 46.1 us -> 83 us
  starting transfers between devices: 40.8 us -> 47.4 us
    psum x2 -> x0, waiting for transfers between devices: 261 us -> none  [the longest x1 154 us: on_device(): late = lax.psum(late, AXES)]
    all_to_all x0 -> x3, blocking collectives: none -> 78.2 us  [the longest x1 31.6 us: on_device(): early = lax.all_to_all(early.reshape(64, 96, 128), CHIPS, 0, 0, tiled=True)]
    unnamed x125 -> x2, local copies, waits for them, and re-layouts: 52.3 us -> 0.01 us
    pallas_call x9 -> x14, Pallas kernels: 46.1 us -> 79.1 us  [call(): pl.pallas_call(body, grid=(1,), out_shape=shapes, in_specs=in_specs, out_...]
    ppermute x0 -> x4, starting transfers between devices: none -> 7.2 us  [swapped(): return lax.ppermute(value, 'core', [(0, 1), (1, 0)])]
  transfers between devices with their start and end apart: 20 -> 23, of which waited for: 6 -> 7; matrix products, arithmetic and copies ran while one was open for 0% -> 0% of each run, Pallas kernels for 4% -> 17%
where the time goes in v2:
time: 239 us
  Pallas kernels  83 us (35%)
  blocking collectives  78.2 us (33%)
  starting transfers between devices  47.4 us (20%)
  waiting for transfers between devices  15.2 us (6%)
  between operations  14.1 us (6%)
    pallas_call x14, Pallas kernels, call(): pl.pallas_call(body, grid=(1,), out_shape=shapes, in_specs=in_specs, out_...  79.1 us
    all_to_all x1, blocking collectives, on_device(): early = lax.all_to_all(early.reshape(64, 96, 128), CHIPS, 0, 0, tiled=True)  31.6 us
    ppermute x16, starting transfers between devices, shifted(): return lax.ppermute(value, axis, pairs)  27.1 us
    all_to_all x1, blocking collectives, on_device(): late = lax.all_to_all(late.reshape(64, 64, 128), CHIPS, 0, 0, tiled=True)  25.1 us
    all_to_all x1, blocking collectives, on_device(): late = lax.all_to_all(late, CHIPS, 0, 0, tiled=True)  21.5 us
    all_to_all x2, starting transfers between devices, on_device(): lax.all_to_all(far_out.reshape(peers, 16, 128), AXES, 0, 0, tiled=True)  13.1 us
    ppermute x16, waiting for transfers between devices, shifted(): return lax.ppermute(value, axis, pairs)  12.9 us
    ppermute x4, starting transfers between devices, swapped(): return lax.ppermute(value, 'core', [(0, 1), (1, 0)])  7.2 us
  transfers between devices with their start and end apart: 23, of which 7 were waited for; matrix products, arithmetic and copies ran while one was open for 0% of the time, Pallas kernels for 17%

profile of v2, /device:TPU:1, one launch (start us, length us, event | category | flops | bytes accessed | tf_op | source)
XLA Modules:
  0.0 238.5 jit_solution(9725087426657254300)
XLA Ops:
  7.2 3.3 %shard_map.164 = (bf16[512,512]{1,0:T(8,128)(2,1)}, bf16[256,512]{1,0:T(8,128)(2,1)}, bf16[256,512]{1,0:T(8,128)(2,1)}, bf16[256,512]{1,0:T(8,128)(2,1)}, bf16[256,512]{1,0:T(8,128)(2,1)}) custom-call(bf16[512,512]{1,0:T(8,128)(2,1)} %grid.3, s32[1,4,256]{2,1,0:T(4,128)} %table.3, bf16[10,512,512]{2,1,0:T(8,128)(2,1)} %w0.3), custom_call_target="tpu_custom_call" | custom-call | flops 1000000000 | bytes 2625536 | tf_op jit(solution)/shard_map/pallas_call | solution.py:139
  12.9 4.6 %collective-permute-start.1 = (bf16[256,512]{1,0:T(8,128)(2,1)}, bf16[256,512]{1,0:T(8,128)(2,1)}, u32[]{:S(2)}, u32[]{:S(2)}) collective-permute-start(bf16[256,512]{1,0:T(8,128)(2,1)} %get-tuple-element.59), channel_id=1, source_target_pairs={{0,15},{1,0},{2,1},{3,2},{4,3},{5,4},{6,5},{7,6},{8,7},{9,8},{10,9... | collective-permute-start | bytes 786440 | tf_op jit(solution)/shard_map/ppermute | solution.py:24
  20.2 4.5 %shard_map.165.own = f32[1024,512]{1,0:T(8,128)} custom-call(bf16[512,512]{1,0:T(8,128)(2,1)} %get-tuple-element.57.project, s32[8,128]{1,0:T(8,128)} %bitcast.22, s32[8,128]{1,0:T(8,128)} %bitcast.26, bf16[128,512]{1,0:T(8,128)(2,1)} %mesh.5, bf16[10,512,512]{2,1,0:T(8,128)(2,1)} %w0.3), custom_call_target="tpu_custom_call" | custom-call | flops 1000000000 | bytes 3284992 | tf_op jit(solution)/shard_map/pallas_call | solution.py:139
  25.6 9.2 %shard_map.166 = (f32[1024,512]{1,0:T(8,128)}, f32[1024,512]{1,0:T(8,128)}, bf16[1024,512]{1,0:T(8,128)(2,1)}, bf16[128,512]{1,0:T(8,128)(2,1)}, bf16[128,512]{1...) custom-call(f32[1024,512]{1,0:T(8,128)} %shard_map.165.own, ...), custom_call_target="tpu_custom_call" | custom-call | flops 2000000000 | bytes 10628096 | tf_op jit(solution)/shard_map/pallas_call | solution.py:139
  34.9 8.3 %all-to-all-start = ((bf16[128,16,128]{2,1,0:T(8,128)(2,1)}), bf16[128,16,128]{2,1,0:T(8,128)(2,1)}, u32[]{:S(2)}, u32[]{:S(2)}) async-start(bf16[128,16,128]{2,1,0:T(8,128)(2,1)} %bitcast.21), calls=%async_computation | async-start | bytes 1048576 | tf_op jit(solution)/shard_map/all_to_all | solution.py:453
  44.7 4.1 %collective-permute-start.5 = (bf16[64,512]{1,0:T(8,128)(2,1)}, bf16[64,512]{1,0:T(8,128)(2,1)}, u32[]{:S(2)}, u32[]{:S(2)}) collective-permute-start(bf16[64,512]{1,0:T(8,128)(2,1)} %get-tuple-element.66), channel_id=1, source_target_pairs={{0,15},{1,0},{2,1},{3,2},{4,3},{5,4},{6,5},{7,6},{8,7},{9,8},{10,9... | collective-permute-start | bytes 196616 | tf_op jit(solution)/shard_map/ppermute | solution.py:24
  50.6 5.4 %shard_map.167 = (f32[1024,512]{1,0:T(8,128)}, f32[128,512]{1,0:T(8,128)}) custom-call(bf16[128,512]{1,0:T(8,128)(2,1)} %get-tuple-element.62.middle, bf16[128,512]{1,0:T(8,128)(2,1)} %get-tuple-element.63.sender, bf16[1024,512]{1,0:T(8,128)(2,1)} %edge.3, s32[8,128]{1,0:T(8,128)} %bitcast.32, s32[8,128]{1,0:T(8,128)} %bitcast.34, bf16[10,512,512]{2,1,0:T(8,128)(2,1)} %w0.3, ...), custom_call_target="tpu_custom_call" | custom-call | flops 2000000000 | bytes 5251072 | tf_op jit(solution)/shard_map/pallas_call | solution.py:139
  56.5 13.9 %shard_map.168 = (bf16[128,512]{1,0:T(8,128)(2,1)}, bf16[1024,512]{1,0:T(8,128)(2,1)}, bf16[128,512]{1,0:T(8,128)(2,1)}, bf16[128,512]{1,0:T(8,128)(2,1)}, bf16[...) custom-call(f32[1024,512]{1,0:T(8,128)} %get-tuple-element.64.own, ...), custom_call_target="tpu_custom_call" | custom-call | flops 8000000000 | bytes 11018240 | tf_op jit(solution)/shard_map/pallas_call | solution.py:139
  70.4 8.8 %shard_map.169 = (bf16[1024,512]{1,0:T(8,128)(2,1)}, f32[128,512]{1,0:T(8,128)}, bf16[32,2,6,16,128]{4,3,2,1,0:T(8,128)(2,1)}, bf16[32,2,6,16,128]{4,3,2,1,0:T(8,128)(2,1)}) custom-call(s32[1]{0:T(128)} %bitcast.8.core, bf16[1024,512]{1,0:T(8,128)(2,1)} %edge.3, bf16[1024,512]{1,0:T(8,128)(2,1)} %get-tuple-element.78.cround, ...), custom_call_target="tpu_custom_call" | custom-call | flops 3000000000 | bytes 12189700 | tf_op jit(solution)/shard_map/pallas_call | solution.py:139
  80.9 4.9 %all-to-all-start.1 = ((bf16[128,16,128]{2,1,0:T(8,128)(2,1)}), bf16[128,16,128]{2,1,0:T(8,128)(2,1)}, u32[]{:S(2)}, u32[]{:S(2)}) async-start(bf16[128,16,128]{2,1,0:T(8,128)(2,1)} %bitcast.20), calls=%async_computation.1 | async-start | bytes 1048576 | tf_op jit(solution)/shard_map/all_to_all | solution.py:474
  85.8 5.6 %collective-permute-start.8 = (bf16[64,512]{1,0:T(8,128)(2,1)}, bf16[64,512]{1,0:T(8,128)(2,1)}, u32[]{:S(2)}, u32[]{:S(2)}) collective-permute-start(bf16[64,512]{1,0:T(8,128)(2,1)} %get-tuple-element.72), channel_id=1, source_target_pairs={{0,15},{1,0},{2,1},{3,2},{4,3},{5,4},{6,5},{7,6},{8,7},{9,8},{10,9... | collective-permute-start | bytes 196616 | tf_op jit(solution)/shard_map/ppermute | solution.py:24
  93.1 3.4 %shard_map.175 = bf16[32,2,6,16,128]{4,3,2,1,0:T(8,128)(2,1)} custom-call(bf16[32,2,6,16,128]{4,3,2,1,0:T(8,128)(2,1)} %get-tuple-element.106.refs_0_, bf16[32,2,6,16,128]{4,3,2,1,0:T(8,128)(2,1)} %collective-permute-done.19.refs_1_), custom_call_target="tpu_custom_call" | custom-call | flops 1000000 | bytes 4718592 | tf_op jit(solution)/shard_map/pallas_call | solution.py:139
  99.3 31.6 %all_to_all.25.terms = bf16[64,96,128]{2,1,0:T(8,128)(2,1)} all-to-all(bf16[64,96,128]{2,1,0:T(8,128)(2,1)} %bitcast.17), channel_id=1, replica_groups=mesh['x'=4,'core'=2,'y'=4,'z'=4] {'x','y','z'}, dimensions={0} | all-to-all | bytes 3145728 | tf_op jit(solution)/shard_map/all_to_all | solution.py:490
  133.2 8.8 %shard_map.170 = (bf16[128,512]{1,0:T(8,128)(2,1)}, f32[128,512]{1,0:T(8,128)}, bf16[1024,512]{1,0:T(8,128)(2,1)}, bf16[1024,512]{1,0:T(8,128)(2,1)}, bf16[256,5...) custom-call(bf16[64,512]{1,0:T(8,128)(2,1)} %collective-permute-done.8.in0, ...), custom_call_target="tpu_custom_call" | custom-call | flops 4000000000 | bytes 10103808 | tf_op jit(solution)/shard_map/pallas_call | solution.py:139
  142.0 5.4 %shard_map.171 = (f32[512,512]{1,0:T(8,128)}, bf16[128,512]{1,0:T(8,128)(2,1)}, bf16[32,2,3,16,128]{4,3,2,1,0:T(8,128)(2,1)}, bf16[32,2,3,16,128]{4,3,2,1,0:T(8,128)(2,1)}) custom-call(s32[1]{0:T(128)} %bitcast.8.core, bf16[1024,512]{1,0:T(8,128)(2,1)} %get-tuple-element.89.upper, s32[8,128]{1,0:T(8,128)} %bitcast.25, s32[8,128]{1,0:T(8,128)} %bitcast.29, ...), custom_call_target="tpu_custom_call" | custom-call | flops 2000000000 | bytes 7086084 | tf_op jit(solution)/shard_map/pallas_call | solution.py:139
  151.5 5.0 %collective-permute-done.12.in0 = bf16[256,512]{1,0:T(8,128)(2,1)} collective-permute-done((bf16[256,512]{1,0:T(8,128)(2,1)}, bf16[256,512]{1,0:T(8,128)(2,1)}, u32[]{:S(2)}, u32[]{:S(2)}) %collective-permute-start.12) | collective-permute-done | bytes 262176 | tf_op jit(solution)/shard_map/ppermute | solution.py:24
  156.5 4.4 %collective-permute-done.13.in1 = bf16[256,512]{1,0:T(8,128)(2,1)} collective-permute-done((bf16[256,512]{1,0:T(8,128)(2,1)}, bf16[256,512]{1,0:T(8,128)(2,1)}, u32[]{:S(2)}, u32[]{:S(2)}) %collective-permute-start.13) | collective-permute-done | bytes 262176 | tf_op jit(solution)/shard_map/ppermute | solution.py:24
  160.9 4.1 %shard_map.172 = (bf16[512,512]{1,0:T(8,128)(2,1)}, bf16[32,2,1,16,128]{4,3,2,1,0:T(8,128)(2,1)}, bf16[32,2,1,16,128]{4,3,2,1,0:T(8,128)(2,1)}) custom-call(s32[1]{0:T(128)} %bitcast.8.core, f32[512,512]{1,0:T(8,128)} %get-tuple-element.94.grid_own, bf16[256,512]{1,0:T(8,128)(2,1)} %collective-permute-done.12.in0, ...), custom_call_target="tpu_custom_call" | custom-call | flops 1000000000 | bytes 4198404 | tf_op jit(solution)/shard_map/pallas_call | solution.py:139
  167.8 2.8 %shard_map.173 = bf16[32,2,4,16,128]{4,3,2,1,0:T(8,128)(2,1)} custom-call(bf16[32,2,1,16,128]{4,3,2,1,0:T(8,128)(2,1)} %get-tuple-element.102.refs_0_, bf16[32,2,1,16,128]{4,3,2,1,0:T(8,128)(2,1)} %collective-permute-done.16.refs_1_, bf16[32,2,3,16,128]{4,3,2,1,0:T(8,128)(2,1)} %get-tuple-element.104.refs_2_, ...), custom_call_target="tpu_custom_call" | custom-call | flops 1000000 | bytes 3145728 | tf_op jit(solution)/shard_map/pallas_call | solution.py:139
  170.5 25.1 %all_to_all.26.terms = bf16[64,64,128]{2,1,0:T(8,128)(2,1)} all-to-all(bf16[64,64,128]{2,1,0:T(8,128)(2,1)} %bitcast.18), channel_id=1, replica_groups=mesh['x'=4,'core'=2,'y'=4,'z'=4] {'x','y','z'}, dimensions={0} | all-to-all | bytes 2097152 | tf_op jit(solution)/shard_map/all_to_all | solution.py:519
  198.1 21.5 %all_to_all.27 = bf16[64,64,128]{2,1,0:T(8,128)(2,1)} all-to-all(bf16[64,64,128]{2,1,0:T(8,128)(2,1)} %shard_map.174), channel_id=1, replica_groups=mesh['x'=4,'core'=2,'y'=4,'z'=4] {'x','y','z'}, dimensions={0} | all-to-all | bytes 2097152 | tf_op jit(solution)/shard_map/all_to_all | solution.py:521
  219.6 3.4 %collective-permute-start.18 = (bf16[64,64,128]{2,1,0:T(8,128)(2,1)}, bf16[64,64,128]{2,1,0:T(8,128)(2,1)}, u32[]{:S(2)}, u32[]{:S(2)}) collective-permute-start(bf16[64,64,128]{2,1,0:T(8,128)(2,1)} %all_to_all.27), channel_id=1, source_target_pairs={{0,16},{16,0},{1,17},{17,1},{2,18},{18,2},{3,19},{19,3},{4,20},{20... | collective-permute-start | bytes 3145736 | tf_op jit(solution)/shard_map/ppermute | solution.py:412
  223.0 4.8 %shard_map.177.kept = bf16[10,512,512]{2,1,0:T(8,128)(2,1)} custom-call(bf16[4,2,8,2,6,16,128]{6,5,4,3,2,1,0:T(8,128)(2,1)} %bitcast.19), custom_call_target="tpu_custom_call" | custom-call | flops 1000000 | bytes 8388608 | tf_op jit(solution)/shard_map/pallas_call | solution.py:139
  227.8 3.9 %place_late.1 = bf16[10,512,512]{2,1,0:T(8,128)(2,1)} custom-call(s32[1]{0:T(128)} %bitcast.8.core, bf16[32,2,4,16,128]{4,3,2,1,0:T(8,128)(2,1)} %bitcast.13.own, bf16[32,2,4,16,128]{4,3,2,1,0:T(8,128)(2,1)} %bitcast.14.other, bf16[10,512,512]{2,1,0:T(8,128)(2,1)} %shard_map.177.kept), custom_call_target="tpu_custom_call", output_to_operand_aliasing={{}: (3, {})} | custom-call | tf_op jit(solution)/shard_map/place_late/pallas_call | solution.py:524
  (44 shorter events, 27.8 us)
Async XLA Ops:
  7.2 12.4 %copy-start = (s32[1,4,64]{2,1,0:T(4,128)S(1)}, s32[1,4,64]{2,1,0:T(4,128)}, u32[]{:S(2)}) copy-start(s32[1,4,64]{2,1,0:T(4,128)} %param.21) | copy-start | bytes 3076
  10.4 14.2 %collective-permute-start = (bf16[256,512]{1,0:T(8,128)(2,1)}, bf16[256,512]{1,0:T(8,128)(2,1)}, u32[]{:S(2)}, u32[]{:S(2)}) collective-permute-start(bf16[256,512]{1,0:T(8,128)(2,1)} %get-tuple-element.58), channel_id=1, source_target_pairs={{0,1},{1,2},{2,3},{3,4},{4,5},{5,6},{6,7},{7,8},{8,9},{9,10},{10,1... | collective-permute-start | bytes 786440 | tf_op jit(solution)/shard_map/ppermute | solution.py:24
  12.9 11.8 %collective-permute-start.1 = (bf16[256,512]{1,0:T(8,128)(2,1)}, bf16[256,512]{1,0:T(8,128)(2,1)}, u32[]{:S(2)}, u32[]{:S(2)}) collective-permute-start(bf16[256,512]{1,0:T(8,128)(2,1)} %get-tuple-element.59), channel_id=1, source_target_pairs={{0,15},{1,0},{2,1},{3,2},{4,3},{5,4},{6,5},{7,6},{8,7},{9,8},{10,9... | collective-permute-start | bytes 786440 | tf_op jit(solution)/shard_map/ppermute | solution.py:24
  17.5 7.2 %collective-permute-start.2 = (bf16[256,512]{1,0:T(8,128)(2,1)}, bf16[256,512]{1,0:T(8,128)(2,1)}, u32[]{:S(2)}, u32[]{:S(2)}) collective-permute-start(bf16[256,512]{1,0:T(8,128)(2,1)} %get-tuple-element.60), channel_id=1, source_target_pairs={{0,16},{16,32},{32,48},{48,64},{64,80},{80,96},{96,112},{112,0},{1... | collective-permute-start | bytes 786440 | tf_op jit(solution)/shard_map/ppermute | solution.py:24
  19.5 6.1 %collective-permute-start.3 = (bf16[256,512]{1,0:T(8,128)(2,1)}, bf16[256,512]{1,0:T(8,128)(2,1)}, u32[]{:S(2)}, u32[]{:S(2)}) collective-permute-start(bf16[256,512]{1,0:T(8,128)(2,1)} %get-tuple-element.61), channel_id=1, source_target_pairs={{0,112},{16,0},{32,16},{48,32},{64,48},{80,64},{96,80},{112,96},{1... | collective-permute-start | bytes 786440 | tf_op jit(solution)/shard_map/ppermute | solution.py:24
  34.9 21.7 %all-to-all-start = ((bf16[128,16,128]{2,1,0:T(8,128)(2,1)}), bf16[128,16,128]{2,1,0:T(8,128)(2,1)}, u32[]{:S(2)}, u32[]{:S(2)}) async-start(bf16[128,16,128]{2,1,0:T(8,128)(2,1)} %bitcast.21), calls=%async_computation | async-start | bytes 1048576 | tf_op jit(solution)/shard_map/all_to_all | solution.py:453
  43.1 12.9 %collective-permute-start.4 = (bf16[64,512]{1,0:T(8,128)(2,1)}, bf16[64,512]{1,0:T(8,128)(2,1)}, u32[]{:S(2)}, u32[]{:S(2)}) collective-permute-start(bf16[64,512]{1,0:T(8,128)(2,1)} %get-tuple-element.65), channel_id=1, source_target_pairs={{0,1},{1,2},{2,3},{3,4},{4,5},{5,6},{6,7},{7,8},{8,9},{9,10},{10,1... | collective-permute-start | bytes 196616 | tf_op jit(solution)/shard_map/ppermute | solution.py:24
  44.7 11.3 %collective-permute-start.5 = (bf16[64,512]{1,0:T(8,128)(2,1)}, bf16[64,512]{1,0:T(8,128)(2,1)}, u32[]{:S(2)}, u32[]{:S(2)}) collective-permute-start(bf16[64,512]{1,0:T(8,128)(2,1)} %get-tuple-element.66), channel_id=1, source_target_pairs={{0,15},{1,0},{2,1},{3,2},{4,3},{5,4},{6,5},{7,6},{8,7},{9,8},{10,9... | collective-permute-start | bytes 196616 | tf_op jit(solution)/shard_map/ppermute | solution.py:24
  48.8 7.2 %collective-permute-start.6 = (bf16[64,512]{1,0:T(8,128)(2,1)}, bf16[64,512]{1,0:T(8,128)(2,1)}, u32[]{:S(2)}, u32[]{:S(2)}) collective-permute-start(bf16[64,512]{1,0:T(8,128)(2,1)} %get-tuple-element.67), channel_id=1, source_target_pairs={{0,16},{16,32},{32,48},{48,64},{64,80},{80,96},{96,112},{112,0},{1... | collective-permute-start | bytes 196616 | tf_op jit(solution)/shard_map/ppermute | solution.py:24
  50.6 5.4 %collective-permute-start.7 = (bf16[64,512]{1,0:T(8,128)(2,1)}, bf16[64,512]{1,0:T(8,128)(2,1)}, u32[]{:S(2)}, u32[]{:S(2)}) collective-permute-start(bf16[64,512]{1,0:T(8,128)(2,1)} %get-tuple-element.68), channel_id=1, source_target_pairs={{0,112},{16,0},{32,16},{48,32},{64,48},{80,64},{96,80},{112,96},{1... | collective-permute-start | bytes 196616 | tf_op jit(solution)/shard_map/ppermute | solution.py:24
  79.3 13.8 %collective-permute-start.19 = (bf16[32,2,6,16,128]{4,3,2,1,0:T(8,128)(2,1)}, bf16[32,2,6,16,128]{4,3,2,1,0:T(8,128)(2,1)}, u32[]{:S(2)}, u32[]{:S(2)}) collective-permute-start(bf16[32,2,6,16,128]{4,3,2,1,0:T(8,128)(2,1)} %get-tuple-element.107), channel_id=1, source_target_pairs={{0,16},{16,0},{1,17},{17,1},{2,18},{18,2},{3,19},{19,3},{4,20},{20... | collective-permute-start | bytes 4718600 | tf_op jit(solution)/shard_map/ppermute | solution.py:412
  80.9 18.5 %all-to-all-start.1 = ((bf16[128,16,128]{2,1,0:T(8,128)(2,1)}), bf16[128,16,128]{2,1,0:T(8,128)(2,1)}, u32[]{:S(2)}, u32[]{:S(2)}) async-start(bf16[128,16,128]{2,1,0:T(8,128)(2,1)} %bitcast.20), calls=%async_computation.1 | async-start | bytes 1048576 | tf_op jit(solution)/shard_map/all_to_all | solution.py:474
  85.7 137.3 %all-gather.2.cloned.1.call-start = ((), (), s32[]{:S(2)}) async-start(), calls=%async_computation.5 | async-start | bytes 3170304 | tf_op jit(solution)/shard_map/all_gather | solution.py:492
  85.8 10.7 %collective-permute-start.8 = (bf16[64,512]{1,0:T(8,128)(2,1)}, bf16[64,512]{1,0:T(8,128)(2,1)}, u32[]{:S(2)}, u32[]{:S(2)}) collective-permute-start(bf16[64,512]{1,0:T(8,128)(2,1)} %get-tuple-element.72), channel_id=1, source_target_pairs={{0,15},{1,0},{2,1},{3,2},{4,3},{5,4},{6,5},{7,6},{8,7},{9,8},{10,9... | collective-permute-start | bytes 196616 | tf_op jit(solution)/shard_map/ppermute | solution.py:24
  91.3 7.7 %collective-permute-start.9 = (bf16[64,512]{1,0:T(8,128)(2,1)}, bf16[64,512]{1,0:T(8,128)(2,1)}, u32[]{:S(2)}, u32[]{:S(2)}) collective-permute-start(bf16[64,512]{1,0:T(8,128)(2,1)} %get-tuple-element.73), channel_id=1, source_target_pairs={{0,1},{1,2},{2,3},{3,4},{4,5},{5,6},{6,7},{7,8},{8,9},{9,10},{10,1... | collective-permute-start | bytes 196616 | tf_op jit(solution)/shard_map/ppermute | solution.py:24
  91.3 7.7 %collective-permute-start.10 = (bf16[64,512]{1,0:T(8,128)(2,1)}, bf16[64,512]{1,0:T(8,128)(2,1)}, u32[]{:S(2)}, u32[]{:S(2)}) collective-permute-start(bf16[64,512]{1,0:T(8,128)(2,1)} %get-tuple-element.74), channel_id=1, source_target_pairs={{0,112},{16,0},{32,16},{48,32},{64,48},{80,64},{96,80},{112,96},{1... | collective-permute-start | bytes 196616 | tf_op jit(solution)/shard_map/ppermute | solution.py:24
  92.0 7.1 %collective-permute-start.11 = (bf16[64,512]{1,0:T(8,128)(2,1)}, bf16[64,512]{1,0:T(8,128)(2,1)}, u32[]{:S(2)}, u32[]{:S(2)}) collective-permute-start(bf16[64,512]{1,0:T(8,128)(2,1)} %get-tuple-element.75), channel_id=1, source_target_pairs={{0,16},{16,32},{32,48},{48,64},{64,80},{80,96},{96,112},{112,0},{1... | collective-permute-start | bytes 196616 | tf_op jit(solution)/shard_map/ppermute | solution.py:24
  147.3 20.4 %collective-permute-start.17 = (bf16[32,2,3,16,128]{4,3,2,1,0:T(8,128)(2,1)}, bf16[32,2,3,16,128]{4,3,2,1,0:T(8,128)(2,1)}, u32[]{:S(2)}, u32[]{:S(2)}) collective-permute-start(bf16[32,2,3,16,128]{4,3,2,1,0:T(8,128)(2,1)} %get-tuple-element.105), channel_id=1, source_target_pairs={{0,16},{16,0},{1,17},{17,1},{2,18},{18,2},{3,19},{19,3},{4,20},{20... | collective-permute-start | bytes 2359304 | tf_op jit(solution)/shard_map/ppermute | solution.py:412
  148.3 8.2 %collective-permute-start.12 = (bf16[256,512]{1,0:T(8,128)(2,1)}, bf16[256,512]{1,0:T(8,128)(2,1)}, u32[]{:S(2)}, u32[]{:S(2)}) collective-permute-start(bf16[256,512]{1,0:T(8,128)(2,1)} %get-tuple-element.95), channel_id=1, source_target_pairs={{0,15},{1,0},{2,1},{3,2},{4,3},{5,4},{6,5},{7,6},{8,7},{9,8},{10,9... | collective-permute-start | bytes 786440 | tf_op jit(solution)/shard_map/ppermute | solution.py:24
  149.8 11.1 %collective-permute-start.13 = (bf16[256,512]{1,0:T(8,128)(2,1)}, bf16[256,512]{1,0:T(8,128)(2,1)}, u32[]{:S(2)}, u32[]{:S(2)}) collective-permute-start(bf16[256,512]{1,0:T(8,128)(2,1)} %get-tuple-element.96), channel_id=1, source_target_pairs={{0,1},{1,2},{2,3},{3,4},{4,5},{5,6},{6,7},{7,8},{8,9},{9,10},{10,1... | collective-permute-start | bytes 786440 | tf_op jit(solution)/shard_map/ppermute | solution.py:24
  149.8 11.1 %collective-permute-start.14 = (bf16[256,512]{1,0:T(8,128)(2,1)}, bf16[256,512]{1,0:T(8,128)(2,1)}, u32[]{:S(2)}, u32[]{:S(2)}) collective-permute-start(bf16[256,512]{1,0:T(8,128)(2,1)} %get-tuple-element.97), channel_id=1, source_target_pairs={{0,112},{16,0},{32,16},{48,32},{64,48},{80,64},{96,80},{112,96},{1... | collective-permute-start | bytes 786440 | tf_op jit(solution)/shard_map/ppermute | solution.py:24
  150.4 10.5 %collective-permute-start.15 = (bf16[256,512]{1,0:T(8,128)(2,1)}, bf16[256,512]{1,0:T(8,128)(2,1)}, u32[]{:S(2)}, u32[]{:S(2)}) collective-permute-start(bf16[256,512]{1,0:T(8,128)(2,1)} %get-tuple-element.98), channel_id=1, source_target_pairs={{0,16},{16,32},{32,48},{48,64},{64,80},{80,96},{96,112},{112,0},{1... | collective-permute-start | bytes 786440 | tf_op jit(solution)/shard_map/ppermute | solution.py:24
  165.1 2.7 %collective-permute-start.16 = (bf16[32,2,1,16,128]{4,3,2,1,0:T(8,128)(2,1)}, bf16[32,2,1,16,128]{4,3,2,1,0:T(8,128)(2,1)}, u32[]{:S(2)}, u32[]{:S(2)}) collective-permute-start(bf16[32,2,1,16,128]{4,3,2,1,0:T(8,128)(2,1)} %get-tuple-element.103), channel_id=1, source_target_pairs={{0,16},{16,0},{1,17},{17,1},{2,18},{18,2},{3,19},{19,3},{4,20},{20... | collective-permute-start | bytes 786440 | tf_op jit(solution)/shard_map/ppermute | solution.py:412
  219.6 8.2 %collective-permute-start.18 = (bf16[64,64,128]{2,1,0:T(8,128)(2,1)}, bf16[64,64,128]{2,1,0:T(8,128)(2,1)}, u32[]{:S(2)}, u32[]{:S(2)}) collective-permute-start(bf16[64,64,128]{2,1,0:T(8,128)(2,1)} %all_to_all.27), channel_id=1, source_target_pairs={{0,16},{16,0},{1,17},{17,1},{2,18},{18,2},{3,19},{19,3},{4,20},{20... | collective-permute-start | bytes 3145736 | tf_op jit(solution)/shard_map/ppermute | solution.py:412
Sparse Core Ops, SparseCore 0:
  133.3 68.0 all-gather.1

commit v3 on v2

--- a/solution.py
+++ b/solution.py
@@ -15,7 +15,8 @@
 CHIPS = ("x", "y", "z")
 FACE = ("x", "core")
 SUB = ("y", "z")
-CHUNK = 256
+CHUNK = 512
+ROWS = CHUNK // 128
 
 
 def shifted(value, axis, steps):
@@ -149,7 +150,7 @@
 
 
 def project_body(grid, table, w0, project, out0, out1, out2, out3):
-    chunks(2, lambda i, s: project.__setitem__((s, slice(None)), dot(grid[s, :], w0[...]).astype(bf16)))
+    chunks(512 // CHUNK, lambda i, s: project.__setitem__((s, slice(None)), dot(grid[s, :], w0[...]).astype(bf16)))
     for k, out in enumerate((out0, out1, out2, out3)):
         picked = jnp.concatenate([pick_rows(row, 0, 512) for row in table_rows(table, k)], axis=0)
         out[...] = dot(picked, project[...]).astype(bf16)
@@ -160,10 +161,10 @@
     source[512:768, :] = stack_halves(dot(mesh[...], w1[...]))
 
     def step(i, s):
-        receiver = pick(target, 2 * i, 2, 0, 128)
-        own[s, :] = dot(jnp.concatenate([pick(slot, 2 * i, 2, 0, 512), twice(receiver)], axis=1), source[...])
-
-    chunks(4, step)
+        receiver = pick(target, ROWS * i, ROWS, 0, 128)
+        own[s, :] = dot(jnp.concatenate([pick(slot, ROWS * i, ROWS, 0, 512), twice(receiver)], axis=1), source[...])
+
+    chunks(1024 // CHUNK, step)
 
 
 def far_slots(slot):
@@ -181,16 +182,16 @@
     def step(i, s):
         pre = own[s, :]
         for k, block in enumerate((in0, in1, in2, in3)):
-            pre = pre + dot(pick(slot, 2 * i, 2, 512 + 256 * k, 256), block[...])
+            pre = pre + dot(pick(slot, ROWS * i, ROWS, 512 + 256 * k, 256), block[...])
         pre_out[s, :] = pre
         hidden = silu(pre).astype(bf16)
         hidden_out[s, :] = hidden
         linear = dot(hidden, w2[...])
         linear_out[s, :] = linear
         message = norm_parts(linear)[0].astype(bf16)
-        total[...] += dot(put(target, 2 * i, 2, 0, 128), message)
-
-    chunks(4, step)
+        total[...] += dot(put(target, ROWS * i, ROWS, 0, 128), message)
+
+    chunks(1024 // CHUNK, step)
     middle = (mesh[...].astype(f32) + total[...]).astype(bf16)
     middle_out[...] = middle
     sender = dot(middle, w4[...]).astype(bf16)
@@ -211,11 +212,11 @@
     update_own[...] = dot(middle[...], w7[...])
 
     def step(i, s):
-        receiver = pick(target, 2 * i, 2, 0, 128)
-        picked = jnp.concatenate([pick(slot, 2 * i, 2, 0, 128), twice(receiver)], axis=1)
+        receiver = pick(target, ROWS * i, ROWS, 0, 128)
+        picked = jnp.concatenate([pick(slot, ROWS * i, ROWS, 0, 128), twice(receiver)], axis=1)
         own[s, :] = dot(edge[s, :], w3[...]) + dot(picked, source[...])
 
-    chunks(4, step)
+    chunks(1024 // CHUNK, step)
 
 
 def gather_far(wide, source, first):
@@ -240,16 +241,16 @@
     total[...] = jnp.zeros_like(total)
 
     def forward(i, s):
-        pre = own[s, :] + dot(pick(slots, 2 * i, 2, 128, 768), source[...])
+        pre = own[s, :] + dot(pick(slots, ROWS * i, ROWS, 128, 768), source[...])
         pre_s[s, :] = pre
         hidden = silu(pre).astype(bf16)
         hidden_out[s, :] = hidden
         normed, inverse = norm_parts(dot(hidden, w6[...]))
         normed_s[s, :] = normed
         inverse_s[s, :] = jnp.broadcast_to(inverse, (CHUNK, 128))
-        total[...] += dot(put(target, 2 * i, 2, 0, 128), normed.astype(bf16))
-
-    chunks(4, forward)
+        total[...] += dot(put(target, ROWS * i, ROWS, 0, 128), normed.astype(bf16))
+
+    chunks(1024 // CHUNK, forward)
     rounded = total[...].astype(bf16)
     round_out[...] = rounded
     pre = update_own[...] + dot(rounded, w8[...])
@@ -264,13 +265,13 @@
     cot_total = stack_halves(dot_nt(cot_update, w8[...]))
 
     def backward(i, s):
-        receiver = pick(target, 2 * i, 2, 0, 128)
+        receiver = pick(target, ROWS * i, ROWS, 0, 128)
         upstream = dot(twice(receiver), cot_total) + edge_cot[s, :].astype(f32)
         cot = norm_back(normed_s[s, :], inverse_s[s, 0:1], upstream).astype(bf16)
         plinear_out[s, :] = cot
         cround_out[s, :] = (dot_nt(cot, w6[...]) * slope(pre_s[s, :])).astype(bf16)
 
-    chunks(4, backward)
+    chunks(1024 // CHUNK, backward)
     kept = jnp.concatenate([put(target, 0, 8, 0, 128), put(slots, 0, 8, 0, 128)], axis=0)
     kept = dot(kept, cround_out[...])
     receive_out[...] = kept[0:128, :].astype(bf16)
@@ -310,7 +311,7 @@
     def step(i, s):
         edge_grad[s, :] = (edge_cot[s, :].astype(f32) + dot_nt(cround[s, :], w3[...])).astype(bf16)
 
-    chunks(4, step)
+    chunks(1024 // CHUNK, step)
 
 
 def encode_back_body(
@@ -330,13 +331,13 @@
     cot_middle = stack_halves(cot_middle)
 
     def step(i, s):
-        receiver = pick(target, 2 * i, 2, 0, 128)
+        receiver = pick(target, ROWS * i, ROWS, 0, 128)
         normed, inverse = norm_parts(linear[s, :])
         cot = norm_back(normed, inverse, dot(twice(receiver), cot_middle)).astype(bf16)
         elinear_out[s, :] = cot
         upper_out[s, :] = (dot_nt(cot, w2[...]) * slope(pre[s, :])).astype(bf16)
 
-    chunks(4, step)
+    chunks(1024 // CHUNK, step)
     for k, out in enumerate((g0, g1, g2, g3)):
         spread = put(slot, 0, 8, 512 + 256 * k, 256)
         out[...] = dot(spread, upper_out[...]).astype(bf16)
@@ -360,10 +361,10 @@
 
 def grid_back_body(scales, core, grid_own, in0, in1, in2, in3, table, grid, w0, grid_grad, grads_own, grads_other, cot, held):
     for i in range(2):
-        s = slice(CHUNK * i, CHUNK * i + CHUNK)
+        s = slice(256 * i, 256 * i + 256)
         total = grid_own[s, :]
         for k, block in enumerate((in0, in1, in2, in3)):
-            total = total + dot(put_rows(table_rows(table, k), i * CHUNK, CHUNK), block[...])
+            total = total + dot(put_rows(table_rows(table, k), i * 256, 256), block[...])
         total = total.astype(bf16)
         cot[s, :] = total
         grid_grad[s, :] = dot_nt(total, w0[...]).astype(bf16)
@@ -391,21 +392,17 @@
             shard[0][p] = total
 
 
-def place_early_body(order, blocks, out):
-    for place, k in enumerate(order):
-        for c in range(2):
-            for q in range(2):
-                first = 256 * c + 128 * q
-                out[k, :, first : first + 128] = blocks[:, c, :, q, place].reshape(512, 128)
-
-
-def place_late_body(core, own, other, kept, out):
-    del kept
+def place_early_body(core, own, other, out):
     first = core[0] == 0
     for q in range(2):
         a, b = own[:, q].reshape(512, 128), other[:, q].reshape(512, 128)
         out[:, 128 * q : 128 * q + 128] = jnp.where(first, a, b)
         out[:, 256 + 128 * q : 384 + 128 * q] = jnp.where(first, b, a)
+
+
+def place_late_body(core, own, other, kept, out):
+    del kept
+    place_early_body(core, own, other, out)
 
 
 def swapped(value):
@@ -485,15 +482,9 @@
          edge_cotangent, mesh_cotangent),
         weights, (3, 5, 7), scratch=(held,), flops=3 * 10**9,
     )
-    (early,) = call(pair_body, [blocks(6)], (early_own, swapped(early_other)), flops=10**6)
+    early = (early_own.astype(f32) + swapped(early_other).astype(f32)).astype(bf16)
     early, _ = lax.optimization_barrier((early, (halo_back, far_back)))
     early = lax.all_to_all(early.reshape(64, 96, 128), CHIPS, 0, 0, tiled=True)
-    (early,) = call(sum_body, [((96, 128), bf16)], (early,), flops=10**7)
-    early = lax.all_gather(early, AXES, axis=0, tiled=True).reshape(4, 2, 8, 2, 6, 16, 128)
-    (placed,) = call(
-        functools.partial(place_early_body, (3, 5, 6, 7, 8, 9)), [(weights.shape, bf16)], (early,),
-        flops=10**6,
-    )
     cot_sender, cot_middle, elinear, upper, *partials = call(
         encode_back_body,
         [(small, bf16), (small, f32), (big, bf16), (big, bf16)] + [((256, latent), bf16)] * 4,
@@ -507,6 +498,8 @@
         (core, upper, gslot, gtarget, cot_middle, mesh_latent, middle, cot_sender, hidden, elinear),
         weights, (1,), scratch=(held,), flops=2 * 10**9,
     )
+    (early,) = call(sum_body, [((64, 96, 128), bf16)], (early,), flops=10**7)
+    early = lax.all_to_all(early, CHIPS, 0, 0, tiled=True)
     grid_grad, last_own, last_other = call(
         scaled(grid_back_body, [grid_scale]), [((512, latent), bf16), blocks(1), blocks(1)],
         (core, grid_own, *partials, grid_table, grid_latent), weights, (0,),
@@ -516,7 +509,22 @@
         pair_body, [blocks(4)], (last_own, swapped(last_other), late_own, swapped(late_other)),
         flops=10**6,
     )
+    late, early = lax.optimization_barrier((late, early))
     late = lax.all_to_all(late.reshape(64, 64, 128), CHIPS, 0, 0, tiled=True)
+    early_swapped = swapped(early).reshape(blocks(6)[0])
+    early = early.reshape(blocks(6)[0])
+    placed = pl.pallas_call(
+        place_early_body,
+        grid_spec=pltpu.PrefetchScalarGridSpec(
+            num_scalar_prefetch=1,
+            grid=(6,),
+            in_specs=[pl.BlockSpec((32, 2, None, 16, 128), lambda i, c: (0, 0, i, 0, 0))] * 2,
+            out_specs=pl.BlockSpec((None, latent, latent), lambda i, c: (i + 3 + (i + 5) // 6, 0, 0)),
+        ),
+        out_shape=jax.ShapeDtypeStruct(weights.shape, bf16),
+        compiler_params=pltpu.CompilerParams(vmem_limit_bytes=67000000),
+        name="place_early",
+    )(core, early, early_swapped)
     (late,) = call(sum_body, [((64, 64, 128), bf16)], (late,), flops=10**7)
     late = lax.all_to_all(late, CHIPS, 0, 0, tiled=True)
     other = swapped(late).reshape(blocks(4)[0])

time: 239 us -> 227 us (0.950)
  blocking collectives: 78.2 us -> 50.8 us
  starting transfers between devices: 47.4 us -> 65.9 us
  waiting for transfers between devices: 15.2 us -> 30.7 us
  between operations: 14.1 us -> 0.74 us
  Pallas kernels: 83 us -> 75 us
    all_to_all x1 -> x0, blocking collectives: 21.5 us -> none  [on_device(): late = lax.all_to_all(late, CHIPS, 0, 0, tiled=True)]
    all_to_all x0 -> x2, waiting for transfers between devices: none -> 13.4 us  [the longest x1 13.4 us: on_device(): late = lax.all_to_all(late, CHIPS, 0, 0, tiled=True)]
    pallas_call x14 -> x12, Pallas kernels: 79.1 us -> 65.7 us  [call(): pl.pallas_call(body, grid=(1,), out_shape=shapes, in_specs=in_specs, out_...]
    all_to_all x0 -> x2, starting transfers between devices: none -> 12.3 us  [the longest x1 6.69 us: on_device(): early = lax.all_to_all(early, CHIPS, 0, 0, tiled=True)]
    pallas_call x0 -> x1, Pallas kernels: none -> 5.43 us  [on_device(): pl.pallas_call(place_early_body, grid_spec=pltpu.PrefetchScalarGridSpec(n...]
    ppermute x4 -> x5, starting transfers between devices: 7.2 us -> 10.6 us  [swapped(): return lax.ppermute(value, 'core', [(0, 1), (1, 0)])]
    all_to_all x1, blocking collectives: 31.6 us -> 28.4 us  [on_device(): early = lax.all_to_all(early.reshape(64, 96, 128), CHIPS, 0, 0, tiled=True)]
    ppermute x16, starting transfers between devices: 27.1 us -> 30.1 us  [shifted(): return lax.ppermute(value, axis, pairs)]
  transfers between devices with their start and end apart: 23 -> 25, of which waited for: 7 -> 8; matrix products, arithmetic and copies ran while one was open for 0% -> 1% of each run, Pallas kernels for 17% -> 15%
where the time goes in v3:
time: 227 us; the launch traced here: 226 us
  Pallas kernels  75 us (33%)
  starting transfers between devices  65.9 us (29%)
  blocking collectives  50.8 us (22%)
  waiting for transfers between devices  30.7 us (14%)
    pallas_call x12, Pallas kernels, call(): pl.pallas_call(body, grid=(1,), out_shape=shapes, in_specs=in_specs, out_...  65.7 us
    ppermute x16, starting transfers between devices, shifted(): return lax.ppermute(value, axis, pairs)  30.1 us
    all_to_all x1, blocking collectives, on_device(): early = lax.all_to_all(early.reshape(64, 96, 128), CHIPS, 0, 0, tiled=True)  28.4 us
    all_to_all x1, blocking collectives, on_device(): late = lax.all_to_all(late.reshape(64, 64, 128), CHIPS, 0, 0, tiled=True)  22.4 us
    ppermute x16, waiting for transfers between devices, shifted(): return lax.ppermute(value, axis, pairs)  14.8 us
    all_to_all x1, waiting for transfers between devices, on_device(): late = lax.all_to_all(late, CHIPS, 0, 0, tiled=True)  13.4 us
    all_to_all x2, starting transfers between devices, on_device(): lax.all_to_all(far_out.reshape(peers, 16, 128), AXES, 0, 0, tiled=True)  12.9 us
    ppermute x5, starting transfers between devices, swapped(): return lax.ppermute(value, 'core', [(0, 1), (1, 0)])  10.6 us
  transfers between devices with their start and end apart: 25, of which 8 were waited for; matrix products, arithmetic and copies ran while one was open for 1% of the time, Pallas kernels for 15%

profile of v3, /device:TPU:1, one launch (start us, length us, event | category | flops | bytes accessed | tf_op | source)
XLA Modules:
  0.0 225.8 jit_solution(14889409734769782192)
XLA Ops:
  6.1 4.6 %collective-permute-start.1 = (bf16[256,512]{1,0:T(8,128)(2,1)}, bf16[256,512]{1,0:T(8,128)(2,1)}, u32[]{:S(2)}, u32[]{:S(2)}) collective-permute-start(bf16[256,512]{1,0:T(8,128)(2,1)} %get-tuple-element.61), channel_id=1, source_target_pairs={{0,15},{1,0},{2,1},{3,2},{4,3},{5,4},{6,5},{7,6},{8,7},{9,8},{10,9... | collective-permute-start | bytes 786440 | tf_op jit(solution)/shard_map/ppermute | solution.py:25
  13.3 4.1 %shard_map.165.own = f32[1024,512]{1,0:T(8,128)} custom-call(bf16[512,512]{1,0:T(8,128)(2,1)} %get-tuple-element.59.project, s32[8,128]{1,0:T(8,128)} %bitcast.22, s32[8,128]{1,0:T(8,128)} %bitcast.26, bf16[128,512]{1,0:T(8,128)(2,1)} %mesh.5, bf16[10,512,512]{2,1,0:T(8,128)(2,1)} %w0.3), custom_call_target="tpu_custom_call" | custom-call | flops 1000000000 | bytes 3284992 | tf_op jit(solution)/shard_map/pallas_call | solution.py:140
  18.8 7.8 %shard_map.166 = (f32[1024,512]{1,0:T(8,128)}, f32[1024,512]{1,0:T(8,128)}, bf16[1024,512]{1,0:T(8,128)(2,1)}, bf16[128,512]{1,0:T(8,128)(2,1)}, bf16[128,512]{1...) custom-call(f32[1024,512]{1,0:T(8,128)} %shard_map.165.own, ...), custom_call_target="tpu_custom_call" | custom-call | flops 2000000000 | bytes 10628096 | tf_op jit(solution)/shard_map/pallas_call | solution.py:140
  26.6 8.3 %all-to-all-start = ((bf16[128,16,128]{2,1,0:T(8,128)(2,1)}), bf16[128,16,128]{2,1,0:T(8,128)(2,1)}, u32[]{:S(2)}, u32[]{:S(2)}) async-start(bf16[128,16,128]{2,1,0:T(8,128)(2,1)} %bitcast.21), calls=%async_computation | async-start | bytes 1048576 | tf_op jit(solution)/shard_map/all_to_all | solution.py:450
  36.4 4.3 %collective-permute-start.5 = (bf16[64,512]{1,0:T(8,128)(2,1)}, bf16[64,512]{1,0:T(8,128)(2,1)}, u32[]{:S(2)}, u32[]{:S(2)}) collective-permute-start(bf16[64,512]{1,0:T(8,128)(2,1)} %get-tuple-element.68), channel_id=1, source_target_pairs={{0,15},{1,0},{2,1},{3,2},{4,3},{5,4},{6,5},{7,6},{8,7},{9,8},{10,9... | collective-permute-start | bytes 196616 | tf_op jit(solution)/shard_map/ppermute | solution.py:25
  42.5 5.0 %shard_map.167 = (f32[1024,512]{1,0:T(8,128)}, f32[128,512]{1,0:T(8,128)}) custom-call(bf16[128,512]{1,0:T(8,128)(2,1)} %get-tuple-element.64.middle, bf16[128,512]{1,0:T(8,128)(2,1)} %get-tuple-element.65.sender, bf16[1024,512]{1,0:T(8,128)(2,1)} %edge.3, s32[8,128]{1,0:T(8,128)} %bitcast.32, s32[8,128]{1,0:T(8,128)} %bitcast.34, bf16[10,512,512]{2,1,0:T(8,128)(2,1)} %w0.3, ...), custom_call_target="tpu_custom_call" | custom-call | flops 2000000000 | bytes 5251072 | tf_op jit(solution)/shard_map/pallas_call | solution.py:140
  48.3 11.9 %shard_map.168 = (bf16[128,512]{1,0:T(8,128)(2,1)}, bf16[1024,512]{1,0:T(8,128)(2,1)}, bf16[128,512]{1,0:T(8,128)(2,1)}, bf16[128,512]{1,0:T(8,128)(2,1)}, bf16[...) custom-call(f32[1024,512]{1,0:T(8,128)} %get-tuple-element.66.own, ...), custom_call_target="tpu_custom_call" | custom-call | flops 8000000000 | bytes 11018240 | tf_op jit(solution)/shard_map/pallas_call | solution.py:140
  60.2 8.3 %shard_map.169 = (bf16[1024,512]{1,0:T(8,128)(2,1)}, f32[128,512]{1,0:T(8,128)}, bf16[32,2,6,16,128]{4,3,2,1,0:T(8,128)(2,1)}, bf16[32,2,6,16,128]{4,3,2,1,0:T(8,128)(2,1)}) custom-call(s32[1]{0:T(128)} %bitcast.8.core, bf16[1024,512]{1,0:T(8,128)(2,1)} %edge.3, bf16[1024,512]{1,0:T(8,128)(2,1)} %get-tuple-element.80.cround, ...), custom_call_target="tpu_custom_call" | custom-call | flops 3000000000 | bytes 12189700 | tf_op jit(solution)/shard_map/pallas_call | solution.py:140
  69.8 4.7 %all-to-all-start.1 = ((bf16[128,16,128]{2,1,0:T(8,128)(2,1)}), bf16[128,16,128]{2,1,0:T(8,128)(2,1)}, u32[]{:S(2)}, u32[]{:S(2)}) async-start(bf16[128,16,128]{2,1,0:T(8,128)(2,1)} %bitcast.20), calls=%async_computation.1 | async-start | bytes 1048576 | tf_op jit(solution)/shard_map/all_to_all | solution.py:471
  74.4 5.6 %collective-permute-start.8 = (bf16[64,512]{1,0:T(8,128)(2,1)}, bf16[64,512]{1,0:T(8,128)(2,1)}, u32[]{:S(2)}, u32[]{:S(2)}) collective-permute-start(bf16[64,512]{1,0:T(8,128)(2,1)} %get-tuple-element.74), channel_id=1, source_target_pairs={{0,15},{1,0},{2,1},{3,2},{4,3},{5,4},{6,5},{7,6},{8,7},{9,8},{10,9... | collective-permute-start | bytes 196616 | tf_op jit(solution)/shard_map/ppermute | solution.py:25
  83.7 4.0 %collective-permute-done.9.in1 = bf16[64,512]{1,0:T(8,128)(2,1)} collective-permute-done((bf16[64,512]{1,0:T(8,128)(2,1)}, bf16[64,512]{1,0:T(8,128)(2,1)}, u32[]{:S(2)}, u32[]{:S(2)}) %collective-permute-start.9) | collective-permute-done | bytes 65568 | tf_op jit(solution)/shard_map/ppermute | solution.py:25
  88.0 28.4 %all_to_all.30.terms = bf16[64,96,128]{2,1,0:T(8,128)(2,1)} all-to-all(bf16[64,96,128]{2,1,0:T(8,128)(2,1)S(1)} %bitcast.18), channel_id=1, replica_groups=mesh['x'=4,'core'=2,'y'=4,'z'=4] {'x','y','z'}, dimensions={0} | all-to-all | bytes 3145728 | tf_op jit(solution)/shard_map/all_to_all | solution.py:487
  119.3 6.7 %all-to-all-start.3 = ((bf16[64,96,128]{2,1,0:T(8,128)(2,1)}), bf16[64,96,128]{2,1,0:T(8,128)(2,1)}, u32[]{:S(2)}, u32[]{:S(2)}) async-start(bf16[64,96,128]{2,1,0:T(8,128)(2,1)} %shard_map.174), calls=%async_computation.3 | async-start | bytes 3145728 | tf_op jit(solution)/shard_map/all_to_all | solution.py:502
  126.0 8.1 %shard_map.170 = (bf16[128,512]{1,0:T(8,128)(2,1)}, f32[128,512]{1,0:T(8,128)}, bf16[1024,512]{1,0:T(8,128)(2,1)}, bf16[1024,512]{1,0:T(8,128)(2,1)}, bf16[256,5...) custom-call(bf16[64,512]{1,0:T(8,128)(2,1)} %collective-permute-done.8.in0, ...), custom_call_target="tpu_custom_call" | custom-call | flops 4000000000 | bytes 10103808 | tf_op jit(solution)/shard_map/pallas_call | solution.py:140
  134.1 5.4 %shard_map.171 = (f32[512,512]{1,0:T(8,128)}, bf16[128,512]{1,0:T(8,128)(2,1)}, bf16[32,2,3,16,128]{4,3,2,1,0:T(8,128)(2,1)}, bf16[32,2,3,16,128]{4,3,2,1,0:T(8,128)(2,1)}) custom-call(s32[1]{0:T(128)} %bitcast.8.core, bf16[1024,512]{1,0:T(8,128)(2,1)} %get-tuple-element.91.upper, s32[8,128]{1,0:T(8,128)} %bitcast.25, s32[8,128]{1,0:T(8,128)} %bitcast.29, ...), custom_call_target="tpu_custom_call" | custom-call | flops 2000000000 | bytes 7086084 | tf_op jit(solution)/shard_map/pallas_call | solution.py:140
  141.6 4.3 %collective-permute-start.12 = (bf16[256,512]{1,0:T(8,128)(2,1)}, bf16[256,512]{1,0:T(8,128)(2,1)}, u32[]{:S(2)}, u32[]{:S(2)}) collective-permute-start(bf16[256,512]{1,0:T(8,128)(2,1)} %get-tuple-element.97), channel_id=1, source_target_pairs={{0,15},{1,0},{2,1},{3,2},{4,3},{5,4},{6,5},{7,6},{8,7},{9,8},{10,9... | collective-permute-start | bytes 786440 | tf_op jit(solution)/shard_map/ppermute | solution.py:25
  147.7 5.1 %collective-permute-done.12.in0 = bf16[256,512]{1,0:T(8,128)(2,1)} collective-permute-done((bf16[256,512]{1,0:T(8,128)(2,1)}, bf16[256,512]{1,0:T(8,128)(2,1)}, u32[]{:S(2)}, u32[]{:S(2)}) %collective-permute-start.12) | collective-permute-done | bytes 262176 | tf_op jit(solution)/shard_map/ppermute | solution.py:25
  152.8 4.2 %collective-permute-done.13.in1 = bf16[256,512]{1,0:T(8,128)(2,1)} collective-permute-done((bf16[256,512]{1,0:T(8,128)(2,1)}, bf16[256,512]{1,0:T(8,128)(2,1)}, u32[]{:S(2)}, u32[]{:S(2)}) %collective-permute-start.13) | collective-permute-done | bytes 262176 | tf_op jit(solution)/shard_map/ppermute | solution.py:25
  157.1 4.1 %shard_map.172 = (bf16[512,512]{1,0:T(8,128)(2,1)}, bf16[32,2,1,16,128]{4,3,2,1,0:T(8,128)(2,1)}, bf16[32,2,1,16,128]{4,3,2,1,0:T(8,128)(2,1)}) custom-call(s32[1]{0:T(128)} %bitcast.8.core, f32[512,512]{1,0:T(8,128)} %get-tuple-element.96.grid_own, bf16[256,512]{1,0:T(8,128)(2,1)} %collective-permute-done.12.in0, ...), custom_call_target="tpu_custom_call" | custom-call | flops 1000000000 | bytes 4198404 | tf_op jit(solution)/shard_map/pallas_call | solution.py:140
  166.7 22.4 %all_to_all.31.terms = bf16[64,64,128]{2,1,0:T(8,128)(2,1)} all-to-all(bf16[64,64,128]{2,1,0:T(8,128)(2,1)} %bitcast.19), channel_id=1, replica_groups=mesh['x'=4,'core'=2,'y'=4,'z'=4] {'x','y','z'}, dimensions={0} | all-to-all | bytes 2097152 | tf_op jit(solution)/shard_map/all_to_all | solution.py:513
  191.5 5.6 %all-to-all-start.5 = ((bf16[64,64,128]{2,1,0:T(8,128)(2,1)}), bf16[64,64,128]{2,1,0:T(8,128)(2,1)}, u32[]{:S(2)}, u32[]{:S(2)}) async-start(bf16[64,64,128]{2,1,0:T(8,128)(2,1)} %shard_map.175), calls=%async_computation.5 | async-start | bytes 2097152 | tf_op jit(solution)/shard_map/all_to_all | solution.py:529
  199.6 13.4 %all-to-all-done.5 = bf16[64,64,128]{2,1,0:T(8,128)(2,1)} async-done(((bf16[64,64,128]{2,1,0:T(8,128)(2,1)}), bf16[64,64,128]{2,1,0:T(8,128)(2,1)}, u32[]{:S(2)}, u32[]{:S(2)}) %all-to-all-start.5) | async-done | bytes 1048608 | tf_op jit(solution)/shard_map/all_to_all | solution.py:529
  216.5 5.4 %place_early.1.kept = bf16[10,512,512]{2,1,0:T(8,128)(2,1)} custom-call(s32[1]{0:T(128)} %bitcast.8.core, bf16[32,2,6,16,128]{4,3,2,1,0:T(8,128)(2,1)} %bitcast.16.own, bf16[32,2,6,16,128]{4,3,2,1,0:T(8,128)(2,1)} %bitcast.17.other), custom_call_target="tpu_custom_call" | custom-call | tf_op jit(solution)/shard_map/place_early/pallas_call | solution.py:516
  221.9 3.9 %place_late.1 = bf16[10,512,512]{2,1,0:T(8,128)(2,1)} custom-call(s32[1]{0:T(128)} %bitcast.8.core, bf16[32,2,4,16,128]{4,3,2,1,0:T(8,128)(2,1)} %bitcast.14.own, bf16[32,2,4,16,128]{4,3,2,1,0:T(8,128)(2,1)} %bitcast.15.other, bf16[10,512,512]{2,1,0:T(8,128)(2,1)} %place_early.1.kept), custom_call_target="tpu_custom_call", output_to_operand_aliasing={{}: (3, {})} | custom-call | tf_op jit(solution)/shard_map/place_late/pallas_call | solution.py:532
  (46 shorter events, 39.4 us)
Async XLA Ops:
  3.6 13.8 %collective-permute-start = (bf16[256,512]{1,0:T(8,128)(2,1)}, bf16[256,512]{1,0:T(8,128)(2,1)}, u32[]{:S(2)}, u32[]{:S(2)}) collective-permute-start(bf16[256,512]{1,0:T(8,128)(2,1)} %get-tuple-element.60), channel_id=1, source_target_pairs={{0,1},{1,2},{2,3},{3,4},{4,5},{5,6},{6,7},{7,8},{8,9},{9,10},{10,1... | collective-permute-start | bytes 786440 | tf_op jit(solution)/shard_map/ppermute | solution.py:25
  6.1 11.4 %collective-permute-start.1 = (bf16[256,512]{1,0:T(8,128)(2,1)}, bf16[256,512]{1,0:T(8,128)(2,1)}, u32[]{:S(2)}, u32[]{:S(2)}) collective-permute-start(bf16[256,512]{1,0:T(8,128)(2,1)} %get-tuple-element.61), channel_id=1, source_target_pairs={{0,15},{1,0},{2,1},{3,2},{4,3},{5,4},{6,5},{7,6},{8,7},{9,8},{10,9... | collective-permute-start | bytes 786440 | tf_op jit(solution)/shard_map/ppermute | solution.py:25
  10.6 6.8 %collective-permute-start.2 = (bf16[256,512]{1,0:T(8,128)(2,1)}, bf16[256,512]{1,0:T(8,128)(2,1)}, u32[]{:S(2)}, u32[]{:S(2)}) collective-permute-start(bf16[256,512]{1,0:T(8,128)(2,1)} %get-tuple-element.62), channel_id=1, source_target_pairs={{0,16},{16,32},{32,48},{48,64},{64,80},{80,96},{96,112},{112,0},{1... | collective-permute-start | bytes 786440 | tf_op jit(solution)/shard_map/ppermute | solution.py:25
  12.7 6.1 %collective-permute-start.3 = (bf16[256,512]{1,0:T(8,128)(2,1)}, bf16[256,512]{1,0:T(8,128)(2,1)}, u32[]{:S(2)}, u32[]{:S(2)}) collective-permute-start(bf16[256,512]{1,0:T(8,128)(2,1)} %get-tuple-element.63), channel_id=1, source_target_pairs={{0,112},{16,0},{32,16},{48,32},{64,48},{80,64},{96,80},{112,96},{1... | collective-permute-start | bytes 786440 | tf_op jit(solution)/shard_map/ppermute | solution.py:25
  26.6 21.7 %all-to-all-start = ((bf16[128,16,128]{2,1,0:T(8,128)(2,1)}), bf16[128,16,128]{2,1,0:T(8,128)(2,1)}, u32[]{:S(2)}, u32[]{:S(2)}) async-start(bf16[128,16,128]{2,1,0:T(8,128)(2,1)} %bitcast.21), calls=%async_computation | async-start | bytes 1048576 | tf_op jit(solution)/shard_map/all_to_all | solution.py:450
  34.9 12.6 %collective-permute-start.4 = (bf16[64,512]{1,0:T(8,128)(2,1)}, bf16[64,512]{1,0:T(8,128)(2,1)}, u32[]{:S(2)}, u32[]{:S(2)}) collective-permute-start(bf16[64,512]{1,0:T(8,128)(2,1)} %get-tuple-element.67), channel_id=1, source_target_pairs={{0,1},{1,2},{2,3},{3,4},{4,5},{5,6},{6,7},{7,8},{8,9},{9,10},{10,1... | collective-permute-start | bytes 196616 | tf_op jit(solution)/shard_map/ppermute | solution.py:25
  36.4 11.1 %collective-permute-start.5 = (bf16[64,512]{1,0:T(8,128)(2,1)}, bf16[64,512]{1,0:T(8,128)(2,1)}, u32[]{:S(2)}, u32[]{:S(2)}) collective-permute-start(bf16[64,512]{1,0:T(8,128)(2,1)} %get-tuple-element.68), channel_id=1, source_target_pairs={{0,15},{1,0},{2,1},{3,2},{4,3},{5,4},{6,5},{7,6},{8,7},{9,8},{10,9... | collective-permute-start | bytes 196616 | tf_op jit(solution)/shard_map/ppermute | solution.py:25
  40.7 6.7 %collective-permute-start.6 = (bf16[64,512]{1,0:T(8,128)(2,1)}, bf16[64,512]{1,0:T(8,128)(2,1)}, u32[]{:S(2)}, u32[]{:S(2)}) collective-permute-start(bf16[64,512]{1,0:T(8,128)(2,1)} %get-tuple-element.69), channel_id=1, source_target_pairs={{0,16},{16,32},{32,48},{48,64},{64,80},{80,96},{96,112},{112,0},{1... | collective-permute-start | bytes 196616 | tf_op jit(solution)/shard_map/ppermute | solution.py:25
  42.5 5.0 %collective-permute-start.7 = (bf16[64,512]{1,0:T(8,128)(2,1)}, bf16[64,512]{1,0:T(8,128)(2,1)}, u32[]{:S(2)}, u32[]{:S(2)}) collective-permute-start(bf16[64,512]{1,0:T(8,128)(2,1)} %get-tuple-element.70), channel_id=1, source_target_pairs={{0,112},{16,0},{32,16},{48,32},{64,48},{80,64},{96,80},{112,96},{1... | collective-permute-start | bytes 196616 | tf_op jit(solution)/shard_map/ppermute | solution.py:25
  68.5 13.3 %collective-permute-start.18 = (bf16[32,2,6,16,128]{4,3,2,1,0:T(8,128)(2,1)}, bf16[32,2,6,16,128]{4,3,2,1,0:T(8,128)(2,1)S(1)}, u32[]{:S(2)}, u32[]{:S(2)}) collective-permute-start(bf16[32,2,6,16,128]{4,3,2,1,0:T(8,128)(2,1)} %get-tuple-element.109), channel_id=1, source_target_pairs={{0,16},{16,0},{1,17},{17,1},{2,18},{18,2},{3,19},{19,3},{4,20},{20... | collective-permute-start | bytes 4718600 | tf_op jit(solution)/shard_map/ppermute | solution.py:409
  69.8 18.3 %all-to-all-start.1 = ((bf16[128,16,128]{2,1,0:T(8,128)(2,1)}), bf16[128,16,128]{2,1,0:T(8,128)(2,1)}, u32[]{:S(2)}, u32[]{:S(2)}) async-start(bf16[128,16,128]{2,1,0:T(8,128)(2,1)} %bitcast.20), calls=%async_computation.1 | async-start | bytes 1048576 | tf_op jit(solution)/shard_map/all_to_all | solution.py:471
  74.4 9.3 %collective-permute-start.8 = (bf16[64,512]{1,0:T(8,128)(2,1)}, bf16[64,512]{1,0:T(8,128)(2,1)}, u32[]{:S(2)}, u32[]{:S(2)}) collective-permute-start(bf16[64,512]{1,0:T(8,128)(2,1)} %get-tuple-element.74), channel_id=1, source_target_pairs={{0,15},{1,0},{2,1},{3,2},{4,3},{5,4},{6,5},{7,6},{8,7},{9,8},{10,9... | collective-permute-start | bytes 196616 | tf_op jit(solution)/shard_map/ppermute | solution.py:25
  80.0 7.8 %collective-permute-start.9 = (bf16[64,512]{1,0:T(8,128)(2,1)}, bf16[64,512]{1,0:T(8,128)(2,1)}, u32[]{:S(2)}, u32[]{:S(2)}) collective-permute-start(bf16[64,512]{1,0:T(8,128)(2,1)} %get-tuple-element.75), channel_id=1, source_target_pairs={{0,1},{1,2},{2,3},{3,4},{4,5},{5,6},{6,7},{7,8},{8,9},{9,10},{10,1... | collective-permute-start | bytes 196616 | tf_op jit(solution)/shard_map/ppermute | solution.py:25
  80.0 7.8 %collective-permute-start.10 = (bf16[64,512]{1,0:T(8,128)(2,1)}, bf16[64,512]{1,0:T(8,128)(2,1)}, u32[]{:S(2)}, u32[]{:S(2)}) collective-permute-start(bf16[64,512]{1,0:T(8,128)(2,1)} %get-tuple-element.76), channel_id=1, source_target_pairs={{0,112},{16,0},{32,16},{48,32},{64,48},{80,64},{96,80},{112,96},{1... | collective-permute-start | bytes 196616 | tf_op jit(solution)/shard_map/ppermute | solution.py:25
  80.7 7.1 %collective-permute-start.11 = (bf16[64,512]{1,0:T(8,128)(2,1)}, bf16[64,512]{1,0:T(8,128)(2,1)}, u32[]{:S(2)}, u32[]{:S(2)}) collective-permute-start(bf16[64,512]{1,0:T(8,128)(2,1)} %get-tuple-element.77), channel_id=1, source_target_pairs={{0,16},{16,32},{32,48},{48,64},{64,80},{80,96},{96,112},{112,0},{1... | collective-permute-start | bytes 196616 | tf_op jit(solution)/shard_map/ppermute | solution.py:25
  119.3 47.4 %all-to-all-start.3 = ((bf16[64,96,128]{2,1,0:T(8,128)(2,1)}), bf16[64,96,128]{2,1,0:T(8,128)(2,1)}, u32[]{:S(2)}, u32[]{:S(2)}) async-start(bf16[64,96,128]{2,1,0:T(8,128)(2,1)} %shard_map.174), calls=%async_computation.3 | async-start | bytes 3145728 | tf_op jit(solution)/shard_map/all_to_all | solution.py:502
  139.5 24.4 %collective-permute-start.17 = (bf16[32,2,3,16,128]{4,3,2,1,0:T(8,128)(2,1)}, bf16[32,2,3,16,128]{4,3,2,1,0:T(8,128)(2,1)}, u32[]{:S(2)}, u32[]{:S(2)}) collective-permute-start(bf16[32,2,3,16,128]{4,3,2,1,0:T(8,128)(2,1)} %get-tuple-element.107), channel_id=1, source_target_pairs={{0,16},{16,0},{1,17},{17,1},{2,18},{18,2},{3,19},{19,3},{4,20},{20... | collective-permute-start | bytes 2359304 | tf_op jit(solution)/shard_map/ppermute | solution.py:409
  141.6 11.2 %collective-permute-start.12 = (bf16[256,512]{1,0:T(8,128)(2,1)}, bf16[256,512]{1,0:T(8,128)(2,1)}, u32[]{:S(2)}, u32[]{:S(2)}) collective-permute-start(bf16[256,512]{1,0:T(8,128)(2,1)} %get-tuple-element.97), channel_id=1, source_target_pairs={{0,15},{1,0},{2,1},{3,2},{4,3},{5,4},{6,5},{7,6},{8,7},{9,8},{10,9... | collective-permute-start | bytes 786440 | tf_op jit(solution)/shard_map/ppermute | solution.py:25
  145.9 11.1 %collective-permute-start.13 = (bf16[256,512]{1,0:T(8,128)(2,1)}, bf16[256,512]{1,0:T(8,128)(2,1)}, u32[]{:S(2)}, u32[]{:S(2)}) collective-permute-start(bf16[256,512]{1,0:T(8,128)(2,1)} %get-tuple-element.98), channel_id=1, source_target_pairs={{0,1},{1,2},{2,3},{3,4},{4,5},{5,6},{6,7},{7,8},{8,9},{9,10},{10,1... | collective-permute-start | bytes 786440 | tf_op jit(solution)/shard_map/ppermute | solution.py:25
  145.9 11.1 %collective-permute-start.14 = (bf16[256,512]{1,0:T(8,128)(2,1)}, bf16[256,512]{1,0:T(8,128)(2,1)}, u32[]{:S(2)}, u32[]{:S(2)}) collective-permute-start(bf16[256,512]{1,0:T(8,128)(2,1)} %get-tuple-element.99), channel_id=1, source_target_pairs={{0,112},{16,0},{32,16},{48,32},{64,48},{80,64},{96,80},{112,96},{1... | collective-permute-start | bytes 786440 | tf_op jit(solution)/shard_map/ppermute | solution.py:25
  146.3 10.8 %collective-permute-start.15 = (bf16[256,512]{1,0:T(8,128)(2,1)}, bf16[256,512]{1,0:T(8,128)(2,1)}, u32[]{:S(2)}, u32[]{:S(2)}) collective-permute-start(bf16[256,512]{1,0:T(8,128)(2,1)} %get-tuple-element.100), channel_id=1, source_target_pairs={{0,16},{16,32},{32,48},{48,64},{64,80},{80,96},{96,112},{112,0},{1... | collective-permute-start | bytes 786440 | tf_op jit(solution)/shard_map/ppermute | solution.py:25
  191.5 21.5 %all-to-all-start.5 = ((bf16[64,64,128]{2,1,0:T(8,128)(2,1)}), bf16[64,64,128]{2,1,0:T(8,128)(2,1)}, u32[]{:S(2)}, u32[]{:S(2)}) async-start(bf16[64,64,128]{2,1,0:T(8,128)(2,1)} %shard_map.175), calls=%async_computation.5 | async-start | bytes 2097152 | tf_op jit(solution)/shard_map/all_to_all | solution.py:529
  197.1 19.3 %collective-permute-start.20 = (bf16[64,96,128]{2,1,0:T(8,128)(2,1)}, bf16[64,96,128]{2,1,0:T(8,128)(2,1)}, u32[]{:S(2)}, u32[]{:S(2)}) collective-permute-start(bf16[64,96,128]{2,1,0:T(8,128)(2,1)} %all-to-all-done.3), channel_id=1, source_target_pairs={{0,16},{16,0},{1,17},{17,1},{2,18},{18,2},{3,19},{19,3},{4,20},{20... | collective-permute-start | bytes 4718600 | tf_op jit(solution)/shard_map/ppermute | solution.py:409
  213.0 8.9 %collective-permute-start.19 = (bf16[64,64,128]{2,1,0:T(8,128)(2,1)}, bf16[64,64,128]{2,1,0:T(8,128)(2,1)}, u32[]{:S(2)}, u32[]{:S(2)}) collective-permute-start(bf16[64,64,128]{2,1,0:T(8,128)(2,1)} %all-to-all-done.5), channel_id=1, source_target_pairs={{0,16},{16,0},{1,17},{17,1},{2,18},{18,2},{3,19},{19,3},{4,20},{20... | collective-permute-start | bytes 3145736 | tf_op jit(solution)/shard_map/ppermute | solution.py:409
  (2 other events, 14.8 us)

commit v4 on v3

--- a/solution.py
+++ b/solution.py
@@ -300,12 +300,15 @@
 
 
 def process_grads_body(
-    scales, core, edge, cround, hidden, plinear, middle, receive, cot_update, rounded, uhidden, cot_linear, edge_cot, mesh_cot,
-    w3, w5, w7, edge_grad, middle_part, grads_own, grads_other, held,
+    scales, core, edge, cround, hidden, plinear, middle, receive, cot_update, rounded, uhidden, cot_linear,
+    grads_own, grads_other, held,
 ):
     pairs = ((edge, cround), (middle, receive), (hidden, plinear), (middle, cot_update), (rounded, cot_update), (uhidden, cot_linear))
     for k, (x, y) in enumerate(pairs):
         store_blocks(grads_own, grads_other, k, dot_tn(x[...], y[...]) * scales[k], held, core)
+
+
+def edge_back_body(cround, edge_cot, receive, cot_update, mesh_cot, w3, w5, w7, edge_grad, middle_part):
     middle_part[...] = mesh_cot[...].astype(f32) + dot_nt(cot_update[...], w7[...]) + dot_nt(receive[...], w5[...])
 
     def step(i, s):
@@ -475,14 +478,18 @@
         return ((32, 2, count, 16, 128), bf16)
 
     held = vm((latent, latent), bf16)
-    edge_grad, middle_part, early_own, early_other = call(
+    early_own, early_other = call(
         scaled(process_grads_body, [edge_scale] * 3 + [node_scale] * 3),
-        [(big, bf16), (small, f32), blocks(6), blocks(6)],
-        (core, edge_latent, cround, phidden, plinear, middle, receive, cot_update, rounded, uhidden, cot_linear,
-         edge_cotangent, mesh_cotangent),
-        weights, (3, 5, 7), scratch=(held,), flops=3 * 10**9,
-    )
-    early = (early_own.astype(f32) + swapped(early_other).astype(f32)).astype(bf16)
+        [blocks(6), blocks(6)],
+        (core, edge_latent, cround, phidden, plinear, middle, receive, cot_update, rounded, uhidden, cot_linear),
+        scratch=(held,), flops=2 * 10**9,
+    )
+    early_other = swapped(early_other)
+    edge_grad, middle_part = call(
+        edge_back_body, [(big, bf16), (small, f32)], (cround, edge_cotangent, receive, cot_update, mesh_cotangent),
+        weights, (3, 5, 7),
+    )
+    early = (early_own.astype(f32) + early_other.astype(f32)).astype(bf16)
     early, _ = lax.optimization_barrier((early, (halo_back, far_back)))
     early = lax.all_to_all(early.reshape(64, 96, 128), CHIPS, 0, 0, tiled=True)
     cot_sender, cot_middle, elinear, upper, *partials = call(
@@ -540,7 +547,7 @@
         ),
         out_shape=jax.ShapeDtypeStruct(weights.shape, bf16),
         input_output_aliases={3: 0},
-        compiler_params=pltpu.CompilerParams(vmem_limit_bytes=67000000),
+        compiler_params=pltpu.CompilerParams(vmem_limit_bytes=12 << 20),
         name="place_late",
     )(core, late, other, placed)
     return (mesh_update, grid_grad, mesh_grad, edge_grad, weight_grads)

time: 227 us -> 229 us (level)
  Pallas kernels: 75 us -> 77.5 us
    pallas_call x12 -> x13, Pallas kernels: 65.7 us -> 68.2 us  [call(): pl.pallas_call(body, grid=(1,), out_shape=shapes, in_specs=in_specs, out_...]
  transfers between devices with their start and end apart: 25 -> 25, of which waited for: 8 -> 7; matrix products, arithmetic and copies ran while one was open for 1% -> 1% of each run, Pallas kernels for 15% -> 17%
where the time goes in v4:
time: 229 us; the launch traced here: 228 us
  Pallas kernels  77.5 us (34%)
  starting transfers between devices  66.4 us (29%)
  blocking collectives  49.5 us (22%)
  waiting for transfers between devices  31.3 us (14%)
    pallas_call x13, Pallas kernels, call(): pl.pallas_call(body, grid=(1,), out_shape=shapes, in_specs=in_specs, out_...  68.2 us
    ppermute x16, starting transfers between devices, shifted(): return lax.ppermute(value, axis, pairs)  30 us
    all_to_all x1, blocking collectives, on_device(): early = lax.all_to_all(early.reshape(64, 96, 128), CHIPS, 0, 0, tiled=True)  27.2 us
    all_to_all x1, blocking collectives, on_device(): late = lax.all_to_all(late.reshape(64, 64, 128), CHIPS, 0, 0, tiled=True)  22.4 us
    ppermute x16, waiting for transfers between devices, shifted(): return lax.ppermute(value, axis, pairs)  15.7 us
    all_to_all x1, waiting for transfers between devices, on_device(): late = lax.all_to_all(late, CHIPS, 0, 0, tiled=True)  13.4 us
    all_to_all x2, starting transfers between devices, on_device(): lax.all_to_all(far_out.reshape(peers, 16, 128), AXES, 0, 0, tiled=True)  12.9 us
    ppermute x5, starting transfers between devices, swapped(): return lax.ppermute(value, 'core', [(0, 1), (1, 0)])  10.6 us
  transfers between devices with their start and end apart: 25, of which 7 were waited for; matrix products, arithmetic and copies ran while one was open for 1% of the time, Pallas kernels for 17%

profile of v4, /device:TPU:1, one launch (start us, length us, event | category | flops | bytes accessed | tf_op | source)
XLA Modules:
  0.0 228.2 jit_solution(5921939605933660354)
XLA Ops:
  6.1 4.6 %collective-permute-start.1 = (bf16[256,512]{1,0:T(8,128)(2,1)}, bf16[256,512]{1,0:T(8,128)(2,1)}, u32[]{:S(2)}, u32[]{:S(2)}) collective-permute-start(bf16[256,512]{1,0:T(8,128)(2,1)} %get-tuple-element.61), channel_id=1, source_target_pairs={{0,15},{1,0},{2,1},{3,2},{4,3},{5,4},{6,5},{7,6},{8,7},{9,8},{10,9... | collective-permute-start | bytes 786440 | tf_op jit(solution)/shard_map/ppermute | solution.py:25
  13.4 4.1 %shard_map.165.own = f32[1024,512]{1,0:T(8,128)} custom-call(bf16[512,512]{1,0:T(8,128)(2,1)} %get-tuple-element.59.project, s32[8,128]{1,0:T(8,128)} %bitcast.22, s32[8,128]{1,0:T(8,128)} %bitcast.26, bf16[128,512]{1,0:T(8,128)(2,1)} %mesh.5, bf16[10,512,512]{2,1,0:T(8,128)(2,1)} %w0.3), custom_call_target="tpu_custom_call" | custom-call | flops 1000000000 | bytes 3284992 | tf_op jit(solution)/shard_map/pallas_call | solution.py:140
  18.8 7.8 %shard_map.166 = (f32[1024,512]{1,0:T(8,128)}, f32[1024,512]{1,0:T(8,128)}, bf16[1024,512]{1,0:T(8,128)(2,1)}, bf16[128,512]{1,0:T(8,128)(2,1)}, bf16[128,512]{1...) custom-call(f32[1024,512]{1,0:T(8,128)} %shard_map.165.own, ...), custom_call_target="tpu_custom_call" | custom-call | flops 2000000000 | bytes 10628096 | tf_op jit(solution)/shard_map/pallas_call | solution.py:140
  26.6 8.3 %all-to-all-start = ((bf16[128,16,128]{2,1,0:T(8,128)(2,1)}), bf16[128,16,128]{2,1,0:T(8,128)(2,1)}, u32[]{:S(2)}, u32[]{:S(2)}) async-start(bf16[128,16,128]{2,1,0:T(8,128)(2,1)} %bitcast.21), calls=%async_computation | async-start | bytes 1048576 | tf_op jit(solution)/shard_map/all_to_all | solution.py:453
  36.4 4.3 %collective-permute-start.5 = (bf16[64,512]{1,0:T(8,128)(2,1)}, bf16[64,512]{1,0:T(8,128)(2,1)}, u32[]{:S(2)}, u32[]{:S(2)}) collective-permute-start(bf16[64,512]{1,0:T(8,128)(2,1)} %get-tuple-element.68), channel_id=1, source_target_pairs={{0,15},{1,0},{2,1},{3,2},{4,3},{5,4},{6,5},{7,6},{8,7},{9,8},{10,9... | collective-permute-start | bytes 196616 | tf_op jit(solution)/shard_map/ppermute | solution.py:25
  42.5 5.0 %shard_map.167 = (f32[1024,512]{1,0:T(8,128)}, f32[128,512]{1,0:T(8,128)}) custom-call(bf16[128,512]{1,0:T(8,128)(2,1)} %get-tuple-element.64.middle, bf16[128,512]{1,0:T(8,128)(2,1)} %get-tuple-element.65.sender, bf16[1024,512]{1,0:T(8,128)(2,1)} %edge.3, s32[8,128]{1,0:T(8,128)} %bitcast.32, s32[8,128]{1,0:T(8,128)} %bitcast.34, bf16[10,512,512]{2,1,0:T(8,128)(2,1)} %w0.3, ...), custom_call_target="tpu_custom_call" | custom-call | flops 2000000000 | bytes 5251072 | tf_op jit(solution)/shard_map/pallas_call | solution.py:140
  48.3 11.9 %shard_map.168 = (bf16[128,512]{1,0:T(8,128)(2,1)}, bf16[1024,512]{1,0:T(8,128)(2,1)}, bf16[128,512]{1,0:T(8,128)(2,1)}, bf16[128,512]{1,0:T(8,128)(2,1)}, bf16[...) custom-call(f32[1024,512]{1,0:T(8,128)} %get-tuple-element.66.own, ...), custom_call_target="tpu_custom_call" | custom-call | flops 8000000000 | bytes 11018240 | tf_op jit(solution)/shard_map/pallas_call | solution.py:140
  60.2 6.2 %shard_map.174 = (bf16[32,2,6,16,128]{4,3,2,1,0:T(8,128)(2,1)}, bf16[32,2,6,16,128]{4,3,2,1,0:T(8,128)(2,1)}) custom-call(s32[1]{0:T(128)} %bitcast.8.core, bf16[1024,512]{1,0:T(8,128)(2,1)} %edge.3, bf16[1024,512]{1,0:T(8,128)(2,1)} %get-tuple-element.80.cround, bf16[1024,512]{1,0:T(8,128)(2,1)} %get-tuple-element.103.hidden, ...), custom_call_target="tpu_custom_call" | custom-call | flops 2000000000 | bytes 8126468 | tf_op jit(solution)/shard_map/pallas_call | solution.py:140
  67.7 4.7 %all-to-all-start.1 = ((bf16[128,16,128]{2,1,0:T(8,128)(2,1)}), bf16[128,16,128]{2,1,0:T(8,128)(2,1)}, u32[]{:S(2)}, u32[]{:S(2)}) async-start(bf16[128,16,128]{2,1,0:T(8,128)(2,1)} %bitcast.20), calls=%async_computation.1 | async-start | bytes 1048576 | tf_op jit(solution)/shard_map/all_to_all | solution.py:474
  74.2 5.5 %collective-permute-start.8 = (bf16[64,512]{1,0:T(8,128)(2,1)}, bf16[64,512]{1,0:T(8,128)(2,1)}, u32[]{:S(2)}, u32[]{:S(2)}) collective-permute-start(bf16[64,512]{1,0:T(8,128)(2,1)} %get-tuple-element.74), channel_id=1, source_target_pairs={{0,15},{1,0},{2,1},{3,2},{4,3},{5,4},{6,5},{7,6},{8,7},{9,8},{10,9... | collective-permute-start | bytes 196616 | tf_op jit(solution)/shard_map/ppermute | solution.py:25
  81.7 5.0 %collective-permute-done.9.in1 = bf16[64,512]{1,0:T(8,128)(2,1)} collective-permute-done((bf16[64,512]{1,0:T(8,128)(2,1)}, bf16[64,512]{1,0:T(8,128)(2,1)}, u32[]{:S(2)}, u32[]{:S(2)}) %collective-permute-start.9) | collective-permute-done | bytes 65568 | tf_op jit(solution)/shard_map/ppermute | solution.py:25
  86.6 27.2 %all_to_all.30.terms = bf16[64,96,128]{2,1,0:T(8,128)(2,1)} all-to-all(bf16[64,96,128]{2,1,0:T(8,128)(2,1)S(1)} %bitcast.18), channel_id=1, replica_groups=mesh['x'=4,'core'=2,'y'=4,'z'=4] {'x','y','z'}, dimensions={0} | all-to-all | bytes 3145728 | tf_op jit(solution)/shard_map/all_to_all | solution.py:494
  116.7 7.2 %all-to-all-start.3 = ((bf16[64,96,128]{2,1,0:T(8,128)(2,1)}), bf16[64,96,128]{2,1,0:T(8,128)(2,1)}, u32[]{:S(2)}, u32[]{:S(2)}) async-start(bf16[64,96,128]{2,1,0:T(8,128)(2,1)} %shard_map.175), calls=%async_computation.3 | async-start | bytes 3145728 | tf_op jit(solution)/shard_map/all_to_all | solution.py:509
  123.8 4.5 %shard_map.169 = (bf16[1024,512]{1,0:T(8,128)(2,1)}, f32[128,512]{1,0:T(8,128)}) custom-call(bf16[1024,512]{1,0:T(8,128)(2,1)} %get-tuple-element.80.cround, bf16[1024,512]{1,0:T(8,128)(2,1)} %edge_cot.3, bf16[128,512]{1,0:T(8,128)(2,1)} %get-tuple-element.81.receive, bf16[128,512]{1,0:T(8,128)(2,1)} %get-tuple-element.82.cot_update, ...), custom_call_target="tpu_custom_call" | custom-call | flops 1000000000 | bytes 5373952 | tf_op jit(solution)/shard_map/pallas_call | solution.py:140
  128.3 8.1 %shard_map.170 = (bf16[128,512]{1,0:T(8,128)(2,1)}, f32[128,512]{1,0:T(8,128)}, bf16[1024,512]{1,0:T(8,128)(2,1)}, bf16[1024,512]{1,0:T(8,128)(2,1)}, bf16[256,5...) custom-call(bf16[64,512]{1,0:T(8,128)(2,1)} %collective-permute-done.8.in0, ...), custom_call_target="tpu_custom_call" | custom-call | flops 4000000000 | bytes 10103808 | tf_op jit(solution)/shard_map/pallas_call | solution.py:140
  136.5 5.4 %shard_map.171 = (f32[512,512]{1,0:T(8,128)}, bf16[128,512]{1,0:T(8,128)(2,1)}, bf16[32,2,3,16,128]{4,3,2,1,0:T(8,128)(2,1)}, bf16[32,2,3,16,128]{4,3,2,1,0:T(8,128)(2,1)}) custom-call(s32[1]{0:T(128)} %bitcast.8.core, bf16[1024,512]{1,0:T(8,128)(2,1)} %get-tuple-element.86.upper, s32[8,128]{1,0:T(8,128)} %bitcast.25, s32[8,128]{1,0:T(8,128)} %bitcast.29, ...), custom_call_target="tpu_custom_call" | custom-call | flops 2000000000 | bytes 7086084 | tf_op jit(solution)/shard_map/pallas_call | solution.py:140
  144.0 4.3 %collective-permute-start.12 = (bf16[256,512]{1,0:T(8,128)(2,1)}, bf16[256,512]{1,0:T(8,128)(2,1)}, u32[]{:S(2)}, u32[]{:S(2)}) collective-permute-start(bf16[256,512]{1,0:T(8,128)(2,1)} %get-tuple-element.92), channel_id=1, source_target_pairs={{0,15},{1,0},{2,1},{3,2},{4,3},{5,4},{6,5},{7,6},{8,7},{9,8},{10,9... | collective-permute-start | bytes 786440 | tf_op jit(solution)/shard_map/ppermute | solution.py:25
  150.1 4.1 %collective-permute-done.12.in0 = bf16[256,512]{1,0:T(8,128)(2,1)} collective-permute-done((bf16[256,512]{1,0:T(8,128)(2,1)}, bf16[256,512]{1,0:T(8,128)(2,1)}, u32[]{:S(2)}, u32[]{:S(2)}) %collective-permute-start.12) | collective-permute-done | bytes 262176 | tf_op jit(solution)/shard_map/ppermute | solution.py:25
  154.2 5.2 %collective-permute-done.13.in1 = bf16[256,512]{1,0:T(8,128)(2,1)} collective-permute-done((bf16[256,512]{1,0:T(8,128)(2,1)}, bf16[256,512]{1,0:T(8,128)(2,1)}, u32[]{:S(2)}, u32[]{:S(2)}) %collective-permute-start.13) | collective-permute-done | bytes 262176 | tf_op jit(solution)/shard_map/ppermute | solution.py:25
  159.5 4.1 %shard_map.172 = (bf16[512,512]{1,0:T(8,128)(2,1)}, bf16[32,2,1,16,128]{4,3,2,1,0:T(8,128)(2,1)}, bf16[32,2,1,16,128]{4,3,2,1,0:T(8,128)(2,1)}) custom-call(s32[1]{0:T(128)} %bitcast.8.core, f32[512,512]{1,0:T(8,128)} %get-tuple-element.91.grid_own, bf16[256,512]{1,0:T(8,128)(2,1)} %collective-permute-done.12.in0, ...), custom_call_target="tpu_custom_call" | custom-call | flops 1000000000 | bytes 4198404 | tf_op jit(solution)/shard_map/pallas_call | solution.py:140
  169.0 22.4 %all_to_all.31.terms = bf16[64,64,128]{2,1,0:T(8,128)(2,1)} all-to-all(bf16[64,64,128]{2,1,0:T(8,128)(2,1)} %bitcast.19), channel_id=1, replica_groups=mesh['x'=4,'core'=2,'y'=4,'z'=4] {'x','y','z'}, dimensions={0} | all-to-all | bytes 2097152 | tf_op jit(solution)/shard_map/all_to_all | solution.py:520
  193.9 5.7 %all-to-all-start.5 = ((bf16[64,64,128]{2,1,0:T(8,128)(2,1)}), bf16[64,64,128]{2,1,0:T(8,128)(2,1)}, u32[]{:S(2)}, u32[]{:S(2)}) async-start(bf16[64,64,128]{2,1,0:T(8,128)(2,1)} %shard_map.176), calls=%async_computation.5 | async-start | bytes 2097152 | tf_op jit(solution)/shard_map/all_to_all | solution.py:536
  202.0 13.4 %all-to-all-done.5 = bf16[64,64,128]{2,1,0:T(8,128)(2,1)} async-done(((bf16[64,64,128]{2,1,0:T(8,128)(2,1)}), bf16[64,64,128]{2,1,0:T(8,128)(2,1)}, u32[]{:S(2)}, u32[]{:S(2)}) %all-to-all-start.5) | async-done | bytes 1048608 | tf_op jit(solution)/shard_map/all_to_all | solution.py:536
  218.9 5.4 %place_early.1.kept = bf16[10,512,512]{2,1,0:T(8,128)(2,1)} custom-call(s32[1]{0:T(128)} %bitcast.8.core, bf16[32,2,6,16,128]{4,3,2,1,0:T(8,128)(2,1)} %bitcast.16.own, bf16[32,2,6,16,128]{4,3,2,1,0:T(8,128)(2,1)} %bitcast.17.other), custom_call_target="tpu_custom_call" | custom-call | tf_op jit(solution)/shard_map/place_early/pallas_call | solution.py:523
  (47 shorter events, 43.2 us)
Async XLA Ops:
  3.6 13.9 %collective-permute-start = (bf16[256,512]{1,0:T(8,128)(2,1)}, bf16[256,512]{1,0:T(8,128)(2,1)}, u32[]{:S(2)}, u32[]{:S(2)}) collective-permute-start(bf16[256,512]{1,0:T(8,128)(2,1)} %get-tuple-element.60), channel_id=1, source_target_pairs={{0,1},{1,2},{2,3},{3,4},{4,5},{5,6},{6,7},{7,8},{8,9},{9,10},{10,1... | collective-permute-start | bytes 786440 | tf_op jit(solution)/shard_map/ppermute | solution.py:25
  6.1 11.4 %collective-permute-start.1 = (bf16[256,512]{1,0:T(8,128)(2,1)}, bf16[256,512]{1,0:T(8,128)(2,1)}, u32[]{:S(2)}, u32[]{:S(2)}) collective-permute-start(bf16[256,512]{1,0:T(8,128)(2,1)} %get-tuple-element.61), channel_id=1, source_target_pairs={{0,15},{1,0},{2,1},{3,2},{4,3},{5,4},{6,5},{7,6},{8,7},{9,8},{10,9... | collective-permute-start | bytes 786440 | tf_op jit(solution)/shard_map/ppermute | solution.py:25
  10.7 6.9 %collective-permute-start.2 = (bf16[256,512]{1,0:T(8,128)(2,1)}, bf16[256,512]{1,0:T(8,128)(2,1)}, u32[]{:S(2)}, u32[]{:S(2)}) collective-permute-start(bf16[256,512]{1,0:T(8,128)(2,1)} %get-tuple-element.62), channel_id=1, source_target_pairs={{0,16},{16,32},{32,48},{48,64},{64,80},{80,96},{96,112},{112,0},{1... | collective-permute-start | bytes 786440 | tf_op jit(solution)/shard_map/ppermute | solution.py:25
  12.7 6.1 %collective-permute-start.3 = (bf16[256,512]{1,0:T(8,128)(2,1)}, bf16[256,512]{1,0:T(8,128)(2,1)}, u32[]{:S(2)}, u32[]{:S(2)}) collective-permute-start(bf16[256,512]{1,0:T(8,128)(2,1)} %get-tuple-element.63), channel_id=1, source_target_pairs={{0,112},{16,0},{32,16},{48,32},{64,48},{80,64},{96,80},{112,96},{1... | collective-permute-start | bytes 786440 | tf_op jit(solution)/shard_map/ppermute | solution.py:25
  26.6 21.7 %all-to-all-start = ((bf16[128,16,128]{2,1,0:T(8,128)(2,1)}), bf16[128,16,128]{2,1,0:T(8,128)(2,1)}, u32[]{:S(2)}, u32[]{:S(2)}) async-start(bf16[128,16,128]{2,1,0:T(8,128)(2,1)} %bitcast.21), calls=%async_computation | async-start | bytes 1048576 | tf_op jit(solution)/shard_map/all_to_all | solution.py:453
  34.9 12.6 %collective-permute-start.4 = (bf16[64,512]{1,0:T(8,128)(2,1)}, bf16[64,512]{1,0:T(8,128)(2,1)}, u32[]{:S(2)}, u32[]{:S(2)}) collective-permute-start(bf16[64,512]{1,0:T(8,128)(2,1)} %get-tuple-element.67), channel_id=1, source_target_pairs={{0,1},{1,2},{2,3},{3,4},{4,5},{5,6},{6,7},{7,8},{8,9},{9,10},{10,1... | collective-permute-start | bytes 196616 | tf_op jit(solution)/shard_map/ppermute | solution.py:25
  36.4 11.1 %collective-permute-start.5 = (bf16[64,512]{1,0:T(8,128)(2,1)}, bf16[64,512]{1,0:T(8,128)(2,1)}, u32[]{:S(2)}, u32[]{:S(2)}) collective-permute-start(bf16[64,512]{1,0:T(8,128)(2,1)} %get-tuple-element.68), channel_id=1, source_target_pairs={{0,15},{1,0},{2,1},{3,2},{4,3},{5,4},{6,5},{7,6},{8,7},{9,8},{10,9... | collective-permute-start | bytes 196616 | tf_op jit(solution)/shard_map/ppermute | solution.py:25
  40.8 6.7 %collective-permute-start.6 = (bf16[64,512]{1,0:T(8,128)(2,1)}, bf16[64,512]{1,0:T(8,128)(2,1)}, u32[]{:S(2)}, u32[]{:S(2)}) collective-permute-start(bf16[64,512]{1,0:T(8,128)(2,1)} %get-tuple-element.69), channel_id=1, source_target_pairs={{0,16},{16,32},{32,48},{48,64},{64,80},{80,96},{96,112},{112,0},{1... | collective-permute-start | bytes 196616 | tf_op jit(solution)/shard_map/ppermute | solution.py:25
  42.5 5.0 %collective-permute-start.7 = (bf16[64,512]{1,0:T(8,128)(2,1)}, bf16[64,512]{1,0:T(8,128)(2,1)}, u32[]{:S(2)}, u32[]{:S(2)}) collective-permute-start(bf16[64,512]{1,0:T(8,128)(2,1)} %get-tuple-element.70), channel_id=1, source_target_pairs={{0,112},{16,0},{32,16},{48,32},{64,48},{80,64},{96,80},{112,96},{1... | collective-permute-start | bytes 196616 | tf_op jit(solution)/shard_map/ppermute | solution.py:25
  66.5 13.2 %collective-permute-start.18 = (bf16[32,2,6,16,128]{4,3,2,1,0:T(8,128)(2,1)}, bf16[32,2,6,16,128]{4,3,2,1,0:T(8,128)(2,1)S(1)}, u32[]{:S(2)}, u32[]{:S(2)}) collective-permute-start(bf16[32,2,6,16,128]{4,3,2,1,0:T(8,128)(2,1)} %get-tuple-element.109), channel_id=1, source_target_pairs={{0,16},{16,0},{1,17},{17,1},{2,18},{18,2},{3,19},{19,3},{4,20},{20... | collective-permute-start | bytes 4718600 | tf_op jit(solution)/shard_map/ppermute | solution.py:412
  67.7 18.9 %all-to-all-start.1 = ((bf16[128,16,128]{2,1,0:T(8,128)(2,1)}), bf16[128,16,128]{2,1,0:T(8,128)(2,1)}, u32[]{:S(2)}, u32[]{:S(2)}) async-start(bf16[128,16,128]{2,1,0:T(8,128)(2,1)} %bitcast.20), calls=%async_computation.1 | async-start | bytes 1048576 | tf_op jit(solution)/shard_map/all_to_all | solution.py:474
  72.4 9.2 %collective-permute-start.10 = (bf16[64,512]{1,0:T(8,128)(2,1)}, bf16[64,512]{1,0:T(8,128)(2,1)}, u32[]{:S(2)}, u32[]{:S(2)}) collective-permute-start(bf16[64,512]{1,0:T(8,128)(2,1)} %get-tuple-element.76), channel_id=1, source_target_pairs={{0,112},{16,0},{32,16},{48,32},{64,48},{80,64},{96,80},{112,96},{1... | collective-permute-start | bytes 196616 | tf_op jit(solution)/shard_map/ppermute | solution.py:25
  73.5 8.1 %collective-permute-start.11 = (bf16[64,512]{1,0:T(8,128)(2,1)}, bf16[64,512]{1,0:T(8,128)(2,1)}, u32[]{:S(2)}, u32[]{:S(2)}) collective-permute-start(bf16[64,512]{1,0:T(8,128)(2,1)} %get-tuple-element.77), channel_id=1, source_target_pairs={{0,16},{16,32},{32,48},{48,64},{64,80},{80,96},{96,112},{112,0},{1... | collective-permute-start | bytes 196616 | tf_op jit(solution)/shard_map/ppermute | solution.py:25
  74.2 7.5 %collective-permute-start.8 = (bf16[64,512]{1,0:T(8,128)(2,1)}, bf16[64,512]{1,0:T(8,128)(2,1)}, u32[]{:S(2)}, u32[]{:S(2)}) collective-permute-start(bf16[64,512]{1,0:T(8,128)(2,1)} %get-tuple-element.74), channel_id=1, source_target_pairs={{0,15},{1,0},{2,1},{3,2},{4,3},{5,4},{6,5},{7,6},{8,7},{9,8},{10,9... | collective-permute-start | bytes 196616 | tf_op jit(solution)/shard_map/ppermute | solution.py:25
  79.6 7.0 %collective-permute-start.9 = (bf16[64,512]{1,0:T(8,128)(2,1)}, bf16[64,512]{1,0:T(8,128)(2,1)}, u32[]{:S(2)}, u32[]{:S(2)}) collective-permute-start(bf16[64,512]{1,0:T(8,128)(2,1)} %get-tuple-element.75), channel_id=1, source_target_pairs={{0,1},{1,2},{2,3},{3,4},{4,5},{5,6},{6,7},{7,8},{8,9},{9,10},{10,1... | collective-permute-start | bytes 196616 | tf_op jit(solution)/shard_map/ppermute | solution.py:25
  116.7 52.4 %all-to-all-start.3 = ((bf16[64,96,128]{2,1,0:T(8,128)(2,1)}), bf16[64,96,128]{2,1,0:T(8,128)(2,1)}, u32[]{:S(2)}, u32[]{:S(2)}) async-start(bf16[64,96,128]{2,1,0:T(8,128)(2,1)} %shard_map.175), calls=%async_computation.3 | async-start | bytes 3145728 | tf_op jit(solution)/shard_map/all_to_all | solution.py:509
  141.8 24.5 %collective-permute-start.17 = (bf16[32,2,3,16,128]{4,3,2,1,0:T(8,128)(2,1)}, bf16[32,2,3,16,128]{4,3,2,1,0:T(8,128)(2,1)}, u32[]{:S(2)}, u32[]{:S(2)}) collective-permute-start(bf16[32,2,3,16,128]{4,3,2,1,0:T(8,128)(2,1)} %get-tuple-element.102), channel_id=1, source_target_pairs={{0,16},{16,0},{1,17},{17,1},{2,18},{18,2},{3,19},{19,3},{4,20},{20... | collective-permute-start | bytes 2359304 | tf_op jit(solution)/shard_map/ppermute | solution.py:412
  144.0 10.2 %collective-permute-start.12 = (bf16[256,512]{1,0:T(8,128)(2,1)}, bf16[256,512]{1,0:T(8,128)(2,1)}, u32[]{:S(2)}, u32[]{:S(2)}) collective-permute-start(bf16[256,512]{1,0:T(8,128)(2,1)} %get-tuple-element.92), channel_id=1, source_target_pairs={{0,15},{1,0},{2,1},{3,2},{4,3},{5,4},{6,5},{7,6},{8,7},{9,8},{10,9... | collective-permute-start | bytes 786440 | tf_op jit(solution)/shard_map/ppermute | solution.py:25
  148.3 11.1 %collective-permute-start.13 = (bf16[256,512]{1,0:T(8,128)(2,1)}, bf16[256,512]{1,0:T(8,128)(2,1)}, u32[]{:S(2)}, u32[]{:S(2)}) collective-permute-start(bf16[256,512]{1,0:T(8,128)(2,1)} %get-tuple-element.93), channel_id=1, source_target_pairs={{0,1},{1,2},{2,3},{3,4},{4,5},{5,6},{6,7},{7,8},{8,9},{9,10},{10,1... | collective-permute-start | bytes 786440 | tf_op jit(solution)/shard_map/ppermute | solution.py:25
  148.3 11.1 %collective-permute-start.14 = (bf16[256,512]{1,0:T(8,128)(2,1)}, bf16[256,512]{1,0:T(8,128)(2,1)}, u32[]{:S(2)}, u32[]{:S(2)}) collective-permute-start(bf16[256,512]{1,0:T(8,128)(2,1)} %get-tuple-element.94), channel_id=1, source_target_pairs={{0,112},{16,0},{32,16},{48,32},{64,48},{80,64},{96,80},{112,96},{1... | collective-permute-start | bytes 786440 | tf_op jit(solution)/shard_map/ppermute | solution.py:25
  148.7 10.8 %collective-permute-start.15 = (bf16[256,512]{1,0:T(8,128)(2,1)}, bf16[256,512]{1,0:T(8,128)(2,1)}, u32[]{:S(2)}, u32[]{:S(2)}) collective-permute-start(bf16[256,512]{1,0:T(8,128)(2,1)} %get-tuple-element.95), channel_id=1, source_target_pairs={{0,16},{16,32},{32,48},{48,64},{64,80},{80,96},{96,112},{112,0},{1... | collective-permute-start | bytes 786440 | tf_op jit(solution)/shard_map/ppermute | solution.py:25
  193.9 21.5 %all-to-all-start.5 = ((bf16[64,64,128]{2,1,0:T(8,128)(2,1)}), bf16[64,64,128]{2,1,0:T(8,128)(2,1)}, u32[]{:S(2)}, u32[]{:S(2)}) async-start(bf16[64,64,128]{2,1,0:T(8,128)(2,1)} %shard_map.176), calls=%async_computation.5 | async-start | bytes 2097152 | tf_op jit(solution)/shard_map/all_to_all | solution.py:536
  199.5 19.3 %collective-permute-start.20 = (bf16[64,96,128]{2,1,0:T(8,128)(2,1)}, bf16[64,96,128]{2,1,0:T(8,128)(2,1)}, u32[]{:S(2)}, u32[]{:S(2)}) collective-permute-start(bf16[64,96,128]{2,1,0:T(8,128)(2,1)} %all-to-all-done.3), channel_id=1, source_target_pairs={{0,16},{16,0},{1,17},{17,1},{2,18},{18,2},{3,19},{19,3},{4,20},{20... | collective-permute-start | bytes 4718600 | tf_op jit(solution)/shard_map/ppermute | solution.py:412
  215.4 8.9 %collective-permute-start.19 = (bf16[64,64,128]{2,1,0:T(8,128)(2,1)}, bf16[64,64,128]{2,1,0:T(8,128)(2,1)}, u32[]{:S(2)}, u32[]{:S(2)}) collective-permute-start(bf16[64,64,128]{2,1,0:T(8,128)(2,1)} %all-to-all-done.5), channel_id=1, source_target_pairs={{0,16},{16,0},{1,17},{17,1},{2,18},{18,2},{3,19},{19,3},{4,20},{20... | collective-permute-start | bytes 3145736 | tf_op jit(solution)/shard_map/ppermute | solution.py:412
  (2 other events, 14.8 us)

commit v5 on v4

--- a/solution.py
+++ b/solution.py
@@ -25,14 +25,20 @@
     return lax.ppermute(value, axis, pairs)
 
 
+def moved_rows(blocks, routes):
+    arrived = {}
+    for k in (2, 3, 0, 1) if routes[2][1] < 0 else (3, 2, 1, 0):
+        axis, step = routes[k]
+        arrived[k] = shifted(blocks[k], axis, step)
+    return [arrived[k] for k in range(4)]
+
+
 def outgoing_rows(blocks):
-    routes = ((SUB, 1), (SUB, -1), (FACE, 1), (FACE, -1))
-    return [shifted(block, axis, step) for block, (axis, step) in zip(blocks, routes)]
+    return moved_rows(blocks, ((SUB, 1), (SUB, -1), (FACE, 1), (FACE, -1)))
 
 
 def returned_rows(blocks):
-    routes = ((SUB, -1), (SUB, 1), (FACE, -1), (FACE, 1))
-    return [shifted(block, axis, step) for block, (axis, step) in zip(blocks, routes)]
+    return moved_rows(blocks, ((SUB, -1), (SUB, 1), (FACE, -1), (FACE, 1)))
 
 
 def dot(a, b):

time: 229 us -> 229 us (level)
  no operation moved by 1% of the time
where the time goes in v5:
time: 229 us; the launch traced here: 228 us
  Pallas kernels  77.5 us (34%)
  starting transfers between devices  66.4 us (29%)
  blocking collectives  49.5 us (22%)
  waiting for transfers between devices  31.3 us (14%)
    pallas_call x13, Pallas kernels, call(): pl.pallas_call(body, grid=(1,), out_shape=shapes, in_specs=in_specs, out_...  68.2 us
    ppermute x16, starting transfers between devices, shifted(): return lax.ppermute(value, axis, pairs)  30 us
    all_to_all x1, blocking collectives, on_device(): early = lax.all_to_all(early.reshape(64, 96, 128), CHIPS, 0, 0, tiled=True)  27.2 us
    all_to_all x1, blocking collectives, on_device(): late = lax.all_to_all(late.reshape(64, 64, 128), CHIPS, 0, 0, tiled=True)  22.4 us
    ppermute x16, waiting for transfers between devices, shifted(): return lax.ppermute(value, axis, pairs)  15.7 us
    all_to_all x1, waiting for transfers between devices, on_device(): late = lax.all_to_all(late, CHIPS, 0, 0, tiled=True)  13.4 us
    all_to_all x2, starting transfers between devices, on_device(): lax.all_to_all(far_out.reshape(peers, 16, 128), AXES, 0, 0, tiled=True)  12.9 us
    ppermute x5, starting transfers between devices, swapped(): return lax.ppermute(value, 'core', [(0, 1), (1, 0)])  10.6 us
  transfers between devices with their start and end apart: 25, of which 7 were waited for; matrix products, arithmetic and copies ran while one was open for 1% of the time, Pallas kernels for 17%

profile of v5, /device:TPU:1, one launch (start us, length us, event | category | flops | bytes accessed | tf_op | source)
XLA Modules:
  0.0 228.2 jit_solution(5921939605933660354)
XLA Ops:
  6.1 4.6 %collective-permute-start.1 = (bf16[256,512]{1,0:T(8,128)(2,1)}, bf16[256,512]{1,0:T(8,128)(2,1)}, u32[]{:S(2)}, u32[]{:S(2)}) collective-permute-start(bf16[256,512]{1,0:T(8,128)(2,1)} %get-tuple-element.61), channel_id=1, source_target_pairs={{0,15},{1,0},{2,1},{3,2},{4,3},{5,4},{6,5},{7,6},{8,7},{9,8},{10,9... | collective-permute-start | bytes 786440 | tf_op jit(solution)/shard_map/ppermute | solution.py:25
  13.4 4.1 %shard_map.165.own = f32[1024,512]{1,0:T(8,128)} custom-call(bf16[512,512]{1,0:T(8,128)(2,1)} %get-tuple-element.59.project, s32[8,128]{1,0:T(8,128)} %bitcast.22, s32[8,128]{1,0:T(8,128)} %bitcast.26, bf16[128,512]{1,0:T(8,128)(2,1)} %mesh.5, bf16[10,512,512]{2,1,0:T(8,128)(2,1)} %w0.3), custom_call_target="tpu_custom_call" | custom-call | flops 1000000000 | bytes 3284992 | tf_op jit(solution)/shard_map/pallas_call | solution.py:146
  18.8 7.8 %shard_map.166 = (f32[1024,512]{1,0:T(8,128)}, f32[1024,512]{1,0:T(8,128)}, bf16[1024,512]{1,0:T(8,128)(2,1)}, bf16[128,512]{1,0:T(8,128)(2,1)}, bf16[128,512]{1...) custom-call(f32[1024,512]{1,0:T(8,128)} %shard_map.165.own, ...), custom_call_target="tpu_custom_call" | custom-call | flops 2000000000 | bytes 10628096 | tf_op jit(solution)/shard_map/pallas_call | solution.py:146
  26.6 8.3 %all-to-all-start = ((bf16[128,16,128]{2,1,0:T(8,128)(2,1)}), bf16[128,16,128]{2,1,0:T(8,128)(2,1)}, u32[]{:S(2)}, u32[]{:S(2)}) async-start(bf16[128,16,128]{2,1,0:T(8,128)(2,1)} %bitcast.21), calls=%async_computation | async-start | bytes 1048576 | tf_op jit(solution)/shard_map/all_to_all | solution.py:459
  36.4 4.3 %collective-permute-start.5 = (bf16[64,512]{1,0:T(8,128)(2,1)}, bf16[64,512]{1,0:T(8,128)(2,1)}, u32[]{:S(2)}, u32[]{:S(2)}) collective-permute-start(bf16[64,512]{1,0:T(8,128)(2,1)} %get-tuple-element.68), channel_id=1, source_target_pairs={{0,15},{1,0},{2,1},{3,2},{4,3},{5,4},{6,5},{7,6},{8,7},{9,8},{10,9... | collective-permute-start | bytes 196616 | tf_op jit(solution)/shard_map/ppermute | solution.py:25
  42.5 5.0 %shard_map.167 = (f32[1024,512]{1,0:T(8,128)}, f32[128,512]{1,0:T(8,128)}) custom-call(bf16[128,512]{1,0:T(8,128)(2,1)} %get-tuple-element.64.middle, bf16[128,512]{1,0:T(8,128)(2,1)} %get-tuple-element.65.sender, bf16[1024,512]{1,0:T(8,128)(2,1)} %edge.3, s32[8,128]{1,0:T(8,128)} %bitcast.32, s32[8,128]{1,0:T(8,128)} %bitcast.34, bf16[10,512,512]{2,1,0:T(8,128)(2,1)} %w0.3, ...), custom_call_target="tpu_custom_call" | custom-call | flops 2000000000 | bytes 5251072 | tf_op jit(solution)/shard_map/pallas_call | solution.py:146
  48.3 11.9 %shard_map.168 = (bf16[128,512]{1,0:T(8,128)(2,1)}, bf16[1024,512]{1,0:T(8,128)(2,1)}, bf16[128,512]{1,0:T(8,128)(2,1)}, bf16[128,512]{1,0:T(8,128)(2,1)}, bf16[...) custom-call(f32[1024,512]{1,0:T(8,128)} %get-tuple-element.66.own, ...), custom_call_target="tpu_custom_call" | custom-call | flops 8000000000 | bytes 11018240 | tf_op jit(solution)/shard_map/pallas_call | solution.py:146
  60.2 6.2 %shard_map.174 = (bf16[32,2,6,16,128]{4,3,2,1,0:T(8,128)(2,1)}, bf16[32,2,6,16,128]{4,3,2,1,0:T(8,128)(2,1)}) custom-call(s32[1]{0:T(128)} %bitcast.8.core, bf16[1024,512]{1,0:T(8,128)(2,1)} %edge.3, bf16[1024,512]{1,0:T(8,128)(2,1)} %get-tuple-element.80.cround, bf16[1024,512]{1,0:T(8,128)(2,1)} %get-tuple-element.103.hidden, ...), custom_call_target="tpu_custom_call" | custom-call | flops 2000000000 | bytes 8126468 | tf_op jit(solution)/shard_map/pallas_call | solution.py:146
  67.7 4.7 %all-to-all-start.1 = ((bf16[128,16,128]{2,1,0:T(8,128)(2,1)}), bf16[128,16,128]{2,1,0:T(8,128)(2,1)}, u32[]{:S(2)}, u32[]{:S(2)}) async-start(bf16[128,16,128]{2,1,0:T(8,128)(2,1)} %bitcast.20), calls=%async_computation.1 | async-start | bytes 1048576 | tf_op jit(solution)/shard_map/all_to_all | solution.py:480
  74.2 5.5 %collective-permute-start.8 = (bf16[64,512]{1,0:T(8,128)(2,1)}, bf16[64,512]{1,0:T(8,128)(2,1)}, u32[]{:S(2)}, u32[]{:S(2)}) collective-permute-start(bf16[64,512]{1,0:T(8,128)(2,1)} %get-tuple-element.74), channel_id=1, source_target_pairs={{0,15},{1,0},{2,1},{3,2},{4,3},{5,4},{6,5},{7,6},{8,7},{9,8},{10,9... | collective-permute-start | bytes 196616 | tf_op jit(solution)/shard_map/ppermute | solution.py:25
  81.7 5.0 %collective-permute-done.9.in1 = bf16[64,512]{1,0:T(8,128)(2,1)} collective-permute-done((bf16[64,512]{1,0:T(8,128)(2,1)}, bf16[64,512]{1,0:T(8,128)(2,1)}, u32[]{:S(2)}, u32[]{:S(2)}) %collective-permute-start.9) | collective-permute-done | bytes 65568 | tf_op jit(solution)/shard_map/ppermute | solution.py:25
  86.6 27.2 %all_to_all.30.terms = bf16[64,96,128]{2,1,0:T(8,128)(2,1)} all-to-all(bf16[64,96,128]{2,1,0:T(8,128)(2,1)S(1)} %bitcast.18), channel_id=1, replica_groups=mesh['x'=4,'core'=2,'y'=4,'z'=4] {'x','y','z'}, dimensions={0} | all-to-all | bytes 3145728 | tf_op jit(solution)/shard_map/all_to_all | solution.py:500
  116.7 7.2 %all-to-all-start.3 = ((bf16[64,96,128]{2,1,0:T(8,128)(2,1)}), bf16[64,96,128]{2,1,0:T(8,128)(2,1)}, u32[]{:S(2)}, u32[]{:S(2)}) async-start(bf16[64,96,128]{2,1,0:T(8,128)(2,1)} %shard_map.175), calls=%async_computation.3 | async-start | bytes 3145728 | tf_op jit(solution)/shard_map/all_to_all | solution.py:515
  123.8 4.5 %shard_map.169 = (bf16[1024,512]{1,0:T(8,128)(2,1)}, f32[128,512]{1,0:T(8,128)}) custom-call(bf16[1024,512]{1,0:T(8,128)(2,1)} %get-tuple-element.80.cround, bf16[1024,512]{1,0:T(8,128)(2,1)} %edge_cot.3, bf16[128,512]{1,0:T(8,128)(2,1)} %get-tuple-element.81.receive, bf16[128,512]{1,0:T(8,128)(2,1)} %get-tuple-element.82.cot_update, ...), custom_call_target="tpu_custom_call" | custom-call | flops 1000000000 | bytes 5373952 | tf_op jit(solution)/shard_map/pallas_call | solution.py:146
  128.3 8.1 %shard_map.170 = (bf16[128,512]{1,0:T(8,128)(2,1)}, f32[128,512]{1,0:T(8,128)}, bf16[1024,512]{1,0:T(8,128)(2,1)}, bf16[1024,512]{1,0:T(8,128)(2,1)}, bf16[256,5...) custom-call(bf16[64,512]{1,0:T(8,128)(2,1)} %collective-permute-done.8.in0, ...), custom_call_target="tpu_custom_call" | custom-call | flops 4000000000 | bytes 10103808 | tf_op jit(solution)/shard_map/pallas_call | solution.py:146
  136.5 5.4 %shard_map.171 = (f32[512,512]{1,0:T(8,128)}, bf16[128,512]{1,0:T(8,128)(2,1)}, bf16[32,2,3,16,128]{4,3,2,1,0:T(8,128)(2,1)}, bf16[32,2,3,16,128]{4,3,2,1,0:T(8,128)(2,1)}) custom-call(s32[1]{0:T(128)} %bitcast.8.core, bf16[1024,512]{1,0:T(8,128)(2,1)} %get-tuple-element.86.upper, s32[8,128]{1,0:T(8,128)} %bitcast.25, s32[8,128]{1,0:T(8,128)} %bitcast.29, ...), custom_call_target="tpu_custom_call" | custom-call | flops 2000000000 | bytes 7086084 | tf_op jit(solution)/shard_map/pallas_call | solution.py:146
  144.0 4.3 %collective-permute-start.12 = (bf16[256,512]{1,0:T(8,128)(2,1)}, bf16[256,512]{1,0:T(8,128)(2,1)}, u32[]{:S(2)}, u32[]{:S(2)}) collective-permute-start(bf16[256,512]{1,0:T(8,128)(2,1)} %get-tuple-element.92), channel_id=1, source_target_pairs={{0,15},{1,0},{2,1},{3,2},{4,3},{5,4},{6,5},{7,6},{8,7},{9,8},{10,9... | collective-permute-start | bytes 786440 | tf_op jit(solution)/shard_map/ppermute | solution.py:25
  150.1 4.1 %collective-permute-done.12.in0 = bf16[256,512]{1,0:T(8,128)(2,1)} collective-permute-done((bf16[256,512]{1,0:T(8,128)(2,1)}, bf16[256,512]{1,0:T(8,128)(2,1)}, u32[]{:S(2)}, u32[]{:S(2)}) %collective-permute-start.12) | collective-permute-done | bytes 262176 | tf_op jit(solution)/shard_map/ppermute | solution.py:25
  154.2 5.2 %collective-permute-done.13.in1 = bf16[256,512]{1,0:T(8,128)(2,1)} collective-permute-done((bf16[256,512]{1,0:T(8,128)(2,1)}, bf16[256,512]{1,0:T(8,128)(2,1)}, u32[]{:S(2)}, u32[]{:S(2)}) %collective-permute-start.13) | collective-permute-done | bytes 262176 | tf_op jit(solution)/shard_map/ppermute | solution.py:25
  159.5 4.1 %shard_map.172 = (bf16[512,512]{1,0:T(8,128)(2,1)}, bf16[32,2,1,16,128]{4,3,2,1,0:T(8,128)(2,1)}, bf16[32,2,1,16,128]{4,3,2,1,0:T(8,128)(2,1)}) custom-call(s32[1]{0:T(128)} %bitcast.8.core, f32[512,512]{1,0:T(8,128)} %get-tuple-element.91.grid_own, bf16[256,512]{1,0:T(8,128)(2,1)} %collective-permute-done.12.in0, ...), custom_call_target="tpu_custom_call" | custom-call | flops 1000000000 | bytes 4198404 | tf_op jit(solution)/shard_map/pallas_call | solution.py:146
  169.0 22.4 %all_to_all.31.terms = bf16[64,64,128]{2,1,0:T(8,128)(2,1)} all-to-all(bf16[64,64,128]{2,1,0:T(8,128)(2,1)} %bitcast.19), channel_id=1, replica_groups=mesh['x'=4,'core'=2,'y'=4,'z'=4] {'x','y','z'}, dimensions={0} | all-to-all | bytes 2097152 | tf_op jit(solution)/shard_map/all_to_all | solution.py:526
  193.9 5.7 %all-to-all-start.5 = ((bf16[64,64,128]{2,1,0:T(8,128)(2,1)}), bf16[64,64,128]{2,1,0:T(8,128)(2,1)}, u32[]{:S(2)}, u32[]{:S(2)}) async-start(bf16[64,64,128]{2,1,0:T(8,128)(2,1)} %shard_map.176), calls=%async_computation.5 | async-start | bytes 2097152 | tf_op jit(solution)/shard_map/all_to_all | solution.py:542
  202.0 13.4 %all-to-all-done.5 = bf16[64,64,128]{2,1,0:T(8,128)(2,1)} async-done(((bf16[64,64,128]{2,1,0:T(8,128)(2,1)}), bf16[64,64,128]{2,1,0:T(8,128)(2,1)}, u32[]{:S(2)}, u32[]{:S(2)}) %all-to-all-start.5) | async-done | bytes 1048608 | tf_op jit(solution)/shard_map/all_to_all | solution.py:542
  218.9 5.4 %place_early.1.kept = bf16[10,512,512]{2,1,0:T(8,128)(2,1)} custom-call(s32[1]{0:T(128)} %bitcast.8.core, bf16[32,2,6,16,128]{4,3,2,1,0:T(8,128)(2,1)} %bitcast.16.own, bf16[32,2,6,16,128]{4,3,2,1,0:T(8,128)(2,1)} %bitcast.17.other), custom_call_target="tpu_custom_call" | custom-call | tf_op jit(solution)/shard_map/place_early/pallas_call | solution.py:529
  (47 shorter events, 43.2 us)
Async XLA Ops:
  3.6 13.9 %collective-permute-start = (bf16[256,512]{1,0:T(8,128)(2,1)}, bf16[256,512]{1,0:T(8,128)(2,1)}, u32[]{:S(2)}, u32[]{:S(2)}) collective-permute-start(bf16[256,512]{1,0:T(8,128)(2,1)} %get-tuple-element.60), channel_id=1, source_target_pairs={{0,1},{1,2},{2,3},{3,4},{4,5},{5,6},{6,7},{7,8},{8,9},{9,10},{10,1... | collective-permute-start | bytes 786440 | tf_op jit(solution)/shard_map/ppermute | solution.py:25
  6.1 11.4 %collective-permute-start.1 = (bf16[256,512]{1,0:T(8,128)(2,1)}, bf16[256,512]{1,0:T(8,128)(2,1)}, u32[]{:S(2)}, u32[]{:S(2)}) collective-permute-start(bf16[256,512]{1,0:T(8,128)(2,1)} %get-tuple-element.61), channel_id=1, source_target_pairs={{0,15},{1,0},{2,1},{3,2},{4,3},{5,4},{6,5},{7,6},{8,7},{9,8},{10,9... | collective-permute-start | bytes 786440 | tf_op jit(solution)/shard_map/ppermute | solution.py:25
  10.7 6.9 %collective-permute-start.2 = (bf16[256,512]{1,0:T(8,128)(2,1)}, bf16[256,512]{1,0:T(8,128)(2,1)}, u32[]{:S(2)}, u32[]{:S(2)}) collective-permute-start(bf16[256,512]{1,0:T(8,128)(2,1)} %get-tuple-element.62), channel_id=1, source_target_pairs={{0,16},{16,32},{32,48},{48,64},{64,80},{80,96},{96,112},{112,0},{1... | collective-permute-start | bytes 786440 | tf_op jit(solution)/shard_map/ppermute | solution.py:25
  12.7 6.1 %collective-permute-start.3 = (bf16[256,512]{1,0:T(8,128)(2,1)}, bf16[256,512]{1,0:T(8,128)(2,1)}, u32[]{:S(2)}, u32[]{:S(2)}) collective-permute-start(bf16[256,512]{1,0:T(8,128)(2,1)} %get-tuple-element.63), channel_id=1, source_target_pairs={{0,112},{16,0},{32,16},{48,32},{64,48},{80,64},{96,80},{112,96},{1... | collective-permute-start | bytes 786440 | tf_op jit(solution)/shard_map/ppermute | solution.py:25
  26.6 21.7 %all-to-all-start = ((bf16[128,16,128]{2,1,0:T(8,128)(2,1)}), bf16[128,16,128]{2,1,0:T(8,128)(2,1)}, u32[]{:S(2)}, u32[]{:S(2)}) async-start(bf16[128,16,128]{2,1,0:T(8,128)(2,1)} %bitcast.21), calls=%async_computation | async-start | bytes 1048576 | tf_op jit(solution)/shard_map/all_to_all | solution.py:459
  34.9 12.6 %collective-permute-start.4 = (bf16[64,512]{1,0:T(8,128)(2,1)}, bf16[64,512]{1,0:T(8,128)(2,1)}, u32[]{:S(2)}, u32[]{:S(2)}) collective-permute-start(bf16[64,512]{1,0:T(8,128)(2,1)} %get-tuple-element.67), channel_id=1, source_target_pairs={{0,1},{1,2},{2,3},{3,4},{4,5},{5,6},{6,7},{7,8},{8,9},{9,10},{10,1... | collective-permute-start | bytes 196616 | tf_op jit(solution)/shard_map/ppermute | solution.py:25
  36.4 11.1 %collective-permute-start.5 = (bf16[64,512]{1,0:T(8,128)(2,1)}, bf16[64,512]{1,0:T(8,128)(2,1)}, u32[]{:S(2)}, u32[]{:S(2)}) collective-permute-start(bf16[64,512]{1,0:T(8,128)(2,1)} %get-tuple-element.68), channel_id=1, source_target_pairs={{0,15},{1,0},{2,1},{3,2},{4,3},{5,4},{6,5},{7,6},{8,7},{9,8},{10,9... | collective-permute-start | bytes 196616 | tf_op jit(solution)/shard_map/ppermute | solution.py:25
  40.8 6.7 %collective-permute-start.6 = (bf16[64,512]{1,0:T(8,128)(2,1)}, bf16[64,512]{1,0:T(8,128)(2,1)}, u32[]{:S(2)}, u32[]{:S(2)}) collective-permute-start(bf16[64,512]{1,0:T(8,128)(2,1)} %get-tuple-element.69), channel_id=1, source_target_pairs={{0,16},{16,32},{32,48},{48,64},{64,80},{80,96},{96,112},{112,0},{1... | collective-permute-start | bytes 196616 | tf_op jit(solution)/shard_map/ppermute | solution.py:25
  42.5 5.0 %collective-permute-start.7 = (bf16[64,512]{1,0:T(8,128)(2,1)}, bf16[64,512]{1,0:T(8,128)(2,1)}, u32[]{:S(2)}, u32[]{:S(2)}) collective-permute-start(bf16[64,512]{1,0:T(8,128)(2,1)} %get-tuple-element.70), channel_id=1, source_target_pairs={{0,112},{16,0},{32,16},{48,32},{64,48},{80,64},{96,80},{112,96},{1... | collective-permute-start | bytes 196616 | tf_op jit(solution)/shard_map/ppermute | solution.py:25
  66.5 13.2 %collective-permute-start.18 = (bf16[32,2,6,16,128]{4,3,2,1,0:T(8,128)(2,1)}, bf16[32,2,6,16,128]{4,3,2,1,0:T(8,128)(2,1)S(1)}, u32[]{:S(2)}, u32[]{:S(2)}) collective-permute-start(bf16[32,2,6,16,128]{4,3,2,1,0:T(8,128)(2,1)} %get-tuple-element.109), channel_id=1, source_target_pairs={{0,16},{16,0},{1,17},{17,1},{2,18},{18,2},{3,19},{19,3},{4,20},{20... | collective-permute-start | bytes 4718600 | tf_op jit(solution)/shard_map/ppermute | solution.py:418
  67.7 18.9 %all-to-all-start.1 = ((bf16[128,16,128]{2,1,0:T(8,128)(2,1)}), bf16[128,16,128]{2,1,0:T(8,128)(2,1)}, u32[]{:S(2)}, u32[]{:S(2)}) async-start(bf16[128,16,128]{2,1,0:T(8,128)(2,1)} %bitcast.20), calls=%async_computation.1 | async-start | bytes 1048576 | tf_op jit(solution)/shard_map/all_to_all | solution.py:480
  72.4 9.2 %collective-permute-start.10 = (bf16[64,512]{1,0:T(8,128)(2,1)}, bf16[64,512]{1,0:T(8,128)(2,1)}, u32[]{:S(2)}, u32[]{:S(2)}) collective-permute-start(bf16[64,512]{1,0:T(8,128)(2,1)} %get-tuple-element.76), channel_id=1, source_target_pairs={{0,112},{16,0},{32,16},{48,32},{64,48},{80,64},{96,80},{112,96},{1... | collective-permute-start | bytes 196616 | tf_op jit(solution)/shard_map/ppermute | solution.py:25
  73.5 8.1 %collective-permute-start.11 = (bf16[64,512]{1,0:T(8,128)(2,1)}, bf16[64,512]{1,0:T(8,128)(2,1)}, u32[]{:S(2)}, u32[]{:S(2)}) collective-permute-start(bf16[64,512]{1,0:T(8,128)(2,1)} %get-tuple-element.77), channel_id=1, source_target_pairs={{0,16},{16,32},{32,48},{48,64},{64,80},{80,96},{96,112},{112,0},{1... | collective-permute-start | bytes 196616 | tf_op jit(solution)/shard_map/ppermute | solution.py:25
  74.2 7.5 %collective-permute-start.8 = (bf16[64,512]{1,0:T(8,128)(2,1)}, bf16[64,512]{1,0:T(8,128)(2,1)}, u32[]{:S(2)}, u32[]{:S(2)}) collective-permute-start(bf16[64,512]{1,0:T(8,128)(2,1)} %get-tuple-element.74), channel_id=1, source_target_pairs={{0,15},{1,0},{2,1},{3,2},{4,3},{5,4},{6,5},{7,6},{8,7},{9,8},{10,9... | collective-permute-start | bytes 196616 | tf_op jit(solution)/shard_map/ppermute | solution.py:25
  79.6 7.0 %collective-permute-start.9 = (bf16[64,512]{1,0:T(8,128)(2,1)}, bf16[64,512]{1,0:T(8,128)(2,1)}, u32[]{:S(2)}, u32[]{:S(2)}) collective-permute-start(bf16[64,512]{1,0:T(8,128)(2,1)} %get-tuple-element.75), channel_id=1, source_target_pairs={{0,1},{1,2},{2,3},{3,4},{4,5},{5,6},{6,7},{7,8},{8,9},{9,10},{10,1... | collective-permute-start | bytes 196616 | tf_op jit(solution)/shard_map/ppermute | solution.py:25
  116.7 52.4 %all-to-all-start.3 = ((bf16[64,96,128]{2,1,0:T(8,128)(2,1)}), bf16[64,96,128]{2,1,0:T(8,128)(2,1)}, u32[]{:S(2)}, u32[]{:S(2)}) async-start(bf16[64,96,128]{2,1,0:T(8,128)(2,1)} %shard_map.175), calls=%async_computation.3 | async-start | bytes 3145728 | tf_op jit(solution)/shard_map/all_to_all | solution.py:515
  141.8 24.5 %collective-permute-start.17 = (bf16[32,2,3,16,128]{4,3,2,1,0:T(8,128)(2,1)}, bf16[32,2,3,16,128]{4,3,2,1,0:T(8,128)(2,1)}, u32[]{:S(2)}, u32[]{:S(2)}) collective-permute-start(bf16[32,2,3,16,128]{4,3,2,1,0:T(8,128)(2,1)} %get-tuple-element.102), channel_id=1, source_target_pairs={{0,16},{16,0},{1,17},{17,1},{2,18},{18,2},{3,19},{19,3},{4,20},{20... | collective-permute-start | bytes 2359304 | tf_op jit(solution)/shard_map/ppermute | solution.py:418
  144.0 10.2 %collective-permute-start.12 = (bf16[256,512]{1,0:T(8,128)(2,1)}, bf16[256,512]{1,0:T(8,128)(2,1)}, u32[]{:S(2)}, u32[]{:S(2)}) collective-permute-start(bf16[256,512]{1,0:T(8,128)(2,1)} %get-tuple-element.92), channel_id=1, source_target_pairs={{0,15},{1,0},{2,1},{3,2},{4,3},{5,4},{6,5},{7,6},{8,7},{9,8},{10,9... | collective-permute-start | bytes 786440 | tf_op jit(solution)/shard_map/ppermute | solution.py:25
  148.3 11.1 %collective-permute-start.13 = (bf16[256,512]{1,0:T(8,128)(2,1)}, bf16[256,512]{1,0:T(8,128)(2,1)}, u32[]{:S(2)}, u32[]{:S(2)}) collective-permute-start(bf16[256,512]{1,0:T(8,128)(2,1)} %get-tuple-element.93), channel_id=1, source_target_pairs={{0,1},{1,2},{2,3},{3,4},{4,5},{5,6},{6,7},{7,8},{8,9},{9,10},{10,1... | collective-permute-start | bytes 786440 | tf_op jit(solution)/shard_map/ppermute | solution.py:25
  148.3 11.1 %collective-permute-start.14 = (bf16[256,512]{1,0:T(8,128)(2,1)}, bf16[256,512]{1,0:T(8,128)(2,1)}, u32[]{:S(2)}, u32[]{:S(2)}) collective-permute-start(bf16[256,512]{1,0:T(8,128)(2,1)} %get-tuple-element.94), channel_id=1, source_target_pairs={{0,112},{16,0},{32,16},{48,32},{64,48},{80,64},{96,80},{112,96},{1... | collective-permute-start | bytes 786440 | tf_op jit(solution)/shard_map/ppermute | solution.py:25
  148.7 10.8 %collective-permute-start.15 = (bf16[256,512]{1,0:T(8,128)(2,1)}, bf16[256,512]{1,0:T(8,128)(2,1)}, u32[]{:S(2)}, u32[]{:S(2)}) collective-permute-start(bf16[256,512]{1,0:T(8,128)(2,1)} %get-tuple-element.95), channel_id=1, source_target_pairs={{0,16},{16,32},{32,48},{48,64},{64,80},{80,96},{96,112},{112,0},{1... | collective-permute-start | bytes 786440 | tf_op jit(solution)/shard_map/ppermute | solution.py:25
  193.9 21.5 %all-to-all-start.5 = ((bf16[64,64,128]{2,1,0:T(8,128)(2,1)}), bf16[64,64,128]{2,1,0:T(8,128)(2,1)}, u32[]{:S(2)}, u32[]{:S(2)}) async-start(bf16[64,64,128]{2,1,0:T(8,128)(2,1)} %shard_map.176), calls=%async_computation.5 | async-start | bytes 2097152 | tf_op jit(solution)/shard_map/all_to_all | solution.py:542
  199.5 19.3 %collective-permute-start.20 = (bf16[64,96,128]{2,1,0:T(8,128)(2,1)}, bf16[64,96,128]{2,1,0:T(8,128)(2,1)}, u32[]{:S(2)}, u32[]{:S(2)}) collective-permute-start(bf16[64,96,128]{2,1,0:T(8,128)(2,1)} %all-to-all-done.3), channel_id=1, source_target_pairs={{0,16},{16,0},{1,17},{17,1},{2,18},{18,2},{3,19},{19,3},{4,20},{20... | collective-permute-start | bytes 4718600 | tf_op jit(solution)/shard_map/ppermute | solution.py:418
  215.4 8.9 %collective-permute-start.19 = (bf16[64,64,128]{2,1,0:T(8,128)(2,1)}, bf16[64,64,128]{2,1,0:T(8,128)(2,1)}, u32[]{:S(2)}, u32[]{:S(2)}) collective-permute-start(bf16[64,64,128]{2,1,0:T(8,128)(2,1)} %all-to-all-done.5), channel_id=1, source_target_pairs={{0,16},{16,0},{1,17},{17,1},{2,18},{18,2},{3,19},{19,3},{4,20},{20... | collective-permute-start | bytes 3145736 | tf_op jit(solution)/shard_map/ppermute | solution.py:418
  (2 other events, 14.8 us)

commit v6 on v4

--- a/solution.py
+++ b/solution.py
@@ -67,7 +67,7 @@
 
 
 def sigmoid(values):
-    return 1.0 / (1.0 + jnp.exp(-values))
+    return 0.5 + 0.5 * jnp.tanh(0.5 * values)
 
 
 def silu(values):
@@ -383,16 +383,25 @@
             place += 1
 
 
-def sum_body(terms, *shard):
+def sum_body(terms, shard):
     total = terms[0].astype(f32)
     for d in range(1, terms.shape[0]):
         total = total + terms[d].astype(f32)
     total = total.astype(bf16)
-    if len(shard[0].shape) == 2:
-        shard[0][...] = total
-    else:
-        for p in range(shard[0].shape[0]):
-            shard[0][p] = total
+    for p in range(shard.shape[0]):
+        shard[p] = total
+
+
+def summed(terms):
+    spec = pl.BlockSpec((terms.shape[0], 32, 128), lambda i: (0, i, 0))
+    return pl.pallas_call(
+        sum_body,
+        grid=(terms.shape[1] // 32,),
+        in_specs=[spec],
+        out_specs=spec,
+        out_shape=jax.ShapeDtypeStruct(terms.shape, bf16),
+        compiler_params=pltpu.CompilerParams(vmem_limit_bytes=67000000),
+    )(terms)
 
 
 def place_early_body(core, own, other, out):
@@ -505,7 +514,7 @@
         (core, upper, gslot, gtarget, cot_middle, mesh_latent, middle, cot_sender, hidden, elinear),
         weights, (1,), scratch=(held,), flops=2 * 10**9,
     )
-    (early,) = call(sum_body, [((64, 96, 128), bf16)], (early,), flops=10**7)
+    early = summed(early)
     early = lax.all_to_all(early, CHIPS, 0, 0, tiled=True)
     grid_grad, last_own, last_other = call(
         scaled(grid_back_body, [grid_scale]), [((512, latent), bf16), blocks(1), blocks(1)],
@@ -532,7 +541,7 @@
         compiler_params=pltpu.CompilerParams(vmem_limit_bytes=67000000),
         name="place_early",
     )(core, early, early_swapped)
-    (late,) = call(sum_body, [((64, 64, 128), bf16)], (late,), flops=10**7)
+    late = summed(late)
     late = lax.all_to_all(late, CHIPS, 0, 0, tiled=True)
     other = swapped(late).reshape(blocks(4)[0])
     late = late.reshape(blocks(4)[0])

time: 229 us -> 229 us (level)
    pallas_call x13 -> x11, Pallas kernels: 68.2 us -> 62.3 us  [call(): pl.pallas_call(body, grid=(1,), out_shape=shapes, in_specs=in_specs, out_...]
    pallas_call x0 -> x2, Pallas kernels: none -> 5.65 us  [summed(): pl.pallas_call(sum_body, grid=(terms.shape[1] // 32,), in_specs=[spec], o...]
where the time goes in v6:
time: 229 us; the launch traced here: 228 us
  Pallas kernels  77.3 us (34%)
  starting transfers between devices  66.4 us (29%)
  blocking collectives  49.5 us (22%)
  waiting for transfers between devices  31.3 us (14%)
    pallas_call x11, Pallas kernels, call(): pl.pallas_call(body, grid=(1,), out_shape=shapes, in_specs=in_specs, out_...  62.3 us
    ppermute x16, starting transfers between devices, shifted(): return lax.ppermute(value, axis, pairs)  30 us
    all_to_all x1, blocking collectives, on_device(): early = lax.all_to_all(early.reshape(64, 96, 128), CHIPS, 0, 0, tiled=True)  27.2 us
    all_to_all x1, blocking collectives, on_device(): late = lax.all_to_all(late.reshape(64, 64, 128), CHIPS, 0, 0, tiled=True)  22.4 us
    ppermute x16, waiting for transfers between devices, shifted(): return lax.ppermute(value, axis, pairs)  15.7 us
    all_to_all x1, waiting for transfers between devices, on_device(): late = lax.all_to_all(late, CHIPS, 0, 0, tiled=True)  13.4 us
    all_to_all x2, starting transfers between devices, on_device(): lax.all_to_all(far_out.reshape(peers, 16, 128), AXES, 0, 0, tiled=True)  12.9 us
    ppermute x5, starting transfers between devices, swapped(): return lax.ppermute(value, 'core', [(0, 1), (1, 0)])  10.6 us
  transfers between devices with their start and end apart: 25, of which 7 were waited for; matrix products, arithmetic and copies ran while one was open for 1% of the time, Pallas kernels for 17%

profile of v6, /device:TPU:1, one launch (start us, length us, event | category | flops | bytes accessed | tf_op | source)
XLA Modules:
  0.0 228.0 jit_solution(663545513909823503)
XLA Ops:
  6.1 4.6 %collective-permute-start.1 = (bf16[256,512]{1,0:T(8,128)(2,1)}, bf16[256,512]{1,0:T(8,128)(2,1)}, u32[]{:S(2)}, u32[]{:S(2)}) collective-permute-start(bf16[256,512]{1,0:T(8,128)(2,1)} %get-tuple-element.61), channel_id=1, source_target_pairs={{0,15},{1,0},{2,1},{3,2},{4,3},{5,4},{6,5},{7,6},{8,7},{9,8},{10,9... | collective-permute-start | bytes 786440 | tf_op jit(solution)/shard_map/ppermute | solution.py:25
  13.4 4.1 %shard_map.165.own = f32[1024,512]{1,0:T(8,128)} custom-call(bf16[512,512]{1,0:T(8,128)(2,1)} %get-tuple-element.59.project, s32[8,128]{1,0:T(8,128)} %bitcast.22, s32[8,128]{1,0:T(8,128)} %bitcast.26, bf16[128,512]{1,0:T(8,128)(2,1)} %mesh.5, bf16[10,512,512]{2,1,0:T(8,128)(2,1)} %w0.3), custom_call_target="tpu_custom_call" | custom-call | flops 1000000000 | bytes 3284992 | tf_op jit(solution)/shard_map/pallas_call | solution.py:140
  18.8 7.6 %shard_map.166 = (f32[1024,512]{1,0:T(8,128)}, f32[1024,512]{1,0:T(8,128)}, bf16[1024,512]{1,0:T(8,128)(2,1)}, bf16[128,512]{1,0:T(8,128)(2,1)}, bf16[128,512]{1...) custom-call(f32[1024,512]{1,0:T(8,128)} %shard_map.165.own, ...), custom_call_target="tpu_custom_call" | custom-call | flops 2000000000 | bytes 10628096 | tf_op jit(solution)/shard_map/pallas_call | solution.py:140
  26.4 8.3 %all-to-all-start = ((bf16[128,16,128]{2,1,0:T(8,128)(2,1)}), bf16[128,16,128]{2,1,0:T(8,128)(2,1)}, u32[]{:S(2)}, u32[]{:S(2)}) async-start(bf16[128,16,128]{2,1,0:T(8,128)(2,1)} %bitcast.21), calls=%async_computation | async-start | bytes 1048576 | tf_op jit(solution)/shard_map/all_to_all | solution.py:462
  36.3 4.3 %collective-permute-start.5 = (bf16[64,512]{1,0:T(8,128)(2,1)}, bf16[64,512]{1,0:T(8,128)(2,1)}, u32[]{:S(2)}, u32[]{:S(2)}) collective-permute-start(bf16[64,512]{1,0:T(8,128)(2,1)} %get-tuple-element.68), channel_id=1, source_target_pairs={{0,15},{1,0},{2,1},{3,2},{4,3},{5,4},{6,5},{7,6},{8,7},{9,8},{10,9... | collective-permute-start | bytes 196616 | tf_op jit(solution)/shard_map/ppermute | solution.py:25
  42.4 5.0 %shard_map.167 = (f32[1024,512]{1,0:T(8,128)}, f32[128,512]{1,0:T(8,128)}) custom-call(bf16[128,512]{1,0:T(8,128)(2,1)} %get-tuple-element.64.middle, bf16[128,512]{1,0:T(8,128)(2,1)} %get-tuple-element.65.sender, bf16[1024,512]{1,0:T(8,128)(2,1)} %edge.3, s32[8,128]{1,0:T(8,128)} %bitcast.32, s32[8,128]{1,0:T(8,128)} %bitcast.34, bf16[10,512,512]{2,1,0:T(8,128)(2,1)} %w0.3, ...), custom_call_target="tpu_custom_call" | custom-call | flops 2000000000 | bytes 5251072 | tf_op jit(solution)/shard_map/pallas_call | solution.py:140
  48.1 11.6 %shard_map.168 = (bf16[128,512]{1,0:T(8,128)(2,1)}, bf16[1024,512]{1,0:T(8,128)(2,1)}, bf16[128,512]{1,0:T(8,128)(2,1)}, bf16[128,512]{1,0:T(8,128)(2,1)}, bf16[...) custom-call(f32[1024,512]{1,0:T(8,128)} %get-tuple-element.66.own, ...), custom_call_target="tpu_custom_call" | custom-call | flops 8000000000 | bytes 11018240 | tf_op jit(solution)/shard_map/pallas_call | solution.py:140
  59.8 6.2 %shard_map.174 = (bf16[32,2,6,16,128]{4,3,2,1,0:T(8,128)(2,1)}, bf16[32,2,6,16,128]{4,3,2,1,0:T(8,128)(2,1)}) custom-call(s32[1]{0:T(128)} %bitcast.8.core, bf16[1024,512]{1,0:T(8,128)(2,1)} %edge.3, bf16[1024,512]{1,0:T(8,128)(2,1)} %get-tuple-element.80.cround, bf16[1024,512]{1,0:T(8,128)(2,1)} %get-tuple-element.103.hidden, ...), custom_call_target="tpu_custom_call" | custom-call | flops 2000000000 | bytes 8126468 | tf_op jit(solution)/shard_map/pallas_call | solution.py:140
  67.3 4.7 %all-to-all-start.1 = ((bf16[128,16,128]{2,1,0:T(8,128)(2,1)}), bf16[128,16,128]{2,1,0:T(8,128)(2,1)}, u32[]{:S(2)}, u32[]{:S(2)}) async-start(bf16[128,16,128]{2,1,0:T(8,128)(2,1)} %bitcast.20), calls=%async_computation.1 | async-start | bytes 1048576 | tf_op jit(solution)/shard_map/all_to_all | solution.py:483
  73.7 5.5 %collective-permute-start.8 = (bf16[64,512]{1,0:T(8,128)(2,1)}, bf16[64,512]{1,0:T(8,128)(2,1)}, u32[]{:S(2)}, u32[]{:S(2)}) collective-permute-start(bf16[64,512]{1,0:T(8,128)(2,1)} %get-tuple-element.74), channel_id=1, source_target_pairs={{0,15},{1,0},{2,1},{3,2},{4,3},{5,4},{6,5},{7,6},{8,7},{9,8},{10,9... | collective-permute-start | bytes 196616 | tf_op jit(solution)/shard_map/ppermute | solution.py:25
  81.2 5.0 %collective-permute-done.9.in1 = bf16[64,512]{1,0:T(8,128)(2,1)} collective-permute-done((bf16[64,512]{1,0:T(8,128)(2,1)}, bf16[64,512]{1,0:T(8,128)(2,1)}, u32[]{:S(2)}, u32[]{:S(2)}) %collective-permute-start.9) | collective-permute-done | bytes 65568 | tf_op jit(solution)/shard_map/ppermute | solution.py:25
  86.2 27.2 %all_to_all.30.terms = bf16[64,96,128]{2,1,0:T(8,128)(2,1)} all-to-all(bf16[64,96,128]{2,1,0:T(8,128)(2,1)S(1)} %bitcast.18), channel_id=1, replica_groups=mesh['x'=4,'core'=2,'y'=4,'z'=4] {'x','y','z'}, dimensions={0} | all-to-all | bytes 3145728 | tf_op jit(solution)/shard_map/all_to_all | solution.py:503
  116.9 7.2 %all-to-all-start.3 = ((bf16[64,96,128]{2,1,0:T(8,128)(2,1)}), bf16[64,96,128]{2,1,0:T(8,128)(2,1)}, u32[]{:S(2)}, u32[]{:S(2)}) async-start(bf16[64,96,128]{2,1,0:T(8,128)(2,1)} %shard_map.175), calls=%async_computation.3 | async-start | bytes 3145728 | tf_op jit(solution)/shard_map/all_to_all | solution.py:518
  124.1 4.5 %shard_map.169 = (bf16[1024,512]{1,0:T(8,128)(2,1)}, f32[128,512]{1,0:T(8,128)}) custom-call(bf16[1024,512]{1,0:T(8,128)(2,1)} %get-tuple-element.80.cround, bf16[1024,512]{1,0:T(8,128)(2,1)} %edge_cot.3, bf16[128,512]{1,0:T(8,128)(2,1)} %get-tuple-element.81.receive, bf16[128,512]{1,0:T(8,128)(2,1)} %get-tuple-element.82.cot_update, ...), custom_call_target="tpu_custom_call" | custom-call | flops 1000000000 | bytes 5373952 | tf_op jit(solution)/shard_map/pallas_call | solution.py:140
  128.6 8.0 %shard_map.170 = (bf16[128,512]{1,0:T(8,128)(2,1)}, f32[128,512]{1,0:T(8,128)}, bf16[1024,512]{1,0:T(8,128)(2,1)}, bf16[1024,512]{1,0:T(8,128)(2,1)}, bf16[256,5...) custom-call(bf16[64,512]{1,0:T(8,128)(2,1)} %collective-permute-done.8.in0, ...), custom_call_target="tpu_custom_call" | custom-call | flops 4000000000 | bytes 10103808 | tf_op jit(solution)/shard_map/pallas_call | solution.py:140
  136.6 5.4 %shard_map.171 = (f32[512,512]{1,0:T(8,128)}, bf16[128,512]{1,0:T(8,128)(2,1)}, bf16[32,2,3,16,128]{4,3,2,1,0:T(8,128)(2,1)}, bf16[32,2,3,16,128]{4,3,2,1,0:T(8,128)(2,1)}) custom-call(s32[1]{0:T(128)} %bitcast.8.core, bf16[1024,512]{1,0:T(8,128)(2,1)} %get-tuple-element.86.upper, s32[8,128]{1,0:T(8,128)} %bitcast.25, s32[8,128]{1,0:T(8,128)} %bitcast.29, ...), custom_call_target="tpu_custom_call" | custom-call | flops 2000000000 | bytes 7086084 | tf_op jit(solution)/shard_map/pallas_call | solution.py:140
  144.1 4.3 %collective-permute-start.12 = (bf16[256,512]{1,0:T(8,128)(2,1)}, bf16[256,512]{1,0:T(8,128)(2,1)}, u32[]{:S(2)}, u32[]{:S(2)}) collective-permute-start(bf16[256,512]{1,0:T(8,128)(2,1)} %get-tuple-element.92), channel_id=1, source_target_pairs={{0,15},{1,0},{2,1},{3,2},{4,3},{5,4},{6,5},{7,6},{8,7},{9,8},{10,9... | collective-permute-start | bytes 786440 | tf_op jit(solution)/shard_map/ppermute | solution.py:25
  150.2 4.1 %collective-permute-done.12.in0 = bf16[256,512]{1,0:T(8,128)(2,1)} collective-permute-done((bf16[256,512]{1,0:T(8,128)(2,1)}, bf16[256,512]{1,0:T(8,128)(2,1)}, u32[]{:S(2)}, u32[]{:S(2)}) %collective-permute-start.12) | collective-permute-done | bytes 262176 | tf_op jit(solution)/shard_map/ppermute | solution.py:25
  154.4 5.2 %collective-permute-done.13.in1 = bf16[256,512]{1,0:T(8,128)(2,1)} collective-permute-done((bf16[256,512]{1,0:T(8,128)(2,1)}, bf16[256,512]{1,0:T(8,128)(2,1)}, u32[]{:S(2)}, u32[]{:S(2)}) %collective-permute-start.13) | collective-permute-done | bytes 262176 | tf_op jit(solution)/shard_map/ppermute | solution.py:25
  159.6 4.1 %shard_map.172 = (bf16[512,512]{1,0:T(8,128)(2,1)}, bf16[32,2,1,16,128]{4,3,2,1,0:T(8,128)(2,1)}, bf16[32,2,1,16,128]{4,3,2,1,0:T(8,128)(2,1)}) custom-call(s32[1]{0:T(128)} %bitcast.8.core, f32[512,512]{1,0:T(8,128)} %get-tuple-element.91.grid_own, bf16[256,512]{1,0:T(8,128)(2,1)} %collective-permute-done.12.in0, ...), custom_call_target="tpu_custom_call" | custom-call | flops 1000000000 | bytes 4198404 | tf_op jit(solution)/shard_map/pallas_call | solution.py:140
  169.2 22.4 %all_to_all.31.terms = bf16[64,64,128]{2,1,0:T(8,128)(2,1)} all-to-all(bf16[64,64,128]{2,1,0:T(8,128)(2,1)} %bitcast.19), channel_id=1, replica_groups=mesh['x'=4,'core'=2,'y'=4,'z'=4] {'x','y','z'}, dimensions={0} | all-to-all | bytes 2097152 | tf_op jit(solution)/shard_map/all_to_all | solution.py:529
  193.7 5.7 %all-to-all-start.5 = ((bf16[64,64,128]{2,1,0:T(8,128)(2,1)}), bf16[64,64,128]{2,1,0:T(8,128)(2,1)}, u32[]{:S(2)}, u32[]{:S(2)}) async-start(bf16[64,64,128]{2,1,0:T(8,128)(2,1)} %shard_map.176), calls=%async_computation.5 | async-start | bytes 2097152 | tf_op jit(solution)/shard_map/all_to_all | solution.py:545
  201.8 13.4 %all-to-all-done.5 = bf16[64,64,128]{2,1,0:T(8,128)(2,1)} async-done(((bf16[64,64,128]{2,1,0:T(8,128)(2,1)}), bf16[64,64,128]{2,1,0:T(8,128)(2,1)}, u32[]{:S(2)}, u32[]{:S(2)}) %all-to-all-start.5) | async-done | bytes 1048608 | tf_op jit(solution)/shard_map/all_to_all | solution.py:545
  218.7 5.4 %place_early.1.kept = bf16[10,512,512]{2,1,0:T(8,128)(2,1)} custom-call(s32[1]{0:T(128)} %bitcast.8.core, bf16[32,2,6,16,128]{4,3,2,1,0:T(8,128)(2,1)} %bitcast.16.own, bf16[32,2,6,16,128]{4,3,2,1,0:T(8,128)(2,1)} %bitcast.17.other), custom_call_target="tpu_custom_call" | custom-call | tf_op jit(solution)/shard_map/place_early/pallas_call | solution.py:532
  (47 shorter events, 43.5 us)
Async XLA Ops:
  3.6 13.9 %collective-permute-start = (bf16[256,512]{1,0:T(8,128)(2,1)}, bf16[256,512]{1,0:T(8,128)(2,1)}, u32[]{:S(2)}, u32[]{:S(2)}) collective-permute-start(bf16[256,512]{1,0:T(8,128)(2,1)} %get-tuple-element.60), channel_id=1, source_target_pairs={{0,1},{1,2},{2,3},{3,4},{4,5},{5,6},{6,7},{7,8},{8,9},{9,10},{10,1... | collective-permute-start | bytes 786440 | tf_op jit(solution)/shard_map/ppermute | solution.py:25
  6.1 11.4 %collective-permute-start.1 = (bf16[256,512]{1,0:T(8,128)(2,1)}, bf16[256,512]{1,0:T(8,128)(2,1)}, u32[]{:S(2)}, u32[]{:S(2)}) collective-permute-start(bf16[256,512]{1,0:T(8,128)(2,1)} %get-tuple-element.61), channel_id=1, source_target_pairs={{0,15},{1,0},{2,1},{3,2},{4,3},{5,4},{6,5},{7,6},{8,7},{9,8},{10,9... | collective-permute-start | bytes 786440 | tf_op jit(solution)/shard_map/ppermute | solution.py:25
  10.7 6.9 %collective-permute-start.2 = (bf16[256,512]{1,0:T(8,128)(2,1)}, bf16[256,512]{1,0:T(8,128)(2,1)}, u32[]{:S(2)}, u32[]{:S(2)}) collective-permute-start(bf16[256,512]{1,0:T(8,128)(2,1)} %get-tuple-element.62), channel_id=1, source_target_pairs={{0,16},{16,32},{32,48},{48,64},{64,80},{80,96},{96,112},{112,0},{1... | collective-permute-start | bytes 786440 | tf_op jit(solution)/shard_map/ppermute | solution.py:25
  12.7 6.1 %collective-permute-start.3 = (bf16[256,512]{1,0:T(8,128)(2,1)}, bf16[256,512]{1,0:T(8,128)(2,1)}, u32[]{:S(2)}, u32[]{:S(2)}) collective-permute-start(bf16[256,512]{1,0:T(8,128)(2,1)} %get-tuple-element.63), channel_id=1, source_target_pairs={{0,112},{16,0},{32,16},{48,32},{64,48},{80,64},{96,80},{112,96},{1... | collective-permute-start | bytes 786440 | tf_op jit(solution)/shard_map/ppermute | solution.py:25
  26.4 21.7 %all-to-all-start = ((bf16[128,16,128]{2,1,0:T(8,128)(2,1)}), bf16[128,16,128]{2,1,0:T(8,128)(2,1)}, u32[]{:S(2)}, u32[]{:S(2)}) async-start(bf16[128,16,128]{2,1,0:T(8,128)(2,1)} %bitcast.21), calls=%async_computation | async-start | bytes 1048576 | tf_op jit(solution)/shard_map/all_to_all | solution.py:462
  34.7 12.6 %collective-permute-start.4 = (bf16[64,512]{1,0:T(8,128)(2,1)}, bf16[64,512]{1,0:T(8,128)(2,1)}, u32[]{:S(2)}, u32[]{:S(2)}) collective-permute-start(bf16[64,512]{1,0:T(8,128)(2,1)} %get-tuple-element.67), channel_id=1, source_target_pairs={{0,1},{1,2},{2,3},{3,4},{4,5},{5,6},{6,7},{7,8},{8,9},{9,10},{10,1... | collective-permute-start | bytes 196616 | tf_op jit(solution)/shard_map/ppermute | solution.py:25
  36.3 11.1 %collective-permute-start.5 = (bf16[64,512]{1,0:T(8,128)(2,1)}, bf16[64,512]{1,0:T(8,128)(2,1)}, u32[]{:S(2)}, u32[]{:S(2)}) collective-permute-start(bf16[64,512]{1,0:T(8,128)(2,1)} %get-tuple-element.68), channel_id=1, source_target_pairs={{0,15},{1,0},{2,1},{3,2},{4,3},{5,4},{6,5},{7,6},{8,7},{9,8},{10,9... | collective-permute-start | bytes 196616 | tf_op jit(solution)/shard_map/ppermute | solution.py:25
  40.6 6.7 %collective-permute-start.6 = (bf16[64,512]{1,0:T(8,128)(2,1)}, bf16[64,512]{1,0:T(8,128)(2,1)}, u32[]{:S(2)}, u32[]{:S(2)}) collective-permute-start(bf16[64,512]{1,0:T(8,128)(2,1)} %get-tuple-element.69), channel_id=1, source_target_pairs={{0,16},{16,32},{32,48},{48,64},{64,80},{80,96},{96,112},{112,0},{1... | collective-permute-start | bytes 196616 | tf_op jit(solution)/shard_map/ppermute | solution.py:25
  42.3 5.0 %collective-permute-start.7 = (bf16[64,512]{1,0:T(8,128)(2,1)}, bf16[64,512]{1,0:T(8,128)(2,1)}, u32[]{:S(2)}, u32[]{:S(2)}) collective-permute-start(bf16[64,512]{1,0:T(8,128)(2,1)} %get-tuple-element.70), channel_id=1, source_target_pairs={{0,112},{16,0},{32,16},{48,32},{64,48},{80,64},{96,80},{112,96},{1... | collective-permute-start | bytes 196616 | tf_op jit(solution)/shard_map/ppermute | solution.py:25
  66.0 13.2 %collective-permute-start.18 = (bf16[32,2,6,16,128]{4,3,2,1,0:T(8,128)(2,1)}, bf16[32,2,6,16,128]{4,3,2,1,0:T(8,128)(2,1)S(1)}, u32[]{:S(2)}, u32[]{:S(2)}) collective-permute-start(bf16[32,2,6,16,128]{4,3,2,1,0:T(8,128)(2,1)} %get-tuple-element.109), channel_id=1, source_target_pairs={{0,16},{16,0},{1,17},{17,1},{2,18},{18,2},{3,19},{19,3},{4,20},{20... | collective-permute-start | bytes 4718600 | tf_op jit(solution)/shard_map/ppermute | solution.py:421
  67.3 18.9 %all-to-all-start.1 = ((bf16[128,16,128]{2,1,0:T(8,128)(2,1)}), bf16[128,16,128]{2,1,0:T(8,128)(2,1)}, u32[]{:S(2)}, u32[]{:S(2)}) async-start(bf16[128,16,128]{2,1,0:T(8,128)(2,1)} %bitcast.20), calls=%async_computation.1 | async-start | bytes 1048576 | tf_op jit(solution)/shard_map/all_to_all | solution.py:483
  72.0 9.2 %collective-permute-start.10 = (bf16[64,512]{1,0:T(8,128)(2,1)}, bf16[64,512]{1,0:T(8,128)(2,1)}, u32[]{:S(2)}, u32[]{:S(2)}) collective-permute-start(bf16[64,512]{1,0:T(8,128)(2,1)} %get-tuple-element.76), channel_id=1, source_target_pairs={{0,112},{16,0},{32,16},{48,32},{64,48},{80,64},{96,80},{112,96},{1... | collective-permute-start | bytes 196616 | tf_op jit(solution)/shard_map/ppermute | solution.py:25
  73.0 8.1 %collective-permute-start.11 = (bf16[64,512]{1,0:T(8,128)(2,1)}, bf16[64,512]{1,0:T(8,128)(2,1)}, u32[]{:S(2)}, u32[]{:S(2)}) collective-permute-start(bf16[64,512]{1,0:T(8,128)(2,1)} %get-tuple-element.77), channel_id=1, source_target_pairs={{0,16},{16,32},{32,48},{48,64},{64,80},{80,96},{96,112},{112,0},{1... | collective-permute-start | bytes 196616 | tf_op jit(solution)/shard_map/ppermute | solution.py:25
  73.7 7.5 %collective-permute-start.8 = (bf16[64,512]{1,0:T(8,128)(2,1)}, bf16[64,512]{1,0:T(8,128)(2,1)}, u32[]{:S(2)}, u32[]{:S(2)}) collective-permute-start(bf16[64,512]{1,0:T(8,128)(2,1)} %get-tuple-element.74), channel_id=1, source_target_pairs={{0,15},{1,0},{2,1},{3,2},{4,3},{5,4},{6,5},{7,6},{8,7},{9,8},{10,9... | collective-permute-start | bytes 196616 | tf_op jit(solution)/shard_map/ppermute | solution.py:25
  79.2 7.0 %collective-permute-start.9 = (bf16[64,512]{1,0:T(8,128)(2,1)}, bf16[64,512]{1,0:T(8,128)(2,1)}, u32[]{:S(2)}, u32[]{:S(2)}) collective-permute-start(bf16[64,512]{1,0:T(8,128)(2,1)} %get-tuple-element.75), channel_id=1, source_target_pairs={{0,1},{1,2},{2,3},{3,4},{4,5},{5,6},{6,7},{7,8},{8,9},{9,10},{10,1... | collective-permute-start | bytes 196616 | tf_op jit(solution)/shard_map/ppermute | solution.py:25
  116.9 52.3 %all-to-all-start.3 = ((bf16[64,96,128]{2,1,0:T(8,128)(2,1)}), bf16[64,96,128]{2,1,0:T(8,128)(2,1)}, u32[]{:S(2)}, u32[]{:S(2)}) async-start(bf16[64,96,128]{2,1,0:T(8,128)(2,1)} %shard_map.175), calls=%async_computation.3 | async-start | bytes 3145728 | tf_op jit(solution)/shard_map/all_to_all | solution.py:518
  142.0 24.5 %collective-permute-start.17 = (bf16[32,2,3,16,128]{4,3,2,1,0:T(8,128)(2,1)}, bf16[32,2,3,16,128]{4,3,2,1,0:T(8,128)(2,1)}, u32[]{:S(2)}, u32[]{:S(2)}) collective-permute-start(bf16[32,2,3,16,128]{4,3,2,1,0:T(8,128)(2,1)} %get-tuple-element.102), channel_id=1, source_target_pairs={{0,16},{16,0},{1,17},{17,1},{2,18},{18,2},{3,19},{19,3},{4,20},{20... | collective-permute-start | bytes 2359304 | tf_op jit(solution)/shard_map/ppermute | solution.py:421
  144.1 10.2 %collective-permute-start.12 = (bf16[256,512]{1,0:T(8,128)(2,1)}, bf16[256,512]{1,0:T(8,128)(2,1)}, u32[]{:S(2)}, u32[]{:S(2)}) collective-permute-start(bf16[256,512]{1,0:T(8,128)(2,1)} %get-tuple-element.92), channel_id=1, source_target_pairs={{0,15},{1,0},{2,1},{3,2},{4,3},{5,4},{6,5},{7,6},{8,7},{9,8},{10,9... | collective-permute-start | bytes 786440 | tf_op jit(solution)/shard_map/ppermute | solution.py:25
  148.5 11.1 %collective-permute-start.13 = (bf16[256,512]{1,0:T(8,128)(2,1)}, bf16[256,512]{1,0:T(8,128)(2,1)}, u32[]{:S(2)}, u32[]{:S(2)}) collective-permute-start(bf16[256,512]{1,0:T(8,128)(2,1)} %get-tuple-element.93), channel_id=1, source_target_pairs={{0,1},{1,2},{2,3},{3,4},{4,5},{5,6},{6,7},{7,8},{8,9},{9,10},{10,1... | collective-permute-start | bytes 786440 | tf_op jit(solution)/shard_map/ppermute | solution.py:25
  148.5 11.1 %collective-permute-start.14 = (bf16[256,512]{1,0:T(8,128)(2,1)}, bf16[256,512]{1,0:T(8,128)(2,1)}, u32[]{:S(2)}, u32[]{:S(2)}) collective-permute-start(bf16[256,512]{1,0:T(8,128)(2,1)} %get-tuple-element.94), channel_id=1, source_target_pairs={{0,112},{16,0},{32,16},{48,32},{64,48},{80,64},{96,80},{112,96},{1... | collective-permute-start | bytes 786440 | tf_op jit(solution)/shard_map/ppermute | solution.py:25
  148.8 10.8 %collective-permute-start.15 = (bf16[256,512]{1,0:T(8,128)(2,1)}, bf16[256,512]{1,0:T(8,128)(2,1)}, u32[]{:S(2)}, u32[]{:S(2)}) collective-permute-start(bf16[256,512]{1,0:T(8,128)(2,1)} %get-tuple-element.95), channel_id=1, source_target_pairs={{0,16},{16,32},{32,48},{48,64},{64,80},{80,96},{96,112},{112,0},{1... | collective-permute-start | bytes 786440 | tf_op jit(solution)/shard_map/ppermute | solution.py:25
  193.7 21.5 %all-to-all-start.5 = ((bf16[64,64,128]{2,1,0:T(8,128)(2,1)}), bf16[64,64,128]{2,1,0:T(8,128)(2,1)}, u32[]{:S(2)}, u32[]{:S(2)}) async-start(bf16[64,64,128]{2,1,0:T(8,128)(2,1)} %shard_map.176), calls=%async_computation.5 | async-start | bytes 2097152 | tf_op jit(solution)/shard_map/all_to_all | solution.py:545
  199.3 19.3 %collective-permute-start.20 = (bf16[64,96,128]{2,1,0:T(8,128)(2,1)}, bf16[64,96,128]{2,1,0:T(8,128)(2,1)}, u32[]{:S(2)}, u32[]{:S(2)}) collective-permute-start(bf16[64,96,128]{2,1,0:T(8,128)(2,1)} %all-to-all-done.3), channel_id=1, source_target_pairs={{0,16},{16,0},{1,17},{17,1},{2,18},{18,2},{3,19},{19,3},{4,20},{20... | collective-permute-start | bytes 4718600 | tf_op jit(solution)/shard_map/ppermute | solution.py:421
  215.2 8.9 %collective-permute-start.19 = (bf16[64,64,128]{2,1,0:T(8,128)(2,1)}, bf16[64,64,128]{2,1,0:T(8,128)(2,1)}, u32[]{:S(2)}, u32[]{:S(2)}) collective-permute-start(bf16[64,64,128]{2,1,0:T(8,128)(2,1)} %all-to-all-done.5), channel_id=1, source_target_pairs={{0,16},{16,0},{1,17},{17,1},{2,18},{18,2},{3,19},{19,3},{4,20},{20... | collective-permute-start | bytes 3145736 | tf_op jit(solution)/shard_map/ppermute | solution.py:421
  (2 other events, 14.8 us)

commit v7 on v6

--- a/solution.py
+++ b/solution.py
@@ -393,10 +393,11 @@
 
 
 def summed(terms):
-    spec = pl.BlockSpec((terms.shape[0], 32, 128), lambda i: (0, i, 0))
+    rows = 32 if terms.shape[1] % 48 else 48
+    spec = pl.BlockSpec((terms.shape[0], rows, 128), lambda i: (0, i, 0))
     return pl.pallas_call(
         sum_body,
-        grid=(terms.shape[1] // 32,),
+        grid=(terms.shape[1] // rows,),
         in_specs=[spec],
         out_specs=spec,
         out_shape=jax.ShapeDtypeStruct(terms.shape, bf16),

time: 229 us -> 228 us (level)
  no operation moved by 1% of the time
where the time goes in v7:
time: 228 us; the launch traced here: 227 us
  Pallas kernels  76.3 us (33%)
  starting transfers between devices  66.4 us (29%)
  blocking collectives  49.5 us (22%)
  waiting for transfers between devices  31.3 us (14%)
    pallas_call x11, Pallas kernels, call(): pl.pallas_call(body, grid=(1,), out_shape=shapes, in_specs=in_specs, out_...  62.3 us
    ppermute x16, starting transfers between devices, shifted(): return lax.ppermute(value, axis, pairs)  30 us
    all_to_all x1, blocking collectives, on_device(): early = lax.all_to_all(early.reshape(64, 96, 128), CHIPS, 0, 0, tiled=True)  27.2 us
    all_to_all x1, blocking collectives, on_device(): late = lax.all_to_all(late.reshape(64, 64, 128), CHIPS, 0, 0, tiled=True)  22.4 us
    ppermute x16, waiting for transfers between devices, shifted(): return lax.ppermute(value, axis, pairs)  15.7 us
    all_to_all x1, waiting for transfers between devices, on_device(): late = lax.all_to_all(late, CHIPS, 0, 0, tiled=True)  13.4 us
    all_to_all x2, starting transfers between devices, on_device(): lax.all_to_all(far_out.reshape(peers, 16, 128), AXES, 0, 0, tiled=True)  12.9 us
    ppermute x5, starting transfers between devices, swapped(): return lax.ppermute(value, 'core', [(0, 1), (1, 0)])  10.6 us
  transfers between devices with their start and end apart: 25, of which 7 were waited for; matrix products, arithmetic and copies ran while one was open for 1% of the time, Pallas kernels for 17%

profile of v7, /device:TPU:1, one launch (start us, length us, event | category | flops | bytes accessed | tf_op | source)
XLA Modules:
  0.0 226.9 jit_solution(13526000054680993306)
XLA Ops:
  6.1 4.6 %collective-permute-start.1 = (bf16[256,512]{1,0:T(8,128)(2,1)}, bf16[256,512]{1,0:T(8,128)(2,1)}, u32[]{:S(2)}, u32[]{:S(2)}) collective-permute-start(bf16[256,512]{1,0:T(8,128)(2,1)} %get-tuple-element.61), channel_id=1, source_target_pairs={{0,15},{1,0},{2,1},{3,2},{4,3},{5,4},{6,5},{7,6},{8,7},{9,8},{10,9... | collective-permute-start | bytes 786440 | tf_op jit(solution)/shard_map/ppermute | solution.py:25
  13.4 4.1 %shard_map.165.own = f32[1024,512]{1,0:T(8,128)} custom-call(bf16[512,512]{1,0:T(8,128)(2,1)} %get-tuple-element.59.project, s32[8,128]{1,0:T(8,128)} %bitcast.22, s32[8,128]{1,0:T(8,128)} %bitcast.26, bf16[128,512]{1,0:T(8,128)(2,1)} %mesh.5, bf16[10,512,512]{2,1,0:T(8,128)(2,1)} %w0.3), custom_call_target="tpu_custom_call" | custom-call | flops 1000000000 | bytes 3284992 | tf_op jit(solution)/shard_map/pallas_call | solution.py:140
  18.8 7.6 %shard_map.166 = (f32[1024,512]{1,0:T(8,128)}, f32[1024,512]{1,0:T(8,128)}, bf16[1024,512]{1,0:T(8,128)(2,1)}, bf16[128,512]{1,0:T(8,128)(2,1)}, bf16[128,512]{1...) custom-call(f32[1024,512]{1,0:T(8,128)} %shard_map.165.own, ...), custom_call_target="tpu_custom_call" | custom-call | flops 2000000000 | bytes 10628096 | tf_op jit(solution)/shard_map/pallas_call | solution.py:140
  26.4 8.3 %all-to-all-start = ((bf16[128,16,128]{2,1,0:T(8,128)(2,1)}), bf16[128,16,128]{2,1,0:T(8,128)(2,1)}, u32[]{:S(2)}, u32[]{:S(2)}) async-start(bf16[128,16,128]{2,1,0:T(8,128)(2,1)} %bitcast.21), calls=%async_computation | async-start | bytes 1048576 | tf_op jit(solution)/shard_map/all_to_all | solution.py:463
  36.3 4.3 %collective-permute-start.5 = (bf16[64,512]{1,0:T(8,128)(2,1)}, bf16[64,512]{1,0:T(8,128)(2,1)}, u32[]{:S(2)}, u32[]{:S(2)}) collective-permute-start(bf16[64,512]{1,0:T(8,128)(2,1)} %get-tuple-element.68), channel_id=1, source_target_pairs={{0,15},{1,0},{2,1},{3,2},{4,3},{5,4},{6,5},{7,6},{8,7},{9,8},{10,9... | collective-permute-start | bytes 196616 | tf_op jit(solution)/shard_map/ppermute | solution.py:25
  42.4 5.0 %shard_map.167 = (f32[1024,512]{1,0:T(8,128)}, f32[128,512]{1,0:T(8,128)}) custom-call(bf16[128,512]{1,0:T(8,128)(2,1)} %get-tuple-element.64.middle, bf16[128,512]{1,0:T(8,128)(2,1)} %get-tuple-element.65.sender, bf16[1024,512]{1,0:T(8,128)(2,1)} %edge.3, s32[8,128]{1,0:T(8,128)} %bitcast.32, s32[8,128]{1,0:T(8,128)} %bitcast.34, bf16[10,512,512]{2,1,0:T(8,128)(2,1)} %w0.3, ...), custom_call_target="tpu_custom_call" | custom-call | flops 2000000000 | bytes 5251072 | tf_op jit(solution)/shard_map/pallas_call | solution.py:140
  48.1 11.6 %shard_map.168 = (bf16[128,512]{1,0:T(8,128)(2,1)}, bf16[1024,512]{1,0:T(8,128)(2,1)}, bf16[128,512]{1,0:T(8,128)(2,1)}, bf16[128,512]{1,0:T(8,128)(2,1)}, bf16[...) custom-call(f32[1024,512]{1,0:T(8,128)} %get-tuple-element.66.own, ...), custom_call_target="tpu_custom_call" | custom-call | flops 8000000000 | bytes 11018240 | tf_op jit(solution)/shard_map/pallas_call | solution.py:140
  59.8 6.2 %shard_map.174 = (bf16[32,2,6,16,128]{4,3,2,1,0:T(8,128)(2,1)}, bf16[32,2,6,16,128]{4,3,2,1,0:T(8,128)(2,1)}) custom-call(s32[1]{0:T(128)} %bitcast.8.core, bf16[1024,512]{1,0:T(8,128)(2,1)} %edge.3, bf16[1024,512]{1,0:T(8,128)(2,1)} %get-tuple-element.80.cround, bf16[1024,512]{1,0:T(8,128)(2,1)} %get-tuple-element.103.hidden, ...), custom_call_target="tpu_custom_call" | custom-call | flops 2000000000 | bytes 8126468 | tf_op jit(solution)/shard_map/pallas_call | solution.py:140
  67.3 4.7 %all-to-all-start.1 = ((bf16[128,16,128]{2,1,0:T(8,128)(2,1)}), bf16[128,16,128]{2,1,0:T(8,128)(2,1)}, u32[]{:S(2)}, u32[]{:S(2)}) async-start(bf16[128,16,128]{2,1,0:T(8,128)(2,1)} %bitcast.20), calls=%async_computation.1 | async-start | bytes 1048576 | tf_op jit(solution)/shard_map/all_to_all | solution.py:484
  73.7 5.5 %collective-permute-start.8 = (bf16[64,512]{1,0:T(8,128)(2,1)}, bf16[64,512]{1,0:T(8,128)(2,1)}, u32[]{:S(2)}, u32[]{:S(2)}) collective-permute-start(bf16[64,512]{1,0:T(8,128)(2,1)} %get-tuple-element.74), channel_id=1, source_target_pairs={{0,15},{1,0},{2,1},{3,2},{4,3},{5,4},{6,5},{7,6},{8,7},{9,8},{10,9... | collective-permute-start | bytes 196616 | tf_op jit(solution)/shard_map/ppermute | solution.py:25
  81.2 5.0 %collective-permute-done.9.in1 = bf16[64,512]{1,0:T(8,128)(2,1)} collective-permute-done((bf16[64,512]{1,0:T(8,128)(2,1)}, bf16[64,512]{1,0:T(8,128)(2,1)}, u32[]{:S(2)}, u32[]{:S(2)}) %collective-permute-start.9) | collective-permute-done | bytes 65568 | tf_op jit(solution)/shard_map/ppermute | solution.py:25
  86.2 27.2 %all_to_all.30.terms = bf16[64,96,128]{2,1,0:T(8,128)(2,1)} all-to-all(bf16[64,96,128]{2,1,0:T(8,128)(2,1)S(1)} %bitcast.18), channel_id=1, replica_groups=mesh['x'=4,'core'=2,'y'=4,'z'=4] {'x','y','z'}, dimensions={0} | all-to-all | bytes 3145728 | tf_op jit(solution)/shard_map/all_to_all | solution.py:504
  115.8 7.2 %all-to-all-start.3 = ((bf16[64,96,128]{2,1,0:T(8,128)(2,1)}), bf16[64,96,128]{2,1,0:T(8,128)(2,1)}, u32[]{:S(2)}, u32[]{:S(2)}) async-start(bf16[64,96,128]{2,1,0:T(8,128)(2,1)} %shard_map.175), calls=%async_computation.3 | async-start | bytes 3145728 | tf_op jit(solution)/shard_map/all_to_all | solution.py:519
  123.0 4.5 %shard_map.169 = (bf16[1024,512]{1,0:T(8,128)(2,1)}, f32[128,512]{1,0:T(8,128)}) custom-call(bf16[1024,512]{1,0:T(8,128)(2,1)} %get-tuple-element.80.cround, bf16[1024,512]{1,0:T(8,128)(2,1)} %edge_cot.3, bf16[128,512]{1,0:T(8,128)(2,1)} %get-tuple-element.81.receive, bf16[128,512]{1,0:T(8,128)(2,1)} %get-tuple-element.82.cot_update, ...), custom_call_target="tpu_custom_call" | custom-call | flops 1000000000 | bytes 5373952 | tf_op jit(solution)/shard_map/pallas_call | solution.py:140
  127.5 8.0 %shard_map.170 = (bf16[128,512]{1,0:T(8,128)(2,1)}, f32[128,512]{1,0:T(8,128)}, bf16[1024,512]{1,0:T(8,128)(2,1)}, bf16[1024,512]{1,0:T(8,128)(2,1)}, bf16[256,5...) custom-call(bf16[64,512]{1,0:T(8,128)(2,1)} %collective-permute-done.8.in0, ...), custom_call_target="tpu_custom_call" | custom-call | flops 4000000000 | bytes 10103808 | tf_op jit(solution)/shard_map/pallas_call | solution.py:140
  135.5 5.4 %shard_map.171 = (f32[512,512]{1,0:T(8,128)}, bf16[128,512]{1,0:T(8,128)(2,1)}, bf16[32,2,3,16,128]{4,3,2,1,0:T(8,128)(2,1)}, bf16[32,2,3,16,128]{4,3,2,1,0:T(8,128)(2,1)}) custom-call(s32[1]{0:T(128)} %bitcast.8.core, bf16[1024,512]{1,0:T(8,128)(2,1)} %get-tuple-element.86.upper, s32[8,128]{1,0:T(8,128)} %bitcast.25, s32[8,128]{1,0:T(8,128)} %bitcast.29, ...), custom_call_target="tpu_custom_call" | custom-call | flops 2000000000 | bytes 7086084 | tf_op jit(solution)/shard_map/pallas_call | solution.py:140
  143.1 4.3 %collective-permute-start.12 = (bf16[256,512]{1,0:T(8,128)(2,1)}, bf16[256,512]{1,0:T(8,128)(2,1)}, u32[]{:S(2)}, u32[]{:S(2)}) collective-permute-start(bf16[256,512]{1,0:T(8,128)(2,1)} %get-tuple-element.92), channel_id=1, source_target_pairs={{0,15},{1,0},{2,1},{3,2},{4,3},{5,4},{6,5},{7,6},{8,7},{9,8},{10,9... | collective-permute-start | bytes 786440 | tf_op jit(solution)/shard_map/ppermute | solution.py:25
  149.1 4.1 %collective-permute-done.12.in0 = bf16[256,512]{1,0:T(8,128)(2,1)} collective-permute-done((bf16[256,512]{1,0:T(8,128)(2,1)}, bf16[256,512]{1,0:T(8,128)(2,1)}, u32[]{:S(2)}, u32[]{:S(2)}) %collective-permute-start.12) | collective-permute-done | bytes 262176 | tf_op jit(solution)/shard_map/ppermute | solution.py:25
  153.3 5.2 %collective-permute-done.13.in1 = bf16[256,512]{1,0:T(8,128)(2,1)} collective-permute-done((bf16[256,512]{1,0:T(8,128)(2,1)}, bf16[256,512]{1,0:T(8,128)(2,1)}, u32[]{:S(2)}, u32[]{:S(2)}) %collective-permute-start.13) | collective-permute-done | bytes 262176 | tf_op jit(solution)/shard_map/ppermute | solution.py:25
  158.5 4.1 %shard_map.172 = (bf16[512,512]{1,0:T(8,128)(2,1)}, bf16[32,2,1,16,128]{4,3,2,1,0:T(8,128)(2,1)}, bf16[32,2,1,16,128]{4,3,2,1,0:T(8,128)(2,1)}) custom-call(s32[1]{0:T(128)} %bitcast.8.core, f32[512,512]{1,0:T(8,128)} %get-tuple-element.91.grid_own, bf16[256,512]{1,0:T(8,128)(2,1)} %collective-permute-done.12.in0, ...), custom_call_target="tpu_custom_call" | custom-call | flops 1000000000 | bytes 4198404 | tf_op jit(solution)/shard_map/pallas_call | solution.py:140
  168.1 22.4 %all_to_all.31.terms = bf16[64,64,128]{2,1,0:T(8,128)(2,1)} all-to-all(bf16[64,64,128]{2,1,0:T(8,128)(2,1)} %bitcast.19), channel_id=1, replica_groups=mesh['x'=4,'core'=2,'y'=4,'z'=4] {'x','y','z'}, dimensions={0} | all-to-all | bytes 2097152 | tf_op jit(solution)/shard_map/all_to_all | solution.py:530
  192.6 5.7 %all-to-all-start.5 = ((bf16[64,64,128]{2,1,0:T(8,128)(2,1)}), bf16[64,64,128]{2,1,0:T(8,128)(2,1)}, u32[]{:S(2)}, u32[]{:S(2)}) async-start(bf16[64,64,128]{2,1,0:T(8,128)(2,1)} %shard_map.176), calls=%async_computation.5 | async-start | bytes 2097152 | tf_op jit(solution)/shard_map/all_to_all | solution.py:546
  200.7 13.4 %all-to-all-done.5 = bf16[64,64,128]{2,1,0:T(8,128)(2,1)} async-done(((bf16[64,64,128]{2,1,0:T(8,128)(2,1)}), bf16[64,64,128]{2,1,0:T(8,128)(2,1)}, u32[]{:S(2)}, u32[]{:S(2)}) %all-to-all-start.5) | async-done | bytes 1048608 | tf_op jit(solution)/shard_map/all_to_all | solution.py:546
  217.6 5.4 %place_early.1.kept = bf16[10,512,512]{2,1,0:T(8,128)(2,1)} custom-call(s32[1]{0:T(128)} %bitcast.8.core, bf16[32,2,6,16,128]{4,3,2,1,0:T(8,128)(2,1)} %bitcast.16.own, bf16[32,2,6,16,128]{4,3,2,1,0:T(8,128)(2,1)} %bitcast.17.other), custom_call_target="tpu_custom_call" | custom-call | tf_op jit(solution)/shard_map/place_early/pallas_call | solution.py:533
  (47 shorter events, 42.4 us)
Async XLA Ops:
  3.6 13.9 %collective-permute-start = (bf16[256,512]{1,0:T(8,128)(2,1)}, bf16[256,512]{1,0:T(8,128)(2,1)}, u32[]{:S(2)}, u32[]{:S(2)}) collective-permute-start(bf16[256,512]{1,0:T(8,128)(2,1)} %get-tuple-element.60), channel_id=1, source_target_pairs={{0,1},{1,2},{2,3},{3,4},{4,5},{5,6},{6,7},{7,8},{8,9},{9,10},{10,1... | collective-permute-start | bytes 786440 | tf_op jit(solution)/shard_map/ppermute | solution.py:25
  6.1 11.4 %collective-permute-start.1 = (bf16[256,512]{1,0:T(8,128)(2,1)}, bf16[256,512]{1,0:T(8,128)(2,1)}, u32[]{:S(2)}, u32[]{:S(2)}) collective-permute-start(bf16[256,512]{1,0:T(8,128)(2,1)} %get-tuple-element.61), channel_id=1, source_target_pairs={{0,15},{1,0},{2,1},{3,2},{4,3},{5,4},{6,5},{7,6},{8,7},{9,8},{10,9... | collective-permute-start | bytes 786440 | tf_op jit(solution)/shard_map/ppermute | solution.py:25
  10.7 6.9 %collective-permute-start.2 = (bf16[256,512]{1,0:T(8,128)(2,1)}, bf16[256,512]{1,0:T(8,128)(2,1)}, u32[]{:S(2)}, u32[]{:S(2)}) collective-permute-start(bf16[256,512]{1,0:T(8,128)(2,1)} %get-tuple-element.62), channel_id=1, source_target_pairs={{0,16},{16,32},{32,48},{48,64},{64,80},{80,96},{96,112},{112,0},{1... | collective-permute-start | bytes 786440 | tf_op jit(solution)/shard_map/ppermute | solution.py:25
  12.7 6.1 %collective-permute-start.3 = (bf16[256,512]{1,0:T(8,128)(2,1)}, bf16[256,512]{1,0:T(8,128)(2,1)}, u32[]{:S(2)}, u32[]{:S(2)}) collective-permute-start(bf16[256,512]{1,0:T(8,128)(2,1)} %get-tuple-element.63), channel_id=1, source_target_pairs={{0,112},{16,0},{32,16},{48,32},{64,48},{80,64},{96,80},{112,96},{1... | collective-permute-start | bytes 786440 | tf_op jit(solution)/shard_map/ppermute | solution.py:25
  26.4 21.7 %all-to-all-start = ((bf16[128,16,128]{2,1,0:T(8,128)(2,1)}), bf16[128,16,128]{2,1,0:T(8,128)(2,1)}, u32[]{:S(2)}, u32[]{:S(2)}) async-start(bf16[128,16,128]{2,1,0:T(8,128)(2,1)} %bitcast.21), calls=%async_computation | async-start | bytes 1048576 | tf_op jit(solution)/shard_map/all_to_all | solution.py:463
  34.7 12.6 %collective-permute-start.4 = (bf16[64,512]{1,0:T(8,128)(2,1)}, bf16[64,512]{1,0:T(8,128)(2,1)}, u32[]{:S(2)}, u32[]{:S(2)}) collective-permute-start(bf16[64,512]{1,0:T(8,128)(2,1)} %get-tuple-element.67), channel_id=1, source_target_pairs={{0,1},{1,2},{2,3},{3,4},{4,5},{5,6},{6,7},{7,8},{8,9},{9,10},{10,1... | collective-permute-start | bytes 196616 | tf_op jit(solution)/shard_map/ppermute | solution.py:25
  36.3 11.1 %collective-permute-start.5 = (bf16[64,512]{1,0:T(8,128)(2,1)}, bf16[64,512]{1,0:T(8,128)(2,1)}, u32[]{:S(2)}, u32[]{:S(2)}) collective-permute-start(bf16[64,512]{1,0:T(8,128)(2,1)} %get-tuple-element.68), channel_id=1, source_target_pairs={{0,15},{1,0},{2,1},{3,2},{4,3},{5,4},{6,5},{7,6},{8,7},{9,8},{10,9... | collective-permute-start | bytes 196616 | tf_op jit(solution)/shard_map/ppermute | solution.py:25
  40.6 6.7 %collective-permute-start.6 = (bf16[64,512]{1,0:T(8,128)(2,1)}, bf16[64,512]{1,0:T(8,128)(2,1)}, u32[]{:S(2)}, u32[]{:S(2)}) collective-permute-start(bf16[64,512]{1,0:T(8,128)(2,1)} %get-tuple-element.69), channel_id=1, source_target_pairs={{0,16},{16,32},{32,48},{48,64},{64,80},{80,96},{96,112},{112,0},{1... | collective-permute-start | bytes 196616 | tf_op jit(solution)/shard_map/ppermute | solution.py:25
  42.3 5.0 %collective-permute-start.7 = (bf16[64,512]{1,0:T(8,128)(2,1)}, bf16[64,512]{1,0:T(8,128)(2,1)}, u32[]{:S(2)}, u32[]{:S(2)}) collective-permute-start(bf16[64,512]{1,0:T(8,128)(2,1)} %get-tuple-element.70), channel_id=1, source_target_pairs={{0,112},{16,0},{32,16},{48,32},{64,48},{80,64},{96,80},{112,96},{1... | collective-permute-start | bytes 196616 | tf_op jit(solution)/shard_map/ppermute | solution.py:25
  66.0 13.2 %collective-permute-start.18 = (bf16[32,2,6,16,128]{4,3,2,1,0:T(8,128)(2,1)}, bf16[32,2,6,16,128]{4,3,2,1,0:T(8,128)(2,1)S(1)}, u32[]{:S(2)}, u32[]{:S(2)}) collective-permute-start(bf16[32,2,6,16,128]{4,3,2,1,0:T(8,128)(2,1)} %get-tuple-element.109), channel_id=1, source_target_pairs={{0,16},{16,0},{1,17},{17,1},{2,18},{18,2},{3,19},{19,3},{4,20},{20... | collective-permute-start | bytes 4718600 | tf_op jit(solution)/shard_map/ppermute | solution.py:422
  67.3 18.9 %all-to-all-start.1 = ((bf16[128,16,128]{2,1,0:T(8,128)(2,1)}), bf16[128,16,128]{2,1,0:T(8,128)(2,1)}, u32[]{:S(2)}, u32[]{:S(2)}) async-start(bf16[128,16,128]{2,1,0:T(8,128)(2,1)} %bitcast.20), calls=%async_computation.1 | async-start | bytes 1048576 | tf_op jit(solution)/shard_map/all_to_all | solution.py:484
  72.0 9.2 %collective-permute-start.10 = (bf16[64,512]{1,0:T(8,128)(2,1)}, bf16[64,512]{1,0:T(8,128)(2,1)}, u32[]{:S(2)}, u32[]{:S(2)}) collective-permute-start(bf16[64,512]{1,0:T(8,128)(2,1)} %get-tuple-element.76), channel_id=1, source_target_pairs={{0,112},{16,0},{32,16},{48,32},{64,48},{80,64},{96,80},{112,96},{1... | collective-permute-start | bytes 196616 | tf_op jit(solution)/shard_map/ppermute | solution.py:25
  73.0 8.1 %collective-permute-start.11 = (bf16[64,512]{1,0:T(8,128)(2,1)}, bf16[64,512]{1,0:T(8,128)(2,1)}, u32[]{:S(2)}, u32[]{:S(2)}) collective-permute-start(bf16[64,512]{1,0:T(8,128)(2,1)} %get-tuple-element.77), channel_id=1, source_target_pairs={{0,16},{16,32},{32,48},{48,64},{64,80},{80,96},{96,112},{112,0},{1... | collective-permute-start | bytes 196616 | tf_op jit(solution)/shard_map/ppermute | solution.py:25
  73.7 7.5 %collective-permute-start.8 = (bf16[64,512]{1,0:T(8,128)(2,1)}, bf16[64,512]{1,0:T(8,128)(2,1)}, u32[]{:S(2)}, u32[]{:S(2)}) collective-permute-start(bf16[64,512]{1,0:T(8,128)(2,1)} %get-tuple-element.74), channel_id=1, source_target_pairs={{0,15},{1,0},{2,1},{3,2},{4,3},{5,4},{6,5},{7,6},{8,7},{9,8},{10,9... | collective-permute-start | bytes 196616 | tf_op jit(solution)/shard_map/ppermute | solution.py:25
  79.2 7.0 %collective-permute-start.9 = (bf16[64,512]{1,0:T(8,128)(2,1)}, bf16[64,512]{1,0:T(8,128)(2,1)}, u32[]{:S(2)}, u32[]{:S(2)}) collective-permute-start(bf16[64,512]{1,0:T(8,128)(2,1)} %get-tuple-element.75), channel_id=1, source_target_pairs={{0,1},{1,2},{2,3},{3,4},{4,5},{5,6},{6,7},{7,8},{8,9},{9,10},{10,1... | collective-permute-start | bytes 196616 | tf_op jit(solution)/shard_map/ppermute | solution.py:25
  115.8 52.3 %all-to-all-start.3 = ((bf16[64,96,128]{2,1,0:T(8,128)(2,1)}), bf16[64,96,128]{2,1,0:T(8,128)(2,1)}, u32[]{:S(2)}, u32[]{:S(2)}) async-start(bf16[64,96,128]{2,1,0:T(8,128)(2,1)} %shard_map.175), calls=%async_computation.3 | async-start | bytes 3145728 | tf_op jit(solution)/shard_map/all_to_all | solution.py:519
  140.9 24.5 %collective-permute-start.17 = (bf16[32,2,3,16,128]{4,3,2,1,0:T(8,128)(2,1)}, bf16[32,2,3,16,128]{4,3,2,1,0:T(8,128)(2,1)}, u32[]{:S(2)}, u32[]{:S(2)}) collective-permute-start(bf16[32,2,3,16,128]{4,3,2,1,0:T(8,128)(2,1)} %get-tuple-element.102), channel_id=1, source_target_pairs={{0,16},{16,0},{1,17},{17,1},{2,18},{18,2},{3,19},{19,3},{4,20},{20... | collective-permute-start | bytes 2359304 | tf_op jit(solution)/shard_map/ppermute | solution.py:422
  143.1 10.2 %collective-permute-start.12 = (bf16[256,512]{1,0:T(8,128)(2,1)}, bf16[256,512]{1,0:T(8,128)(2,1)}, u32[]{:S(2)}, u32[]{:S(2)}) collective-permute-start(bf16[256,512]{1,0:T(8,128)(2,1)} %get-tuple-element.92), channel_id=1, source_target_pairs={{0,15},{1,0},{2,1},{3,2},{4,3},{5,4},{6,5},{7,6},{8,7},{9,8},{10,9... | collective-permute-start | bytes 786440 | tf_op jit(solution)/shard_map/ppermute | solution.py:25
  147.4 11.1 %collective-permute-start.13 = (bf16[256,512]{1,0:T(8,128)(2,1)}, bf16[256,512]{1,0:T(8,128)(2,1)}, u32[]{:S(2)}, u32[]{:S(2)}) collective-permute-start(bf16[256,512]{1,0:T(8,128)(2,1)} %get-tuple-element.93), channel_id=1, source_target_pairs={{0,1},{1,2},{2,3},{3,4},{4,5},{5,6},{6,7},{7,8},{8,9},{9,10},{10,1... | collective-permute-start | bytes 786440 | tf_op jit(solution)/shard_map/ppermute | solution.py:25
  147.4 11.1 %collective-permute-start.14 = (bf16[256,512]{1,0:T(8,128)(2,1)}, bf16[256,512]{1,0:T(8,128)(2,1)}, u32[]{:S(2)}, u32[]{:S(2)}) collective-permute-start(bf16[256,512]{1,0:T(8,128)(2,1)} %get-tuple-element.94), channel_id=1, source_target_pairs={{0,112},{16,0},{32,16},{48,32},{64,48},{80,64},{96,80},{112,96},{1... | collective-permute-start | bytes 786440 | tf_op jit(solution)/shard_map/ppermute | solution.py:25
  147.7 10.8 %collective-permute-start.15 = (bf16[256,512]{1,0:T(8,128)(2,1)}, bf16[256,512]{1,0:T(8,128)(2,1)}, u32[]{:S(2)}, u32[]{:S(2)}) collective-permute-start(bf16[256,512]{1,0:T(8,128)(2,1)} %get-tuple-element.95), channel_id=1, source_target_pairs={{0,16},{16,32},{32,48},{48,64},{64,80},{80,96},{96,112},{112,0},{1... | collective-permute-start | bytes 786440 | tf_op jit(solution)/shard_map/ppermute | solution.py:25
  192.6 21.5 %all-to-all-start.5 = ((bf16[64,64,128]{2,1,0:T(8,128)(2,1)}), bf16[64,64,128]{2,1,0:T(8,128)(2,1)}, u32[]{:S(2)}, u32[]{:S(2)}) async-start(bf16[64,64,128]{2,1,0:T(8,128)(2,1)} %shard_map.176), calls=%async_computation.5 | async-start | bytes 2097152 | tf_op jit(solution)/shard_map/all_to_all | solution.py:546
  198.3 19.3 %collective-permute-start.20 = (bf16[64,96,128]{2,1,0:T(8,128)(2,1)}, bf16[64,96,128]{2,1,0:T(8,128)(2,1)}, u32[]{:S(2)}, u32[]{:S(2)}) collective-permute-start(bf16[64,96,128]{2,1,0:T(8,128)(2,1)} %all-to-all-done.3), channel_id=1, source_target_pairs={{0,16},{16,0},{1,17},{17,1},{2,18},{18,2},{3,19},{19,3},{4,20},{20... | collective-permute-start | bytes 4718600 | tf_op jit(solution)/shard_map/ppermute | solution.py:422
  214.1 8.9 %collective-permute-start.19 = (bf16[64,64,128]{2,1,0:T(8,128)(2,1)}, bf16[64,64,128]{2,1,0:T(8,128)(2,1)}, u32[]{:S(2)}, u32[]{:S(2)}) collective-permute-start(bf16[64,64,128]{2,1,0:T(8,128)(2,1)} %all-to-all-done.5), channel_id=1, source_target_pairs={{0,16},{16,0},{1,17},{17,1},{2,18},{18,2},{3,19},{19,3},{4,20},{20... | collective-permute-start | bytes 3145736 | tf_op jit(solution)/shard_map/ppermute | solution.py:422
  (2 other events, 14.8 us)
